TPU v7x, 32 devices: a whole 2x2x4 slice. The times are simulated.
32 devices in a mesh: groups: 2 (over x), expert: 8 (over z, y), attn: 2 (over core).
Axes of the slice: x: 2, y: 2, z: 4, core: 2. Of those that a mesh axis runs over, the one named last changes fastest.
Arguments:
- queries: bfloat16 [4096, 2048], P(('groups', 'expert'), 'attn'), parts along dimension 0, may hold values from -180 to 180
- new_keys: bfloat16 [4096, 256], P(('groups', 'expert'), 'attn'), parts along dimension 0, may hold values from -6 to 6
- new_values: bfloat16 [4096, 256], P(('groups', 'expert'), 'attn'), parts along dimension 0, may hold values from -6 to 6
- cache_keys: bfloat16 [32, 1024, 256], P(('groups', 'expert'), None, 'attn'), parts along dimension 0, may hold values from -6 to 6
- cache_values: bfloat16 [32, 1024, 256], P(('groups', 'expert'), None, 'attn'), parts along dimension 0, may hold values from -6 to 6
- cache_len: int32 [32], P(('groups', 'expert')), parts along dimension 0, may hold values from 1 to 1024, as said below
- span_req: int32 [32], P(('groups', 'expert')), parts along dimension 0, may hold values from 0 to 15, as said below
- out_proj: bfloat16 [2048, 2048], P('attn'), may hold values from -0.5 to 0.5
- resid: bfloat16 [4096, 2048], P(('groups', 'expert', 'attn')), parts along dimension 0, may hold values from -60 to 60
- norm_gain: float32 [2048], replicated, may hold values from 0.1 to 1.9
- routes: int32 [4096, 8], P(('groups', 'expert', 'attn')), parts along dimension 0, may hold values from 0 to 15, all different within a row; in each aligned block of 128 rows (0 to 127, 128 to 255, ...) at most 128 rows name the same one
- gates: float32 [4096, 8], P(('groups', 'expert', 'attn')), parts along dimension 0, may hold values from 0.05 to 1
- w_gate: bfloat16 [16, 2048, 384], P(('expert', 'attn')), may hold values from -0.125 to 0.125
- w_up: bfloat16 [16, 2048, 384], P(('expert', 'attn')), may hold values from -0.125 to 0.125
- w_down: bfloat16 [16, 384, 2048], P(('expert', 'attn')), may hold values from -0.3125 to 0.3125
Outputs:
- layer_out: bfloat16 [4096, 2048], P(('groups', 'expert', 'attn')), parts along dimension 0
There are 2 independent parts, one for each index of `groups`. A program takes and returns all parts, laid end to end along the dimension named above; an argument that names none is the same for every part. Nothing has to cross between parts.
Inputs may be any that keep to these rules, and one draw needn't show every extreme that they name: `cache_len`: some request has exactly 1024 cached tokens. `span_req`: the 2 spans c with c // 2 = b belong to the 2 distinct requests b * 2 to (b + 1) * 2 - 1. `routes`: among the 128 tokens of one device no expert is named more than 128 times.
All inputs are finite; a program needn't handle non-finite values.
Results may differ from a plain program's by a relative error of at most 0.0054.
Values may be sent and summed in bfloat16 or wider, within the bound.
No kernel may reach another device: no remote copies, remote signals or barrier semaphores. Data moves between devices by JAX's collectives and lax.ppermute only.
A program may use at most 128 MiB of HBM per device.

v0:
```python
import math

import jax
import jax.numpy as jnp
from jax import lax
from jax.sharding import PartitionSpec as P

HD = 128


negative_fill = -1e30


def per_device(
    queries,
    new_keys,
    new_values,
    cache_keys,
    cache_values,
    cache_len,
    span_req,
    out_proj,
    resid,
    norm_gain,
    routes,
    gates,
    w_gate,
    w_up,
    w_down,
):
    n_attn = lax.axis_size("attn")
    n_expert = lax.axis_size("expert")
    spans = cache_keys.shape[0]
    cache_size = cache_keys.shape[1]
    length = queries.shape[0] // spans
    kv_local = cache_keys.shape[2] // HD
    head_count = queries.shape[1] // HD
    group_size = head_count // kv_local
    model_width = resid.shape[1]
    own_rows = resid.shape[0]
    local_req = span_req % spans
    lengths = cache_len[local_req]
    queries_split = queries.reshape(spans, length, kv_local, group_size, HD)
    own_keys = new_keys.reshape(spans, length, kv_local, HD)
    own_values = new_values.reshape(spans, length, kv_local, HD)
    keys_cached = cache_keys[local_req].reshape(spans, cache_size, kv_local, HD)
    values_cached = cache_values[local_req].reshape(spans, cache_size, kv_local, HD)
    all_keys = jnp.concatenate([keys_cached, own_keys], axis=1)
    all_values = jnp.concatenate([values_cached, own_values], axis=1)
    scores = jnp.einsum(
        "clgqd,ckgd->cgqlk", queries_split, all_keys, preferred_element_type=jnp.float32
    ) * (1.0 / math.sqrt(HD))
    key_pos = jnp.arange(cache_size + length, dtype=jnp.int32)
    query_pos = jnp.arange(length, dtype=jnp.int32)
    in_cache = key_pos[None, None, :] < lengths[:, None, None]
    own_seen = key_pos[None, None, :] - cache_size <= query_pos[None, :, None]
    visible = jnp.where(key_pos[None, None, :] < cache_size, in_cache, own_seen)
    scores = jnp.where(visible[:, None, None], scores, negative_fill)
    weights = jax.nn.softmax(scores, axis=-1).astype(jnp.bfloat16)
    attended = jnp.einsum(
        "cgqlk,ckgd->clgqd", weights, all_values, preferred_element_type=jnp.float32
    )
    attended = attended.astype(jnp.bfloat16).reshape(spans * length, head_count * HD)
    attn_out = lax.psum_scatter(
        jnp.dot(attended, out_proj, preferred_element_type=jnp.float32),
        "attn",
        scatter_dimension=0,
        tiled=True,
    )
    hidden = (resid.astype(jnp.float32) + attn_out).astype(jnp.bfloat16)
    state_float = hidden.astype(jnp.float32)
    mean_square = jnp.mean(state_float * state_float, axis=-1, keepdims=True)
    normed = (state_float * lax.rsqrt(mean_square + 1e-06) * norm_gain).astype(jnp.bfloat16)
    top_count = routes.shape[1]
    experts = n_expert * n_attn
    capacity = 2 * top_count * own_rows // experts
    flat_routes = routes.reshape(-1)
    one_hot = (flat_routes[:, None] == jnp.arange(experts, dtype=jnp.int32)[None, :]).astype(
        jnp.int32
    )
    earlier = jnp.cumsum(one_hot, axis=0) - one_hot
    slot_index = jnp.sum(earlier * one_hot, axis=1)
    slot_target = flat_routes * capacity + slot_index
    pair_token = jnp.arange(flat_routes.shape[0], dtype=jnp.int32) // top_count
    source_row = (
        jnp.full((experts * capacity,), own_rows, jnp.int32).at[slot_target].set(pair_token)
    )
    padded_rows = jnp.concatenate([normed, jnp.zeros((1, model_width), jnp.bfloat16)], axis=0)
    outgoing = padded_rows[source_row].reshape(experts, capacity, model_width)
    slot_block = lax.all_to_all(
        outgoing, ("expert", "attn"), split_axis=0, concat_axis=0, tiled=True
    )
    rows_in = slot_block.reshape(-1, model_width)
    gate_part = jnp.dot(rows_in, w_gate[0], preferred_element_type=jnp.float32)
    up_part = jnp.dot(rows_in, w_up[0], preferred_element_type=jnp.float32)
    act = (jax.nn.silu(gate_part) * up_part).astype(jnp.bfloat16)
    expert_out = jnp.dot(act, w_down[0], preferred_element_type=jnp.float32).astype(jnp.bfloat16)
    computed = expert_out.reshape(slot_block.shape)
    returned = lax.all_to_all(computed, ("expert", "attn"), split_axis=0, concat_axis=0, tiled=True)
    picked = returned.reshape(experts * capacity, model_width)[slot_target].astype(jnp.float32)
    weight = gates / jnp.sum(gates, axis=-1, keepdims=True)
    mixed = jnp.sum(
        (picked * weight.reshape(-1, 1)).reshape(own_rows, top_count, model_width), axis=1
    )
    return (state_float + mixed).astype(jnp.bfloat16)


def solution(mesh):
    placed = (
        P(("groups", "expert"), "attn"),
        P(("groups", "expert"), "attn"),
        P(("groups", "expert"), "attn"),
        P(("groups", "expert"), None, "attn"),
        P(("groups", "expert"), None, "attn"),
        P(("groups", "expert")),
        P(("groups", "expert")),
        P("attn", None),
        P(("groups", "expert", "attn"), None),
        P(),
        P(("groups", "expert", "attn"), None),
        P(("groups", "expert", "attn"), None),
        P(("expert", "attn"), None, None),
        P(("expert", "attn"), None, None),
        P(("expert", "attn"), None, None),
    )
    return jax.shard_map(
        per_device,
        mesh=mesh,
        in_specs=placed,
        out_specs=P(("groups", "expert", "attn"), None),
        check_vma=False,
    )
```

profile of v0, /device:TPU:13, one launch (start us, length us, event | category | flops | bytes accessed | tf_op | source)
XLA Modules:
  0.0 471.7 jit_solution(5815793045091362308)
XLA Ops:
  6.5 0.0 copy-start
  6.5 0.0 copy-start.2
  6.5 0.0 copy-start.8
  6.5 0.0 reduce-scatter.2.cloned.1.call-start
  6.6 0.8 compare_select_fusion.2
  7.4 2.4 gather_fusion.2
  9.8 1.3 gather_fusion.1
  11.1 0.1 iota_compare_fusion.3
  11.2 0.2 iota_compare_fusion
  11.4 1.1 copy.35
  12.6 1.7 gather_fusion
  14.3 0.2 copy.21
  14.5 0.0 copy-done.2
  14.5 0.1 copy.22
  14.6 0.9 broadcast_select_fusion
  15.5 0.0 copy-done.8
  15.5 2.5 fusion.39
  18.1 1.3 fusion.1
  19.3 2.1 fusion.11
  21.4 0.3 copy.25
  21.7 0.0 copy-start.3
  21.7 0.0 copy-start.1
  21.7 4.9 %fusion.22 = f32[256,2048]{1,0:T(8,128)} fusion(bf16[1024,2048]{1,0:T(8,128)(2,1)} %param.22, bf16[32,8,8,128]{3,2,1,0:T(8,128)(2,1)S(1)} %bitcast.89), kind=kOutput, calls=%fused_computation.38 | convolution fusion | flops 1073741824 | bytes 6815744 | tf_op jit(solution)/shard_map/dot_general | solution.py:65
  26.6 0.0 copy-start.5
  26.6 0.0 reduce-scatter.2.cloned.1.call-update
  26.6 0.0 copy-done.3
  26.6 0.1 copy.27
  26.7 0.1 eq.31
  26.8 0.1 eq.27
  26.9 4.5 reduce-window.6
  31.5 0.1 slice.18
  31.5 0.1 copy.29
  31.7 0.1 copy.30
  31.8 0.1 copy.26
  31.9 0.1 mul.77
  32.0 0.1 broadcast_add_fusion
  32.1 4.3 scatter_custom_fusion
  36.5 1.9 reduce-scatter.2.cloned.1.call-done
  38.4 0.0 copy-done.1
  38.4 1.5 fusion.14
  39.8 0.0 copy-done.5
  39.8 0.2 fusion.16
  40.1 11.0 %gather_fusion.3 = bf16[2048,2048]{1,0:T(8,128)(2,1)} fusion(bf16[129,2048]{1,0:T(8,128)(2,1)S(1)} %concatenate.11, s32[2048]{0:T(1024)S(1)} %fusion.30), kind=kCustom, calls=%fused_computation.3 | custom fusion | bytes 16785408 | tf_op jit(solution)/shard_map/gather | solution.py:89
  51.1 0.0 copy-start.6
  51.1 188.2 %all_to_all.10 = bf16[16,128,2048]{2,1,0:T(8,128)(2,1)S(1)} all-to-all(bf16[16,128,2048]{2,1,0:T(8,128)(2,1)} %bitcast.82), channel_id=1, replica_groups=mesh['groups'=2,'expert'=8,'attn'=2] {'expert','attn'}, dimensions={0} | all-to-all | bytes 16777216 | tf_op jit(solution)/shard_map/all_to_all | solution.py:90
  239.3 0.0 copy-done.6
  239.3 0.0 copy-start.7
  239.3 4.5 fusion.6
  243.9 0.0 copy-done.7
  243.9 5.3 %multiply_convert_fusion = bf16[2048,384]{1,0:T(8,128)(2,1)S(1)} fusion(f32[2048,384]{1,0:T(8,128)S(1)} %fusion.6, bf16[2048,2048]{1,0:T(8,128)(2,1)S(1)} %bitcast.85, bf16[1,2048,384]{2,1,0:T(8,128)(2,1)S(1)} %copy-done.7), kind=kOutput, calls=%fused_computation.15 | convolution fusion | flops 3225944064 | bytes 14680064 | tf_op jit(solution)/shard_map/dot_general | solution.py:95
  249.2 0.0 copy-done
  249.3 6.8 %convolution_convert_fusion = bf16[2048,2048]{1,0:T(8,128)(2,1)} fusion(bf16[2048,384]{1,0:T(8,128)(2,1)S(1)} %multiply_convert_fusion, bf16[1,384,2048]{2,1,0:T(8,128)(2,1)S(1)} %copy-done), kind=kOutput, calls=%fused_computation.12 | convolution fusion | flops 3225419776 | bytes 11534336 | tf_op jit(solution)/shard_map/dot_general | solution.py:97
  256.0 0.0 copy-start.4
  256.0 5.7 %all-to-all-start.1 = ((bf16[16,128,2048]{2,1,0:T(8,128)(2,1)}), bf16[16,128,2048]{2,1,0:T(8,128)(2,1)}, u32[]{:S(2)}, u32[]{:S(2)}) async-start(bf16[16,128,2048]{2,1,0:T(8,128)(2,1)} %bitcast.83), calls=%async_computation.2 | async-start | bytes 16777216 | tf_op jit(solution)/shard_map/all_to_all | solution.py:99
  261.8 0.0 copy-done.4
  261.8 0.1 copy.31
  261.9 182.2 %all-to-all-done.1 = bf16[16,128,2048]{2,1,0:T(8,128)(2,1)} async-done(((bf16[16,128,2048]{2,1,0:T(8,128)(2,1)}), bf16[16,128,2048]{2,1,0:T(8,128)(2,1)}, u32[]{:S(2)}, u32[]{:S(2)}) %all-to-all-start.1) | async-done | bytes 8388640 | tf_op jit(solution)/shard_map/all_to_all | solution.py:99
  444.1 13.3 %gather_fusion.4 = bf16[1024,2048]{1,0:T(8,128)(2,1)} fusion(bf16[2048,2048]{1,0:T(8,128)(2,1)} %bitcast.25, s32[1024]{0:T(1024)S(1)} %broadcast_clamp_fusion), kind=kCustom, calls=%fused_computation.4 | custom fusion | bytes 8392704 | tf_op jit(solution)/shard_map/gather | solution.py:100
  457.4 6.5 %fusion = f32[128,2048]{1,0:T(8,128)S(1)} fusion(bf16[1024,2048]{1,0:T(8,128)(2,1)} %gather_fusion.4, f32[128,8]{1,0:T(8,128)S(1)} %copy.31), kind=kLoop, calls=%fused_computation.10 | loop fusion | flops 6029312 | bytes 5246976 | tf_op jit(solution)/shard_map/reduce_sum | solution.py:102
  463.9 0.9 fusion.17
  (16 shorter events, 0.2 us)
Async XLA Ops:
  6.5 242.7 %copy-start = (bf16[1,384,2048]{2,1,0:T(8,128)(2,1)S(1)}, bf16[1,384,2048]{2,1,0:T(8,128)(2,1)}, u32[]{:S(2)}) copy-start(bf16[1,384,2048]{2,1,0:T(8,128)(2,1)} %param.29) | copy-start | bytes 4718596
  6.5 7.9 %copy-start.2 = (bf16[256,128]{1,0:T(8,128)(2,1)S(1)}, bf16[256,128]{1,0:T(8,128)(2,1)}, u32[]{:S(2)}) copy-start(bf16[256,128]{1,0:T(8,128)(2,1)} %param.17) | copy-start | bytes 196612
  6.5 9.0 %copy-start.8 = (bf16[256,128]{1,0:T(8,128)(2,1)S(1)}, bf16[256,128]{1,0:T(8,128)(2,1)}, u32[]{:S(2)}) copy-start(bf16[256,128]{1,0:T(8,128)(2,1)} %param.16) | copy-start | bytes 196612
  6.5 31.8 %reduce-scatter.2.cloned.1.call-start = ((), (), s32[]{:S(2)}) async-start(), calls=%async_computation.3 | async-start | bytes 3145728 | tf_op jit(solution)/shard_map/reduce_scatter | solution.py:64
  21.7 4.9 %copy-start.3 = (s32[128,8]{0,1:T(8,128)S(1)}, s32[128,8]{0,1:T(8,128)}, u32[]{:S(2)}) copy-start(s32[128,8]{0,1:T(8,128)} %param.25) | copy-start | bytes 12292
  21.7 16.6 %copy-start.1 = (bf16[128,2048]{1,0:T(8,128)(2,1)S(1)}, bf16[128,2048]{1,0:T(8,128)(2,1)}, u32[]{:S(2)}) copy-start(bf16[128,2048]{1,0:T(8,128)(2,1)} %param.23) | copy-start | bytes 1572868
  26.6 13.2 %copy-start.5 = (f32[2048]{0:T(1024)S(1)}, f32[2048]{0:T(1024)}, u32[]{:S(2)}) copy-start(f32[2048]{0:T(1024)} %param.24) | copy-start | bytes 24580
  51.1 188.2 %copy-start.6 = (bf16[1,2048,384]{2,1,0:T(8,128)(2,1)S(1)}, bf16[1,2048,384]{2,1,0:T(8,128)(2,1)}, u32[]{:S(2)}) copy-start(bf16[1,2048,384]{2,1,0:T(8,128)(2,1)} %param.27) | copy-start | bytes 4718596
  239.3 4.6 copy-start.7
  256.0 5.7 %copy-start.4 = (f32[128,8]{0,1:T(8,128)S(1)}, f32[128,8]{0,1:T(8,128)}, u32[]{:S(2)}) copy-start(f32[128,8]{0,1:T(8,128)} %param.26) | copy-start | bytes 12292
  256.0 188.1 %all-to-all-start.1 = ((bf16[16,128,2048]{2,1,0:T(8,128)(2,1)}), bf16[16,128,2048]{2,1,0:T(8,128)(2,1)}, u32[]{:S(2)}, u32[]{:S(2)}) async-start(bf16[16,128,2048]{2,1,0:T(8,128)(2,1)} %bitcast.83), calls=%async_computation.2 | async-start | bytes 16777216 | tf_op jit(solution)/shard_map/all_to_all | solution.py:99
Sparse Core Ops, SparseCore 0:
  26.7 11.5 reduce-scatter.1
where the time goes:
time: 472 us
  blocking collectives  188 us (40%)
  waiting for transfers between devices  184 us (39%)
  local copies, waits for them, and re-layouts  36.8 us (8%)
  matrix products  26.1 us (6%)
  other arithmetic  17.1 us (4%)
  between operations  13.7 us (3%)
  starting transfers between devices  5.74 us (1%)
    all_to_all x1, blocking collectives, per_device(): lax.all_to_all(outgoing, ('expert', 'attn'), split_axis=0, concat_axis=0,...  188 us
    all_to_all x1, waiting for transfers between devices, per_device(): lax.all_to_all(computed, ('expert', 'attn'), split_axis=0, concat_axis=0,...  182 us
    gather x1, local copies, waits for them, and re-layouts, per_device(): returned.reshape(experts * capacity, model_width)[slot_target]  13.3 us
    gather x1, local copies, waits for them, and re-layouts, per_device(): outgoing = padded_rows[source_row].reshape(experts, capacity, model_width)  11 us
  transfers between devices with their start and end apart: 2, of which 2 were waited for; matrix products, arithmetic and copies ran while one was open for 2% of the time, Pallas kernels for 0%

commit v1 on v0

--- a/solution.py
+++ b/solution.py
@@ -11,33 +11,17 @@
 negative_fill = -1e30
 
 
-def per_device(
-    queries,
-    new_keys,
-    new_values,
-    cache_keys,
-    cache_values,
-    cache_len,
-    span_req,
-    out_proj,
-    resid,
-    norm_gain,
-    routes,
-    gates,
-    w_gate,
-    w_up,
-    w_down,
-):
-    n_attn = lax.axis_size("attn")
-    n_expert = lax.axis_size("expert")
+def ring_order(count):
+    return list(range(0, count, 2)) + list(range(count - 1, 0, -2))
+
+
+def attend(queries, new_keys, new_values, cache_keys, cache_values, cache_len, span_req):
     spans = cache_keys.shape[0]
     cache_size = cache_keys.shape[1]
     length = queries.shape[0] // spans
     kv_local = cache_keys.shape[2] // HD
     head_count = queries.shape[1] // HD
     group_size = head_count // kv_local
-    model_width = resid.shape[1]
-    own_rows = resid.shape[0]
     local_req = span_req % spans
     lengths = cache_len[local_req]
     queries_split = queries.reshape(spans, length, kv_local, group_size, HD)
@@ -60,20 +44,12 @@
     attended = jnp.einsum(
         "cgqlk,ckgd->clgqd", weights, all_values, preferred_element_type=jnp.float32
     )
-    attended = attended.astype(jnp.bfloat16).reshape(spans * length, head_count * HD)
-    attn_out = lax.psum_scatter(
-        jnp.dot(attended, out_proj, preferred_element_type=jnp.float32),
-        "attn",
-        scatter_dimension=0,
-        tiled=True,
-    )
-    hidden = (resid.astype(jnp.float32) + attn_out).astype(jnp.bfloat16)
-    state_float = hidden.astype(jnp.float32)
-    mean_square = jnp.mean(state_float * state_float, axis=-1, keepdims=True)
-    normed = (state_float * lax.rsqrt(mean_square + 1e-06) * norm_gain).astype(jnp.bfloat16)
+    return attended.astype(jnp.bfloat16).reshape(spans * length, head_count * HD)
+
+
+def routed_mix(normed, routes, gates, w_gate, w_up, w_down, capacity, experts):
+    own_rows, model_width = normed.shape
     top_count = routes.shape[1]
-    experts = n_expert * n_attn
-    capacity = 2 * top_count * own_rows // experts
     flat_routes = routes.reshape(-1)
     one_hot = (flat_routes[:, None] == jnp.arange(experts, dtype=jnp.int32)[None, :]).astype(
         jnp.int32
@@ -99,9 +75,135 @@
     returned = lax.all_to_all(computed, ("expert", "attn"), split_axis=0, concat_axis=0, tiled=True)
     picked = returned.reshape(experts * capacity, model_width)[slot_target].astype(jnp.float32)
     weight = gates / jnp.sum(gates, axis=-1, keepdims=True)
-    mixed = jnp.sum(
+    return jnp.sum(
         (picked * weight.reshape(-1, 1)).reshape(own_rows, top_count, model_width), axis=1
     )
+
+
+def ring_mix(normed, table, weights, n_expert):
+    order = ring_order(n_expert)
+    up = [(order[i], order[(i + 1) % n_expert]) for i in range(n_expert)]
+    down = [(b, a) for a, b in up]
+    place = jnp.zeros((n_expert,), jnp.int32).at[jnp.array(order)].set(jnp.arange(n_expert))
+    order_of = jnp.array(order, jnp.int32)
+    e = lax.axis_index("expert")
+    c = lax.axis_index("attn")
+    mine = place[e]
+    rows = normed.shape[0]
+    half = rows // 2
+    tables = table.T[None]
+    for bit in range(n_expert.bit_length() - 1):
+        swap = [(i, i ^ (1 << bit)) for i in range(n_expert)]
+        tables = jnp.concatenate([tables, lax.ppermute(tables, "expert", swap)], axis=0)
+    (g0, u0, d0), (g1, u1, d1) = weights
+
+    def column(source, expert):
+        return lax.dynamic_slice(tables, (source ^ e, expert, 0), (1, 1, rows)).reshape(rows, 1)
+
+    def contribution(block, source, lo, hi):
+        out = None
+        for g, u, d, expert in ((g0, u0, d0, 2 * e + c), (g1, u1, d1, 2 * e + 1 - c)):
+            scale = column(source, expert)[lo:hi]
+            gate_part = jnp.dot(block, g, preferred_element_type=jnp.float32)
+            up_part = jnp.dot(block, u, preferred_element_type=jnp.float32)
+            act = (jax.nn.silu(gate_part) * up_part * scale).astype(jnp.bfloat16)
+            part = jnp.dot(act, d, preferred_element_type=jnp.float32)
+            out = part if out is None else out + part
+        return lax.optimization_barrier(out)
+
+    reach = n_expert // 2
+    ahead = behind = normed
+    parts_up, parts_down = {}, {}
+    home = contribution(normed, e, 0, rows)
+    for step in range(1, reach + 1):
+        if step < reach:
+            ahead = lax.ppermute(ahead, "expert", up)
+            behind = lax.ppermute(behind, "expert", down)
+            src_a = order_of[(mine - step) % n_expert]
+            src_b = order_of[(mine + step) % n_expert]
+            parts_down[step] = contribution(ahead, src_a, 0, rows)
+            parts_up[step] = contribution(behind, src_b, 0, rows)
+        else:
+            ahead = lax.ppermute(ahead[:half], "expert", up)
+            behind = lax.ppermute(behind[half:], "expert", down)
+            src = order_of[(mine + reach) % n_expert]
+            both = contribution(jnp.concatenate([ahead, behind], axis=0), src, 0, rows)
+            parts_up[step] = both[:half]
+            parts_down[step] = both[half:]
+    got_up = lax.ppermute(parts_up[reach].astype(jnp.bfloat16), "expert", up)
+    got_down = lax.ppermute(parts_down[reach].astype(jnp.bfloat16), "expert", down)
+    for step in range(reach - 1, 0, -1):
+        if step == reach - 1:
+            p = parts_up[step]
+            send_up = jnp.concatenate([p[:half] + got_up.astype(jnp.float32), p[half:]], axis=0)
+            q = parts_down[step]
+            send_down = jnp.concatenate([q[:half], q[half:] + got_down.astype(jnp.float32)], axis=0)
+        else:
+            send_up = parts_up[step] + got_up.astype(jnp.float32)
+            send_down = parts_down[step] + got_down.astype(jnp.float32)
+        got_up = lax.ppermute(send_up.astype(jnp.bfloat16), "expert", up)
+        got_down = lax.ppermute(send_down.astype(jnp.bfloat16), "expert", down)
+    return home + got_up.astype(jnp.float32) + got_down.astype(jnp.float32)
+
+
+def per_device(
+    queries,
+    new_keys,
+    new_values,
+    cache_keys,
+    cache_values,
+    cache_len,
+    span_req,
+    out_proj,
+    resid,
+    norm_gain,
+    routes,
+    gates,
+    w_gate,
+    w_up,
+    w_down,
+):
+    n_attn = lax.axis_size("attn")
+    n_expert = lax.axis_size("expert")
+    own_rows = resid.shape[0]
+    top_count = routes.shape[1]
+    experts = n_expert * n_attn
+    capacity = min(own_rows, 2 * top_count * own_rows // experts)
+    dense = capacity == own_rows and n_attn == 2 and n_expert > 2 and n_expert & (n_expert - 1) == 0
+    swap = [(0, 1), (1, 0)]
+    if dense:
+        mine = (w_gate[0], w_up[0], w_down[0])
+        other = tuple(lax.ppermute(w, "attn", swap) for w in mine)
+    attended = attend(
+        queries, new_keys, new_values, cache_keys, cache_values, cache_len, span_req
+    )
+    if dense:
+        c = lax.axis_index("attn")
+        near = lax.dynamic_slice_in_dim(attended, c * own_rows, own_rows, 0)
+        far = lax.dynamic_slice_in_dim(attended, (1 - c) * own_rows, own_rows, 0)
+        theirs = jnp.dot(far, out_proj, preferred_element_type=jnp.float32)
+        theirs = lax.ppermute(theirs, "attn", swap)
+        attn_out = jnp.dot(near, out_proj, preferred_element_type=jnp.float32) + theirs
+    else:
+        attn_out = lax.psum_scatter(
+            jnp.dot(attended, out_proj, preferred_element_type=jnp.float32),
+            "attn",
+            scatter_dimension=0,
+            tiled=True,
+        )
+    hidden = (resid.astype(jnp.float32) + attn_out).astype(jnp.bfloat16)
+    state_float = hidden.astype(jnp.float32)
+    mean_square = jnp.mean(state_float * state_float, axis=-1, keepdims=True)
+    normed = (state_float * lax.rsqrt(mean_square + 1e-06) * norm_gain).astype(jnp.bfloat16)
+    if dense:
+        weight = gates / jnp.sum(gates, axis=-1, keepdims=True)
+        names = jnp.arange(experts, dtype=jnp.int32)
+        table = jnp.sum(
+            jnp.where(routes[:, :, None] == names[None, None, :], weight[:, :, None], 0.0), axis=1
+        )
+        mixed = ring_mix(normed, table, (mine, other), n_expert)
+    else:
+        mixed = routed_mix(normed, routes, gates, w_gate, w_up, w_down, capacity, experts)
     return (state_float + mixed).astype(jnp.bfloat16)
 
 

time: 472 us -> 190 us (0.40)
  the two profiles are of different devices: /device:TPU:13 before, /device:TPU:0 now
where the time goes in v1:
time: 190 us; the launch traced here: 189 us
  matrix products  99.6 us (52%)
  starting transfers between devices  25.3 us (13%)
  waiting for transfers between devices  23.6 us (12%)
  other arithmetic  16.5 us (9%)
  local copies, waits for them, and re-layouts  14.1 us (7%)
  between operations  9.64 us (5%)
    dot_general x16, matrix products, contribution(): part = jnp.dot(act, d, preferred_element_type=jnp.float32)  58.4 us
    dot_general x16, matrix products, contribution(): gate_part = jnp.dot(block, g, preferred_element_type=jnp.float32)  30.2 us
    ppermute x3, waiting for transfers between devices, ring_mix(): behind = lax.ppermute(behind, 'expert', down)  8.73 us
    ppermute x3, starting transfers between devices, ring_mix(): lax.ppermute(tables, 'expert', swap)  7.68 us
    ppermute x3, waiting for transfers between devices, ring_mix(): got_up = lax.ppermute(send_up.astype(jnp.bfloat16), 'expert', up)  5.09 us
    ppermute x3, starting transfers between devices, ring_mix(): got_up = lax.ppermute(send_up.astype(jnp.bfloat16), 'expert', up)  4.74 us
    ppermute x3, starting transfers between devices, ring_mix(): behind = lax.ppermute(behind, 'expert', down)  4.61 us
    convert_element_type x2, other arithmetic, ring_mix(): got_up = lax.ppermute(send_up.astype(jnp.bfloat16), 'expert', up)  4.59 us
  transfers between devices with their start and end apart: 23, of which 8 were waited for; matrix products, arithmetic and copies ran while one was open for 53% of the time, Pallas kernels for 0%

profile of v1, /device:TPU:0, one launch (start us, length us, event | category | flops | bytes accessed | tf_op | source)
XLA Modules:
  0.0 188.7 jit_solution(8585189943543621862)
XLA Ops:
  1.7 1.3 gather_fusion.1
  5.4 1.5 fusion.169
  6.9 1.3 fusion
  8.2 2.1 %fusion.9 = bf16[2,128,1,8,128]{1,4,3,0,2:T(8,128)(2,1)S(1)} fusion(f32[2,8,128]{2,1,0:T(8,128)S(1)} %fusion, f32[2,1,8,128,1152]{3,4,2,0,1:T(8,128)S(1)} %get-tuple-element.31, f32[2,8,128]{2,1,0:T(8,128)S(1)} %get-tuple-element.30, bf16[2,128,1,128]{1,3,0,2:T(8,128)(2,1)S(1)} %copy.30, bf16[2,1024,1,128]{1,3,0,2:T(8,128)(2,1)S(1)} %bitcast.236), kind=kOutput, calls=%fused_computation.22 | convolution fusion | flops 612499456 | bytes 10567680 | tf_op jit(solution)/shard_map/cgqlk,ckgd->clgqd/dot_general | solution.py:44
  10.7 4.1 %fusion.19 = f32[128,2048]{1,0:T(8,128)} fusion(bf16[1024,2048]{1,0:T(8,128)(2,1)} %param.24, bf16[256,1024]{1,0:T(8,128)(2,1)S(1)} %bitcast.233, s32[]{:T(128)S(6)} %select_n.144), kind=kOutput, calls=%fused_computation.49 | convolution fusion | flops 536870912 | bytes 5505028 | tf_op jit(solution)/shard_map/dot_general | solution.py:184
  15.3 2.6 %collective-permute-start.1 = (f32[1,16,128]{2,1,0:T(8,128)S(1)}, f32[1,16,128]{2,1,0:T(8,128)S(1)}, u32[]{:S(2)}, u32[]{:S(2)}) collective-permute-start(f32[1,16,128]{2,1,0:T(8,128)S(1)} %bitcast.239), channel_id=1, source_target_pairs={{0,2},{2,0},{4,6},{6,4},{8,10},{10,8},{12,14},{14,12},{1,3},{3,1},... | collective-permute-start | bytes 24584 | tf_op jit(solution)/shard_map/ppermute | solution.py:97
  17.9 1.6 collective-permute-done.1
  19.5 2.1 %collective-permute-start.2 = (f32[2,16,128]{2,1,0:T(8,128)S(1)}, f32[2,16,128]{2,1,0:T(8,128)S(1)}, u32[]{:S(2)}, u32[]{:S(2)}) collective-permute-start(f32[2,16,128]{2,1,0:T(8,128)S(1)} %pad_maximum_fusion.4), channel_id=1, source_target_pairs={{0,4},{2,6},{4,0},{6,2},{8,12},{10,14},{12,8},{14,10},{1,5},{3,7},... | collective-permute-start | bytes 49160 | tf_op jit(solution)/shard_map/ppermute | solution.py:97
  21.6 1.7 collective-permute-done.2
  23.3 3.0 %collective-permute-start.3 = (f32[4,16,128]{2,1,0:T(8,128)S(1)}, f32[4,16,128]{2,1,0:T(8,128)S(1)}, u32[]{:S(2)}, u32[]{:S(2)}) collective-permute-start(f32[4,16,128]{2,1,0:T(8,128)S(1)} %pad_maximum_fusion.3), channel_id=1, source_target_pairs={{0,8},{2,10},{4,12},{6,14},{8,0},{10,2},{12,4},{14,6},{1,9},{3,11}... | collective-permute-start | bytes 98312 | tf_op jit(solution)/shard_map/ppermute | solution.py:97
  37.9 3.4 %multiply_reduce_fusion = (f32[128]{0:T(128)S(1)}, f32[128,2048]{1,0:T(8,128)S(1)}) fusion(f32[128,2048]{1,0:T(8,128)} %collective-permute-done, bf16[1024,2048]{1,0:T(8,128)(2,1)} %param.24, bf16[256,1024]{1,0:T(8,128)(2,1)S(1)} %bitcast.234, s32[]{:T(128)S(6)} %select_n.143, bf16[128,2048]{1,0:T(8,128)(2,1)S(1)} %copy-done.24), kind=kOutput, calls=%fused_computation.30 | convolution fusion | flops 538705792 | bytes 7078404 | tf_op jit(solution)/shard_map/dot_general | solution.py:186
  41.5 1.6 collective-permute-start.7
  44.1 3.2 %fusion.22 = f32[128,2048]{1,0:T(8,128)} fusion(bf16[128,2048]{1,0:T(8,128)(2,1)S(1)} %multiply_convert_fusion, f32[128,384]{1,0:T(8,128)S(1)} %fusion.149, f32[128]{0:T(128)S(1)} %get-tuple-element.22, bf16[1,384,2048]{2,1,0:T(8,128)(2,1)S(1)} %copy-done.1, bf16[1,2048,384]{2,1,0:T(8,128)(2,1)} %param.30), kind=kOutput, calls=%fused_computation.68 | convolution fusion | flops 402997248 | bytes 4915712 | tf_op jit(solution)/shard_map/dot_general | solution.py:110
  47.3 8.7 %collective-permute-done.7 = bf16[128,2048]{1,0:T(8,128)(2,1)} collective-permute-done((bf16[128,2048]{1,0:T(8,128)(2,1)S(1)}, bf16[128,2048]{1,0:T(8,128)(2,1)}, u32[]{:S(2)}, u32[]{:S(2)}) %collective-permute-start.7) | collective-permute-done | bytes 524320 | tf_op jit(solution)/shard_map/ppermute | solution.py:121
  56.0 1.5 collective-permute-start.8
  57.6 2.0 %fusion.147 = f32[128,384]{1,0:T(8,128)S(1)} fusion(bf16[128,2048]{1,0:T(8,128)(2,1)} %collective-permute-done.7, bf16[1,2048,384]{2,1,0:T(8,128)(2,1)} %param.29), kind=kOutput, calls=%fused_computation.197 | convolution fusion | flops 201326592 | bytes 2293760 | tf_op jit(solution)/shard_map/dot_general | solution.py:107
  60.8 3.4 %fusion.23 = f32[128,2048]{1,0:T(8,128)} fusion(f32[128,384]{1,0:T(8,128)S(1)} %fusion.147, f32[128]{0:T(128)} %get-tuple-element.20, bf16[1,384,2048]{2,1,0:T(8,128)(2,1)S(1)} %copy-done.1, bf16[128,2048]{1,0:T(8,128)(2,1)} %collective-permute-done.7, bf16[1,2048,384]{2,1,0:T(8,128)(2,1)} %param.30), kind=kOutput, calls=%fused_computation.69 | convolution fusion | flops 402997248 | bytes 4915712 | tf_op jit(solution)/shard_map/dot_general | solution.py:110
  64.2 3.3 %fusion.27 = f32[128,2048]{1,0:T(8,128)} fusion(f32[128,384]{1,0:T(8,128)S(1)} %fusion.139, f32[128]{0:T(128)} %get-tuple-element.13, bf16[1,384,2048]{2,1,0:T(8,128)(2,1)S(1)} %copy-done.1, bf16[128,2048]{1,0:T(8,128)(2,1)S(1)} %collective-permute-done.10, bf16[1,2048,384]{2,1,0:T(8,128)(2,1)} %param.30), kind=kOutput, calls=%fused_computation.73 | convolution fusion | flops 402997248 | bytes 4915712 | tf_op jit(solution)/shard_map/dot_general | solution.py:110
  67.4 2.0 %fusion.187 = f32[128,384]{1,0:T(8,128)S(1)} fusion(bf16[128,2048]{1,0:T(8,128)(2,1)} %collective-permute-done.7, bf16[2048,384]{1,0:T(8,128)(2,1)} %collective-permute-done.4), kind=kOutput, calls=%fused_computation.229 | convolution fusion | flops 201326592 | bytes 2293760 | tf_op jit(solution)/shard_map/dot_general | solution.py:107
  69.5 2.5 %fusion.191 = f32[128,384]{1,0:T(8,128)} fusion(bf16[128,2048]{1,0:T(8,128)(2,1)S(1)} %collective-permute-done.10, bf16[2048,384]{1,0:T(8,128)(2,1)} %collective-permute-done.4), kind=kOutput, calls=%fused_computation.233 | convolution fusion | flops 201326592 | bytes 2293760 | tf_op jit(solution)/shard_map/dot_general | solution.py:107
  72.0 4.2 %convolution_add_fusion.6 = f32[128,2048]{1,0:T(8,128)} fusion(f32[128,2048]{1,0:T(8,128)} %fusion.23, bf16[384,2048]{1,0:T(8,128)(2,1)} %collective-permute-done.6, f32[128,384]{1,0:T(8,128)S(1)} %fusion.187, f32[128]{0:T(128)S(1)} %copy-done.33, bf16[128,2048]{1,0:T(8,128)(2,1)} %collective-permute-done.7, bf16[2048,384]{1,0:T(8,128)(2,1)} %collective-permute-done.5), kind=kOutput, calls=%fused_computation.15 | convolution fusion | flops 403259392 | bytes 5964288 | tf_op jit(solution)/shard_map/dot_general | solution.py:110
  76.2 1.5 collective-permute-start.9
  77.7 2.0 %fusion.145 = f32[128,384]{1,0:T(8,128)S(1)} fusion(bf16[128,2048]{1,0:T(8,128)(2,1)} %collective-permute-done.8, bf16[1,2048,384]{2,1,0:T(8,128)(2,1)} %param.29), kind=kOutput, calls=%fused_computation.195 | convolution fusion | flops 201326592 | bytes 2293760 | tf_op jit(solution)/shard_map/dot_general | solution.py:107
  79.7 2.1 %fusion.188 = f32[128,384]{1,0:T(8,128)S(1)} fusion(bf16[128,2048]{1,0:T(8,128)(2,1)} %collective-permute-done.8, bf16[2048,384]{1,0:T(8,128)(2,1)} %collective-permute-done.4), kind=kOutput, calls=%fused_computation.230 | convolution fusion | flops 201326592 | bytes 2293760 | tf_op jit(solution)/shard_map/dot_general | solution.py:107
  82.4 2.2 %fusion.137 = f32[128,384]{1,0:T(8,128)} fusion(bf16[128,2048]{1,0:T(8,128)(2,1)} %collective-permute-done.11, bf16[1,2048,384]{2,1,0:T(8,128)(2,1)S(1)} %copy-done.4), kind=kOutput, calls=%fused_computation.187 | convolution fusion | flops 201326592 | bytes 2293760 | tf_op jit(solution)/shard_map/dot_general | solution.py:107
  84.6 3.3 %fusion.24 = f32[128,2048]{1,0:T(8,128)} fusion(f32[128,384]{1,0:T(8,128)S(1)} %fusion.145, f32[128]{0:T(128)} %get-tuple-element.18, bf16[1,384,2048]{2,1,0:T(8,128)(2,1)S(1)} %copy-done.1, bf16[128,2048]{1,0:T(8,128)(2,1)} %collective-permute-done.8, bf16[1,2048,384]{2,1,0:T(8,128)(2,1)} %param.30), kind=kOutput, calls=%fused_computation.70 | convolution fusion | flops 402997248 | bytes 4915712 | tf_op jit(solution)/shard_map/dot_general | solution.py:110
  88.0 3.4 %fusion.28 = f32[128,2048]{1,0:T(8,128)} fusion(f32[128,384]{1,0:T(8,128)} %fusion.137, f32[128]{0:T(128)} %get-tuple-element.11, bf16[1,384,2048]{2,1,0:T(8,128)(2,1)S(1)} %copy-done.1, bf16[128,2048]{1,0:T(8,128)(2,1)} %collective-permute-done.11, bf16[1,2048,384]{2,1,0:T(8,128)(2,1)} %param.30), kind=kOutput, calls=%fused_computation.74 | convolution fusion | flops 402997248 | bytes 4915712 | tf_op jit(solution)/shard_map/dot_general | solution.py:110
  91.4 2.7 %fusion.192 = f32[128,384]{1,0:T(8,128)} fusion(bf16[128,2048]{1,0:T(8,128)(2,1)} %collective-permute-done.11, bf16[2048,384]{1,0:T(8,128)(2,1)} %collective-permute-done.4), kind=kOutput, calls=%fused_computation.234 | convolution fusion | flops 201326592 | bytes 2293760 | tf_op jit(solution)/shard_map/dot_general | solution.py:107
  94.1 4.1 %convolution_add_fusion.5 = f32[128,2048]{1,0:T(8,128)} fusion(f32[128,2048]{1,0:T(8,128)} %fusion.24, bf16[384,2048]{1,0:T(8,128)(2,1)} %collective-permute-done.6, f32[128,384]{1,0:T(8,128)S(1)} %fusion.188, f32[128]{0:T(128)S(1)} %copy-done.32, bf16[128,2048]{1,0:T(8,128)(2,1)} %collective-permute-done.8, bf16[2048,384]{1,0:T(8,128)(2,1)} %collective-permute-done.5), kind=kOutput, calls=%fused_computation.14 | convolution fusion | flops 403259392 | bytes 5964288 | tf_op jit(solution)/shard_map/dot_general | solution.py:110
  98.9 1.6 collective-permute-start.13
  100.5 1.7 slice.44
  102.6 2.7 %fusion.143 = f32[128,384]{1,0:T(8,128)} fusion(bf16[128,2048]{1,0:T(8,128)(2,1)} %collective-permute-done.9, bf16[1,2048,384]{2,1,0:T(8,128)(2,1)} %param.29), kind=kOutput, calls=%fused_computation.193 | convolution fusion | flops 201326592 | bytes 2293760 | tf_op jit(solution)/shard_map/dot_general | solution.py:107
  105.3 2.1 %fusion.189 = f32[128,384]{1,0:T(8,128)S(1)} fusion(bf16[128,2048]{1,0:T(8,128)(2,1)} %collective-permute-done.9, bf16[2048,384]{1,0:T(8,128)(2,1)} %collective-permute-done.4), kind=kOutput, calls=%fused_computation.231 | convolution fusion | flops 201326592 | bytes 2293760 | tf_op jit(solution)/shard_map/dot_general | solution.py:107
  107.9 3.4 %fusion.25 = f32[128,2048]{1,0:T(8,128)} fusion(f32[128,384]{1,0:T(8,128)} %fusion.143, f32[128]{0:T(128)} %get-tuple-element.16, bf16[1,384,2048]{2,1,0:T(8,128)(2,1)S(1)} %copy-done.1, bf16[128,2048]{1,0:T(8,128)(2,1)} %collective-permute-done.9, bf16[1,2048,384]{2,1,0:T(8,128)(2,1)} %param.30), kind=kOutput, calls=%fused_computation.71 | convolution fusion | flops 402997248 | bytes 4915712 | tf_op jit(solution)/shard_map/dot_general | solution.py:110
  111.4 3.2 %fusion.29 = f32[128,2048]{1,0:T(8,128)} fusion(f32[128,384]{1,0:T(8,128)S(1)} %fusion.135, f32[128]{0:T(128)} %get-tuple-element.9, bf16[1,384,2048]{2,1,0:T(8,128)(2,1)S(1)} %copy-done.1, bf16[128,2048]{1,0:T(8,128)(2,1)S(1)} %collective-permute-done.12, bf16[1,2048,384]{2,1,0:T(8,128)(2,1)} %param.30), kind=kOutput, calls=%fused_computation.75 | convolution fusion | flops 402997248 | bytes 4915712 | tf_op jit(solution)/shard_map/dot_general | solution.py:110
  114.6 4.2 %convolution_add_fusion.4 = f32[128,2048]{1,0:T(8,128)} fusion(f32[128,2048]{1,0:T(8,128)} %fusion.25, bf16[384,2048]{1,0:T(8,128)(2,1)} %collective-permute-done.6, f32[128,384]{1,0:T(8,128)S(1)} %fusion.189, f32[128]{0:T(128)} %get-tuple-element.7, bf16[128,2048]{1,0:T(8,128)(2,1)} %collective-permute-done.9, bf16[2048,384]{1,0:T(8,128)(2,1)} %collective-permute-done.5), kind=kOutput, calls=%fused_computation.13 | convolution fusion | flops 403259392 | bytes 5964288 | tf_op jit(solution)/shard_map/dot_general | solution.py:110
  118.8 2.6 %fusion.193 = f32[128,384]{1,0:T(8,128)} fusion(bf16[128,2048]{1,0:T(8,128)(2,1)S(1)} %collective-permute-done.12, bf16[2048,384]{1,0:T(8,128)(2,1)} %collective-permute-done.4), kind=kOutput, calls=%fused_computation.235 | convolution fusion | flops 201326592 | bytes 2293760 | tf_op jit(solution)/shard_map/dot_general | solution.py:107
  121.4 1.1 slice.59
  123.5 1.0 constant_dynamic-update-slice_fusion
  124.5 1.1 fusion.141
  125.6 3.3 %fusion.26 = f32[128,2048]{1,0:T(8,128)} fusion(f32[128,384]{1,0:T(8,128)} %fusion.141, f32[128]{0:T(128)S(1)} %copy-done.31, bf16[1,384,2048]{2,1,0:T(8,128)(2,1)S(1)} %copy-done.1, bf16[128,2048]{1,0:T(8,128)(2,1)} %copy-done.7, bf16[1,2048,384]{2,1,0:T(8,128)(2,1)} %param.30), kind=kOutput, calls=%fused_computation.72 | convolution fusion | flops 402997248 | bytes 4915712 | tf_op jit(solution)/shard_map/dot_general | solution.py:110
  129.0 2.8 %fusion.190 = f32[128,384]{1,0:T(8,128)} fusion(bf16[128,2048]{1,0:T(8,128)(2,1)} %copy-done.7, bf16[2048,384]{1,0:T(8,128)(2,1)} %collective-permute-done.4), kind=kOutput, calls=%fused_computation.232 | convolution fusion | flops 201326592 | bytes 2293760 | tf_op jit(solution)/shard_map/dot_general | solution.py:107
  131.8 3.7 %convolution_add_fusion.3 = bf16[128,2048]{1,0:T(8,128)(2,1)} fusion(f32[128,2048]{1,0:T(8,128)S(1)} %copy-done.16, bf16[384,2048]{1,0:T(8,128)(2,1)} %collective-permute-done.6, f32[128,384]{1,0:T(8,128)} %fusion.190, f32[128]{0:T(128)S(1)} %copy-done.30, bf16[128,2048]{1,0:T(8,128)(2,1)S(1)} %copy-done.8, bf16[2048,384]{1,0:T(8,128)(2,1)} %collective-permute-done.5), kind=kOutput, calls=%fused_computation.12 | convolution fusion | flops 403521536 | bytes 5440000 | tf_op jit(solution)/shard_map/dot_general | solution.py:110
  135.5 1.9 fusion.167
  137.3 1.6 collective-permute-start.15
  138.9 3.8 %convolution_add_fusion = f32[128,2048]{1,0:T(8,128)} fusion(f32[128,2048]{1,0:T(8,128)S(1)} %copy-done.15, bf16[384,2048]{1,0:T(8,128)(2,1)} %collective-permute-done.6, f32[128,384]{1,0:T(8,128)} %fusion.193, f32[128]{0:T(128)S(1)} %get-tuple-element.8, bf16[128,2048]{1,0:T(8,128)(2,1)S(1)} %collective-permute-done.12, ...), kind=kOutput, calls=%fused_computation.9 | convolution fusion | flops 403259392 | bytes 5964288 | tf_op jit(solution)/shard_map/dot_general | solution.py:110
  142.8 1.2 slice.58
  144.4 1.2 fusion.17
  146.4 1.6 collective-permute-start.16
  148.0 3.3 %collective-permute-done.19 = bf16[64,2048]{1,0:T(8,128)(2,1)S(1)} collective-permute-done((bf16[64,2048]{1,0:T(8,128)(2,1)}, bf16[64,2048]{1,0:T(8,128)(2,1)S(1)}, u32[]{:S(2)}, u32[]{:S(2)}) %collective-permute-start.19) | collective-permute-done | bytes 262176 | tf_op jit(solution)/shard_map/ppermute | solution.py:134
  151.9 3.9 %convolution_add_fusion.1 = f32[128,2048]{1,0:T(8,128)} fusion(f32[128,2048]{1,0:T(8,128)S(1)} %copy-done.14, bf16[384,2048]{1,0:T(8,128)(2,1)} %collective-permute-done.6, f32[128,384]{1,0:T(8,128)S(1)} %copy-done.21, f32[128]{0:T(128)S(1)} %get-tuple-element.10, bf16[128,2048]{1,0:T(8,128)(2,1)} %collective-permute-done.11, ...), kind=kOutput, calls=%fused_computation.10 | convolution fusion | flops 403259392 | bytes 5964288 | tf_op jit(solution)/shard_map/dot_general | solution.py:110
  155.8 2.2 %collective-permute-done.16 = bf16[128,2048]{1,0:T(8,128)(2,1)} collective-permute-done((bf16[128,2048]{1,0:T(8,128)(2,1)}, bf16[128,2048]{1,0:T(8,128)(2,1)}, u32[]{:S(2)}, u32[]{:S(2)}) %collective-permute-start.16) | collective-permute-done | bytes 524320 | tf_op jit(solution)/shard_map/ppermute | solution.py:144
  158.0 2.3 %add_convert_fusion.4 = bf16[128,2048]{1,0:T(8,128)(2,1)} fusion(f32[128,2048]{1,0:T(8,128)} %convolution_add_fusion.5, bf16[128,2048]{1,0:T(8,128)(2,1)} %collective-permute-done.16), kind=kLoop, calls=%fused_computation.28 | loop fusion | flops 786432 | bytes 2097152 | tf_op jit(solution)/shard_map/convert_element_type | solution.py:144
  160.3 1.6 collective-permute-start.17
  161.9 2.0 %add_convert_fusion.2 = bf16[128,2048]{1,0:T(8,128)(2,1)} fusion(f32[128,2048]{1,0:T(8,128)S(1)} %copy-done.17, bf16[128,2048]{1,0:T(8,128)(2,1)} %collective-permute-done.20), kind=kLoop, calls=%fused_computation.26 | loop fusion | flops 786432 | bytes 2097152 | tf_op jit(solution)/shard_map/convert_element_type | solution.py:145
  164.3 3.7 %convolution_add_fusion.2 = f32[128,2048]{1,0:T(8,128)} fusion(f32[128,2048]{1,0:T(8,128)S(1)} %copy-done.13, bf16[384,2048]{1,0:T(8,128)(2,1)} %collective-permute-done.6, f32[128,384]{1,0:T(8,128)S(1)} %copy-done.20, f32[128]{0:T(128)S(1)} %get-tuple-element.12, bf16[128,2048]{1,0:T(8,128)(2,1)S(1)} %copy-done.12, ...), kind=kOutput, calls=%fused_computation.11 | convolution fusion | flops 403259392 | bytes 5964288 | tf_op jit(solution)/shard_map/dot_general | solution.py:110
  168.1 2.9 %collective-permute-done.17 = bf16[128,2048]{1,0:T(8,128)(2,1)} collective-permute-done((bf16[128,2048]{1,0:T(8,128)(2,1)}, bf16[128,2048]{1,0:T(8,128)(2,1)}, u32[]{:S(2)}, u32[]{:S(2)}) %collective-permute-start.17) | collective-permute-done | bytes 524320 | tf_op jit(solution)/shard_map/ppermute | solution.py:144
  171.0 2.3 %add_convert_fusion.3 = bf16[128,2048]{1,0:T(8,128)(2,1)} fusion(f32[128,2048]{1,0:T(8,128)} %convolution_add_fusion.6, bf16[128,2048]{1,0:T(8,128)(2,1)} %collective-permute-done.17), kind=kLoop, calls=%fused_computation.27 | loop fusion | flops 786432 | bytes 2097152 | tf_op jit(solution)/shard_map/convert_element_type | solution.py:144
  173.3 1.6 collective-permute-start.18
  174.8 1.9 %add_convert_fusion.1 = bf16[128,2048]{1,0:T(8,128)(2,1)} fusion(f32[128,2048]{1,0:T(8,128)S(1)} %copy-done.18, bf16[128,2048]{1,0:T(8,128)(2,1)} %collective-permute-done.21), kind=kLoop, calls=%fused_computation.25 | loop fusion | flops 786432 | bytes 2097152 | tf_op jit(solution)/shard_map/convert_element_type | solution.py:145
  177.2 1.8 fusion.186
  179.1 4.1 %convolution_add_fusion.7 = f32[128,2048]{1,0:T(8,128)} fusion(f32[128,2048]{1,0:T(8,128)} %fusion.22, bf16[384,2048]{1,0:T(8,128)(2,1)} %collective-permute-done.6, f32[128,384]{1,0:T(8,128)S(1)} %fusion.186, f32[128]{0:T(128)S(1)} %get-tuple-element.21, bf16[128,2048]{1,0:T(8,128)(2,1)S(1)} %multiply_convert_fusion, ...), kind=kOutput, calls=%fused_computation.16 | convolution fusion | flops 403259392 | bytes 5964288 | tf_op jit(solution)/shard_map/dot_general | solution.py:110
  183.2 3.1 %collective-permute-done.22 = bf16[128,2048]{1,0:T(8,128)(2,1)} collective-permute-done((bf16[128,2048]{1,0:T(8,128)(2,1)}, bf16[128,2048]{1,0:T(8,128)(2,1)}, u32[]{:S(2)}, u32[]{:S(2)}) %collective-permute-start.22) | collective-permute-done | bytes 524320 | tf_op jit(solution)/shard_map/ppermute | solution.py:145
  186.3 2.4 %add_convert_fusion = bf16[128,2048]{1,0:T(8,128)(2,1)} fusion(f32[128,2048]{1,0:T(8,128)S(1)} %copy-done.10, bf16[128,2048]{1,0:T(8,128)(2,1)} %collective-permute-done.22, f32[128,2048]{1,0:T(8,128)} %convolution_add_fusion.7, bf16[128,2048]{1,0:T(8,128)(2,1)S(1)} %collective-permute-done.18), kind=kLoop, calls=%fused_computation.24 | loop fusion | flops 1572864 | bytes 3670016 | tf_op jit(solution)/shard_map/convert_element_type | solution.py:207
  (133 shorter events, 15.7 us)
Async XLA Ops:
  0.0 1.1 copy-start
  0.0 3.3 %copy-start.22 = (bf16[256,1024]{1,0:T(8,128)(2,1)S(1)}, bf16[256,1024]{1,0:T(8,128)(2,1)}, u32[]{:S(2)}) copy-start(bf16[256,1024]{1,0:T(8,128)(2,1)} %param.17) | copy-start | bytes 1572868
  0.0 3.4 %copy-start.23 = (bf16[2,1024,128]{2,1,0:T(8,128)(2,1)S(1)}, bf16[2,1024,128]{2,1,0:T(8,128)(2,1)}, u32[]{:S(2)}) copy-start(bf16[2,1024,128]{2,1,0:T(8,128)(2,1)} %param.21) | copy-start | bytes 1572868
  3.3 1.0 copy-start.25
  3.4 1.9 %copy-start.34 = (bf16[256,128]{1,0:T(8,128)(2,1)S(1)}, bf16[256,128]{1,0:T(8,128)(2,1)}, u32[]{:S(2)}) copy-start(bf16[256,128]{1,0:T(8,128)(2,1)} %param.18) | copy-start | bytes 196612
  10.6 4.6 %copy-start.27 = (f32[128,8]{0,1:T(8,128)S(1)}, f32[128,8]{0,1:T(8,128)}, u32[]{:S(2)}) copy-start(f32[128,8]{0,1:T(8,128)} %param.28) | copy-start | bytes 12292
  10.7 4.7 %copy-start.29 = (s32[128,8]{0,1:T(8,128)S(1)}, s32[128,8]{0,1:T(8,128)}, u32[]{:S(2)}) copy-start(s32[128,8]{0,1:T(8,128)} %param.27) | copy-start | bytes 12292
  10.7 16.2 %copy-start.1 = (bf16[1,384,2048]{2,1,0:T(8,128)(2,1)S(1)}, bf16[1,384,2048]{2,1,0:T(8,128)(2,1)}, u32[]{:S(2)}) copy-start(bf16[1,384,2048]{2,1,0:T(8,128)(2,1)} %param.31) | copy-start | bytes 4718596
  10.7 16.2 %copy-start.35 = (s32[8]{0:T(128)S(1)}, s32[8]{0:T(128)}, u32[]{:S(2)}) copy-start(s32[8]{0:T(128)} %constant.140) | copy-start | bytes 100
  10.7 21.5 %copy-start.26 = (s32[8]{0:T(128)S(1)}, s32[8]{0:T(128)}, u32[]{:S(2)}) copy-start(s32[8]{0:T(128)} %constant.128.clone) | copy-start | bytes 100
  10.7 27.2 %copy-start.24 = (bf16[128,2048]{1,0:T(8,128)(2,1)S(1)}, bf16[128,2048]{1,0:T(8,128)(2,1)}, u32[]{:S(2)}) copy-start(bf16[128,2048]{1,0:T(8,128)(2,1)} %param.25) | copy-start | bytes 1572868
  14.8 23.1 %collective-permute-start = (f32[128,2048]{1,0:T(8,128)}, f32[128,2048]{1,0:T(8,128)}, u32[]{:S(2)}, u32[]{:S(2)}) collective-permute-start(f32[128,2048]{1,0:T(8,128)} %fusion.19), channel_id=1, source_target_pairs={{0,1},{1,0},{2,3},{3,2},{4,5},{5,4},{6,7},{7,6},{8,9},{9,8},{10,11... | collective-permute-start | bytes 3145736 | tf_op jit(solution)/shard_map/ppermute | solution.py:185
  15.3 4.2 %collective-permute-start.1 = (f32[1,16,128]{2,1,0:T(8,128)S(1)}, f32[1,16,128]{2,1,0:T(8,128)S(1)}, u32[]{:S(2)}, u32[]{:S(2)}) collective-permute-start(f32[1,16,128]{2,1,0:T(8,128)S(1)} %bitcast.239), channel_id=1, source_target_pairs={{0,2},{2,0},{4,6},{6,4},{8,10},{10,8},{12,14},{14,12},{1,3},{3,1},... | collective-permute-start | bytes 24584 | tf_op jit(solution)/shard_map/ppermute | solution.py:97
  19.5 3.8 %collective-permute-start.2 = (f32[2,16,128]{2,1,0:T(8,128)S(1)}, f32[2,16,128]{2,1,0:T(8,128)S(1)}, u32[]{:S(2)}, u32[]{:S(2)}) collective-permute-start(f32[2,16,128]{2,1,0:T(8,128)S(1)} %pad_maximum_fusion.4), channel_id=1, source_target_pairs={{0,4},{2,6},{4,0},{6,2},{8,12},{10,14},{12,8},{14,10},{1,5},{3,7},... | collective-permute-start | bytes 49160 | tf_op jit(solution)/shard_map/ppermute | solution.py:97
  23.3 13.9 %collective-permute-start.3 = (f32[4,16,128]{2,1,0:T(8,128)S(1)}, f32[4,16,128]{2,1,0:T(8,128)S(1)}, u32[]{:S(2)}, u32[]{:S(2)}) collective-permute-start(f32[4,16,128]{2,1,0:T(8,128)S(1)} %pad_maximum_fusion.3), channel_id=1, source_target_pairs={{0,8},{2,10},{4,12},{6,14},{8,0},{10,2},{12,4},{14,6},{1,9},{3,11}... | collective-permute-start | bytes 98312 | tf_op jit(solution)/shard_map/ppermute | solution.py:97
  26.4 41.1 %collective-permute-start.4 = (bf16[2048,384]{1,0:T(8,128)(2,1)}, bf16[2048,384]{1,0:T(8,128)(2,1)}, u32[]{:S(2)}, u32[]{:S(2)}) collective-permute-start(bf16[2048,384]{1,0:T(8,128)(2,1)} %bitcast.231), channel_id=1, source_target_pairs={{0,1},{1,0},{2,3},{3,2},{4,5},{5,4},{6,7},{7,6},{8,9},{9,8},{10,11... | collective-permute-start | bytes 4718600 | tf_op jit(solution)/shard_map/ppermute | solution.py:176
  26.4 45.6 %collective-permute-start.5 = (bf16[2048,384]{1,0:T(8,128)(2,1)}, bf16[2048,384]{1,0:T(8,128)(2,1)}, u32[]{:S(2)}, u32[]{:S(2)}) collective-permute-start(bf16[2048,384]{1,0:T(8,128)(2,1)} %bitcast.230), channel_id=1, source_target_pairs={{0,1},{1,0},{2,3},{3,2},{4,5},{5,4},{6,7},{7,6},{8,9},{9,8},{10,11... | collective-permute-start | bytes 4718600 | tf_op jit(solution)/shard_map/ppermute | solution.py:176
  26.9 45.1 %collective-permute-start.6 = (bf16[384,2048]{1,0:T(8,128)(2,1)S(1)}, bf16[384,2048]{1,0:T(8,128)(2,1)}, u32[]{:S(2)}, u32[]{:S(2)}) collective-permute-start(bf16[384,2048]{1,0:T(8,128)(2,1)S(1)} %bitcast.229), channel_id=1, source_target_pairs={{0,1},{1,0},{2,3},{3,2},{4,5},{5,4},{6,7},{7,6},{8,9},{9,8},{10,11... | collective-permute-start | bytes 4718600 | tf_op jit(solution)/shard_map/ppermute | solution.py:176
  37.9 3.5 %copy-start.28 = (f32[2048]{0:T(1024)S(1)}, f32[2048]{0:T(1024)}, u32[]{:S(2)}) copy-start(f32[2048]{0:T(1024)} %param.26) | copy-start | bytes 24580
  41.3 2.7 %copy-start.9 = (f32[128,2048]{1,0:T(8,128)}, f32[128,2048]{1,0:T(8,128)S(1)}, u32[]{:S(2)}) copy-start(f32[128,2048]{1,0:T(8,128)S(1)} %get-tuple-element.33) | copy-start | bytes 3145732
  41.4 2.3 %copy-start.2 = (bf16[1,2048,384]{2,1,0:T(8,128)(2,1)S(1)}, bf16[1,2048,384]{2,1,0:T(8,128)(2,1)}, u32[]{:S(2)}) copy-start(bf16[1,2048,384]{2,1,0:T(8,128)(2,1)} %param.29) | copy-start | bytes 4718596
  41.5 14.5 %collective-permute-start.7 = (bf16[128,2048]{1,0:T(8,128)(2,1)S(1)}, bf16[128,2048]{1,0:T(8,128)(2,1)}, u32[]{:S(2)}, u32[]{:S(2)}) collective-permute-start(bf16[128,2048]{1,0:T(8,128)(2,1)S(1)} %multiply_convert_fusion), channel_id=1, source_target_pairs={{4,0},{8,4},{12,8},{14,12},{10,14},{6,10},{2,6},{0,2},{5,1},{9,5},... | collective-permute-start | bytes 1572872 | tf_op jit(solution)/shard_map/ppermute | solution.py:121
  43.1 16.4 %collective-permute-start.10 = (bf16[128,2048]{1,0:T(8,128)(2,1)S(1)}, bf16[128,2048]{1,0:T(8,128)(2,1)S(1)}, u32[]{:S(2)}, u32[]{:S(2)}) collective-permute-start(bf16[128,2048]{1,0:T(8,128)(2,1)S(1)} %multiply_convert_fusion), channel_id=1, source_target_pairs={{0,4},{4,8},{8,12},{12,14},{14,10},{10,6},{6,2},{2,0},{1,5},{5,9},... | collective-permute-start | bytes 1572872 | tf_op jit(solution)/shard_map/ppermute | solution.py:120
  47.3 13.0 %copy-start.3 = (bf16[1,2048,384]{2,1,0:T(8,128)(2,1)S(1)}, bf16[1,2048,384]{2,1,0:T(8,128)(2,1)}, u32[]{:S(2)}) copy-start(bf16[1,2048,384]{2,1,0:T(8,128)(2,1)} %param.29) | copy-start | bytes 4718596
  56.0 20.1 %collective-permute-start.8 = (bf16[128,2048]{1,0:T(8,128)(2,1)}, bf16[128,2048]{1,0:T(8,128)(2,1)}, u32[]{:S(2)}, u32[]{:S(2)}) collective-permute-start(bf16[128,2048]{1,0:T(8,128)(2,1)} %collective-permute-done.7), channel_id=1, source_target_pairs={{4,0},{8,4},{12,8},{14,12},{10,14},{6,10},{2,6},{0,2},{5,1},{9,5},... | collective-permute-start | bytes 1572872 | tf_op jit(solution)/shard_map/ppermute | solution.py:121
  59.6 9.9 %copy-start.11 = (bf16[128,2048]{1,0:T(8,128)(2,1)}, bf16[128,2048]{1,0:T(8,128)(2,1)S(1)}, u32[]{:S(2)}) copy-start(bf16[128,2048]{1,0:T(8,128)(2,1)S(1)} %collective-permute-done.10) | copy-start | bytes 1572868
  59.6 22.3 %collective-permute-start.11 = (bf16[128,2048]{1,0:T(8,128)(2,1)S(1)}, bf16[128,2048]{1,0:T(8,128)(2,1)}, u32[]{:S(2)}, u32[]{:S(2)}) collective-permute-start(bf16[128,2048]{1,0:T(8,128)(2,1)S(1)} %collective-permute-done.10), channel_id=1, source_target_pairs={{0,4},{4,8},{8,12},{12,14},{14,10},{10,6},{6,2},{2,0},{1,5},{5,9},... | collective-permute-start | bytes 1572872 | tf_op jit(solution)/shard_map/ppermute | solution.py:120
  69.5 2.5 %copy-start.33 = (f32[128]{0:T(128)S(1)}, f32[128]{0:T(128)}, u32[]{:S(2)}) copy-start(f32[128]{0:T(128)} %get-tuple-element.19) | copy-start | bytes 1540
  76.2 24.4 %collective-permute-start.9 = (bf16[128,2048]{1,0:T(8,128)(2,1)}, bf16[128,2048]{1,0:T(8,128)(2,1)}, u32[]{:S(2)}, u32[]{:S(2)}) collective-permute-start(bf16[128,2048]{1,0:T(8,128)(2,1)} %collective-permute-done.8), channel_id=1, source_target_pairs={{4,0},{8,4},{12,8},{14,12},{10,14},{6,10},{2,6},{0,2},{5,1},{9,5},... | collective-permute-start | bytes 1572872 | tf_op jit(solution)/shard_map/ppermute | solution.py:121
  79.7 2.7 %copy-start.4 = (bf16[1,2048,384]{2,1,0:T(8,128)(2,1)S(1)}, bf16[1,2048,384]{2,1,0:T(8,128)(2,1)}, u32[]{:S(2)}) copy-start(bf16[1,2048,384]{2,1,0:T(8,128)(2,1)} %param.29) | copy-start | bytes 4718596
  81.8 16.4 %collective-permute-start.12 = (bf16[128,2048]{1,0:T(8,128)(2,1)}, bf16[128,2048]{1,0:T(8,128)(2,1)S(1)}, u32[]{:S(2)}, u32[]{:S(2)}) collective-permute-start(bf16[128,2048]{1,0:T(8,128)(2,1)} %collective-permute-done.11), channel_id=1, source_target_pairs={{0,4},{4,8},{8,12},{12,14},{14,10},{10,6},{6,2},{2,0},{1,5},{5,9},... | collective-permute-start | bytes 1572872 | tf_op jit(solution)/shard_map/ppermute | solution.py:120
  91.4 2.7 %copy-start.32 = (f32[128]{0:T(128)S(1)}, f32[128]{0:T(128)}, u32[]{:S(2)}) copy-start(f32[128]{0:T(128)} %get-tuple-element.17) | copy-start | bytes 1540
  98.9 23.6 %collective-permute-start.13 = (bf16[64,2048]{1,0:T(8,128)(2,1)}, bf16[64,2048]{1,0:T(8,128)(2,1)}, u32[]{:S(2)}, u32[]{:S(2)}) collective-permute-start(bf16[64,2048]{1,0:T(8,128)(2,1)} %slice.43), channel_id=1, source_target_pairs={{0,4},{4,8},{8,12},{12,14},{14,10},{10,6},{6,2},{2,0},{1,5},{5,9},... | collective-permute-start | bytes 786440 | tf_op jit(solution)/shard_map/ppermute | solution.py:127
  102.2 21.3 %collective-permute-start.14 = (bf16[64,2048]{1,0:T(8,128)(2,1)}, bf16[64,2048]{1,0:T(8,128)(2,1)}, u32[]{:S(2)}, u32[]{:S(2)}) collective-permute-start(bf16[64,2048]{1,0:T(8,128)(2,1)} %slice.44), channel_id=1, source_target_pairs={{4,0},{8,4},{12,8},{14,12},{10,14},{6,10},{2,6},{0,2},{5,1},{9,5},... | collective-permute-start | bytes 786440 | tf_op jit(solution)/shard_map/ppermute | solution.py:128
  105.3 2.1 %copy-start.5 = (bf16[1,2048,384]{2,1,0:T(8,128)(2,1)S(1)}, bf16[1,2048,384]{2,1,0:T(8,128)(2,1)}, u32[]{:S(2)}) copy-start(bf16[1,2048,384]{2,1,0:T(8,128)(2,1)} %param.29) | copy-start | bytes 4718596
  118.8 5.7 %copy-start.6 = (bf16[1,2048,384]{2,1,0:T(8,128)(2,1)S(1)}, bf16[1,2048,384]{2,1,0:T(8,128)(2,1)}, u32[]{:S(2)}) copy-start(bf16[1,2048,384]{2,1,0:T(8,128)(2,1)} %param.29) | copy-start | bytes 4718596
  122.5 3.1 %copy-start.31 = (f32[128]{0:T(128)S(1)}, f32[128]{0:T(128)}, u32[]{:S(2)}) copy-start(f32[128]{0:T(128)} %get-tuple-element.15) | copy-start | bytes 1540
  124.5 1.1 copy-start.7
  129.0 2.8 %copy-start.8 = (bf16[128,2048]{1,0:T(8,128)(2,1)S(1)}, bf16[128,2048]{1,0:T(8,128)(2,1)}, u32[]{:S(2)}) copy-start(bf16[128,2048]{1,0:T(8,128)(2,1)} %copy-done.7) | copy-start | bytes 1572868
  129.0 2.8 %copy-start.16 = (f32[128,2048]{1,0:T(8,128)S(1)}, f32[128,2048]{1,0:T(8,128)}, u32[]{:S(2)}) copy-start(f32[128,2048]{1,0:T(8,128)} %fusion.26) | copy-start | bytes 3145732
  129.0 2.8 %copy-start.30 = (f32[128]{0:T(128)S(1)}, f32[128]{0:T(128)}, u32[]{:S(2)}) copy-start(f32[128]{0:T(128)} %get-tuple-element.14) | copy-start | bytes 1540
  135.5 3.5 %copy-start.15 = (f32[128,2048]{1,0:T(8,128)S(1)}, f32[128,2048]{1,0:T(8,128)}, u32[]{:S(2)}) copy-start(f32[128,2048]{1,0:T(8,128)} %fusion.29) | copy-start | bytes 3145732
  137.3 7.1 %collective-permute-start.15 = (bf16[64,2048]{1,0:T(8,128)(2,1)S(1)}, bf16[64,2048]{1,0:T(8,128)(2,1)}, u32[]{:S(2)}, u32[]{:S(2)}) collective-permute-start(bf16[64,2048]{1,0:T(8,128)(2,1)S(1)} %get-tuple-element.5), channel_id=1, source_target_pairs={{0,4},{4,8},{8,12},{12,14},{14,10},{10,6},{6,2},{2,0},{1,5},{5,9},... | collective-permute-start | bytes 786440 | tf_op jit(solution)/shard_map/ppermute | solution.py:133
  142.8 8.5 %copy-start.19 = (f32[128,2048]{1,0:T(8,128)S(1)}, f32[128,2048]{1,0:T(8,128)}, u32[]{:S(2)}) copy-start(f32[128,2048]{1,0:T(8,128)} %convolution_add_fusion) | copy-start | bytes 3145732
  143.9 7.4 %collective-permute-start.19 = (bf16[64,2048]{1,0:T(8,128)(2,1)}, bf16[64,2048]{1,0:T(8,128)(2,1)S(1)}, u32[]{:S(2)}, u32[]{:S(2)}) collective-permute-start(bf16[64,2048]{1,0:T(8,128)(2,1)} %get-tuple-element.6), channel_id=1, source_target_pairs={{4,0},{8,4},{12,8},{14,12},{10,14},{6,10},{2,6},{0,2},{5,1},{9,5},... | collective-permute-start | bytes 786440 | tf_op jit(solution)/shard_map/ppermute | solution.py:134
  145.6 6.3 %copy-start.14 = (f32[128,2048]{1,0:T(8,128)S(1)}, f32[128,2048]{1,0:T(8,128)}, u32[]{:S(2)}) copy-start(f32[128,2048]{1,0:T(8,128)} %fusion.28) | copy-start | bytes 3145732
  145.6 6.3 %copy-start.21 = (f32[128,384]{1,0:T(8,128)S(1)}, f32[128,384]{1,0:T(8,128)}, u32[]{:S(2)}) copy-start(f32[128,384]{1,0:T(8,128)} %fusion.192) | copy-start | bytes 589828
  146.4 11.5 %collective-permute-start.16 = (bf16[128,2048]{1,0:T(8,128)(2,1)}, bf16[128,2048]{1,0:T(8,128)(2,1)}, u32[]{:S(2)}, u32[]{:S(2)}) collective-permute-start(bf16[128,2048]{1,0:T(8,128)(2,1)} %pad_maximum_fusion), channel_id=1, source_target_pairs={{0,4},{4,8},{8,12},{12,14},{14,10},{10,6},{6,2},{2,0},{1,5},{5,9},... | collective-permute-start | bytes 1572872 | tf_op jit(solution)/shard_map/ppermute | solution.py:144
  151.4 10.5 %collective-permute-start.20 = (bf16[128,2048]{1,0:T(8,128)(2,1)S(1)}, bf16[128,2048]{1,0:T(8,128)(2,1)}, u32[]{:S(2)}, u32[]{:S(2)}) collective-permute-start(bf16[128,2048]{1,0:T(8,128)(2,1)S(1)} %pad_maximum_fusion.1), channel_id=1, source_target_pairs={{4,0},{8,4},{12,8},{14,12},{10,14},{6,10},{2,6},{0,2},{5,1},{9,5},... | collective-permute-start | bytes 1572872 | tf_op jit(solution)/shard_map/ppermute | solution.py:145
  155.8 6.1 %copy-start.17 = (f32[128,2048]{1,0:T(8,128)S(1)}, f32[128,2048]{1,0:T(8,128)}, u32[]{:S(2)}) copy-start(f32[128,2048]{1,0:T(8,128)} %convolution_add_fusion.1) | copy-start | bytes 3145732
  160.3 4.0 %copy-start.12 = (bf16[128,2048]{1,0:T(8,128)(2,1)S(1)}, bf16[128,2048]{1,0:T(8,128)(2,1)}, u32[]{:S(2)}) copy-start(bf16[128,2048]{1,0:T(8,128)(2,1)} %copy-done.11) | copy-start | bytes 1572868
  160.3 4.0 %copy-start.13 = (f32[128,2048]{1,0:T(8,128)S(1)}, f32[128,2048]{1,0:T(8,128)}, u32[]{:S(2)}) copy-start(f32[128,2048]{1,0:T(8,128)} %fusion.27) | copy-start | bytes 3145732
  160.3 4.0 %copy-start.20 = (f32[128,384]{1,0:T(8,128)S(1)}, f32[128,384]{1,0:T(8,128)}, u32[]{:S(2)}) copy-start(f32[128,384]{1,0:T(8,128)} %fusion.191) | copy-start | bytes 589828
  160.3 10.7 %collective-permute-start.17 = (bf16[128,2048]{1,0:T(8,128)(2,1)}, bf16[128,2048]{1,0:T(8,128)(2,1)}, u32[]{:S(2)}, u32[]{:S(2)}) collective-permute-start(bf16[128,2048]{1,0:T(8,128)(2,1)} %add_convert_fusion.4), channel_id=1, source_target_pairs={{0,4},{4,8},{8,12},{12,14},{14,10},{10,6},{6,2},{2,0},{1,5},{5,9},... | collective-permute-start | bytes 1572872 | tf_op jit(solution)/shard_map/ppermute | solution.py:144
  163.9 11.0 %collective-permute-start.21 = (bf16[128,2048]{1,0:T(8,128)(2,1)}, bf16[128,2048]{1,0:T(8,128)(2,1)}, u32[]{:S(2)}, u32[]{:S(2)}) collective-permute-start(bf16[128,2048]{1,0:T(8,128)(2,1)} %add_convert_fusion.2), channel_id=1, source_target_pairs={{4,0},{8,4},{12,8},{14,12},{10,14},{6,10},{2,6},{0,2},{5,1},{9,5},... | collective-permute-start | bytes 1572872 | tf_op jit(solution)/shard_map/ppermute | solution.py:145
  168.1 6.8 %copy-start.18 = (f32[128,2048]{1,0:T(8,128)S(1)}, f32[128,2048]{1,0:T(8,128)}, u32[]{:S(2)}) copy-start(f32[128,2048]{1,0:T(8,128)} %convolution_add_fusion.2) | copy-start | bytes 3145732
  173.3 9.9 %collective-permute-start.18 = (bf16[128,2048]{1,0:T(8,128)(2,1)}, bf16[128,2048]{1,0:T(8,128)(2,1)S(1)}, u32[]{:S(2)}, u32[]{:S(2)}) collective-permute-start(bf16[128,2048]{1,0:T(8,128)(2,1)} %add_convert_fusion.3), channel_id=1, source_target_pairs={{0,4},{4,8},{8,12},{12,14},{14,10},{10,6},{6,2},{2,0},{1,5},{5,9},... | collective-permute-start | bytes 1572872 | tf_op jit(solution)/shard_map/ppermute | solution.py:144
  176.8 9.5 %collective-permute-start.22 = (bf16[128,2048]{1,0:T(8,128)(2,1)}, bf16[128,2048]{1,0:T(8,128)(2,1)}, u32[]{:S(2)}, u32[]{:S(2)}) collective-permute-start(bf16[128,2048]{1,0:T(8,128)(2,1)} %add_convert_fusion.1), channel_id=1, source_target_pairs={{4,0},{8,4},{12,8},{14,12},{10,14},{6,10},{2,6},{0,2},{5,1},{9,5},... | collective-permute-start | bytes 1572872 | tf_op jit(solution)/shard_map/ppermute | solution.py:145
  179.1 7.2 %copy-start.10 = (f32[128,2048]{1,0:T(8,128)S(1)}, f32[128,2048]{1,0:T(8,128)}, u32[]{:S(2)}) copy-start(f32[128,2048]{1,0:T(8,128)} %copy-done.9) | copy-start | bytes 3145732

commit v2 on v0

--- a/solution.py
+++ b/solution.py
@@ -1,17 +1,321 @@
+import functools
 import math
 
 import jax
 import jax.numpy as jnp
 from jax import lax
+from jax.experimental import pallas as pl
+from jax.experimental.pallas import tpu as pltpu
 from jax.sharding import PartitionSpec as P
 
+
 HD = 128
-
+CHUNKS = 2
+SMALL = pltpu.CompilerParams(vmem_limit_bytes=6 << 20)
+VMEM = pl.BlockSpec(memory_space=pltpu.VMEM)
+SMEM = pl.BlockSpec(memory_space=pltpu.SMEM)
 
 negative_fill = -1e30
 
 
-def per_device(
+def ring_order(count):
+    return list(range(0, count, 2)) + list(range(count - 1, 0, -2))
+
+
+def place_of(chip, count):
+    return jnp.where((chip & 1) == 0, chip >> 1, count - 1 - (chip >> 1))
+
+
+def chip_at(place, count):
+    return jnp.where(place < count // 2, 2 * place, 2 * (count - 1 - place) + 1)
+
+
+def in_hbm(x):
+    return pltpu.with_memory_space_constraint(x, pltpu.HBM)
+
+
+def in_vmem(x):
+    return pltpu.with_memory_space_constraint(x, pltpu.VMEM)
+
+
+def attend_kernel(
+    first_row,
+    core,
+    span_req,
+    cache_len,
+    q_ref,
+    nk_ref,
+    nv_ref,
+    ck_ref,
+    cv_ref,
+    w_hbm,
+    far_ref,
+    near_ref,
+    w_ref,
+    w_sem,
+):
+    step = pl.program_id(0)
+    spans = pl.num_programs(0)
+    fetch = pltpu.make_async_copy(w_hbm, w_ref, w_sem)
+
+    @pl.when(step == 0)
+    def _():
+        fetch.start()
+
+    rows = q_ref.shape[0]
+    heads = q_ref.shape[1] // HD
+    length = nk_ref.shape[0]
+    to_exp2 = math.log2(math.e) / math.sqrt(HD)
+    span = lax.rem(core[0] + step + 1, spans)
+    held = cache_len[lax.rem(span_req[span], spans)]
+    q = jnp.concatenate([q_ref[:, h * HD : (h + 1) * HD] for h in range(heads)], axis=0)
+    dims = (((1,), (1,)), ((), ()))
+    old = lax.dot_general(q, ck_ref[0], dims, preferred_element_type=jnp.float32)
+    new = lax.dot_general(q, nk_ref[...], dims, preferred_element_type=jnp.float32)
+    key_at = lax.broadcasted_iota(jnp.int32, (1, old.shape[1]), 1)
+    old = jnp.where(key_at < held, old, negative_fill)
+    own_at = lax.broadcasted_iota(jnp.int32, (rows, length), 1)
+    own_row = first_row + lax.broadcasted_iota(jnp.int32, (rows, length), 0)
+    fill = jnp.where(own_at <= own_row, 0.0, negative_fill)
+    new = new + jnp.concatenate([fill] * heads, axis=0)
+    top = jnp.maximum(
+        jnp.max(old, axis=1, keepdims=True), jnp.max(new, axis=1, keepdims=True)
+    )
+    old = jnp.exp2((old - top) * to_exp2)
+    new = jnp.exp2((new - top) * to_exp2)
+    total = jnp.sum(old, axis=1, keepdims=True) + jnp.sum(new, axis=1, keepdims=True)
+    out = jnp.dot(old.astype(jnp.bfloat16), cv_ref[0], preferred_element_type=jnp.float32)
+    out += jnp.dot(new.astype(jnp.bfloat16), nv_ref[...], preferred_element_type=jnp.float32)
+    out = (out / total).astype(jnp.bfloat16)
+    out = jnp.concatenate([out[h * rows : (h + 1) * rows] for h in range(heads)], axis=1)
+
+    @pl.when(step == 0)
+    def _():
+        fetch.wait()
+
+    out = jnp.dot(out, w_ref[...], preferred_element_type=jnp.float32)
+
+    @pl.when(step == 0)
+    def _():
+        far_ref[...] = out
+
+    @pl.when(step == spans - 1)
+    def _():
+        near_ref[...] = out
+
+
+def attend_chunk(
+    chunk,
+    core,
+    span_req,
+    cache_len,
+    queries,
+    new_keys,
+    new_values,
+    cache_keys,
+    cache_values,
+    out_proj,
+):
+    spans, cache_size, _ = cache_keys.shape
+    length = queries.shape[0] // spans
+    rows = length // CHUNKS
+    width = out_proj.shape[1]
+    shape = pltpu.VMEM((rows, width), jnp.float32)
+    macs = spans * rows * (queries.shape[1] * (2 * (cache_size + length) + width))
+
+    def span_at(i, core):
+        return lax.rem(core[0] + i + 1, spans)
+
+    def request_at(i, core, span_req):
+        return lax.rem(span_req[span_at(i, core)], spans)
+
+    new_spec = pl.BlockSpec((length, HD), lambda i, c, r, n: (span_at(i, c), 0))
+    old_spec = pl.BlockSpec((1, cache_size, HD), lambda i, c, r, n: (request_at(i, c, r), 0, 0))
+    out_spec = pl.BlockSpec((rows, width), lambda i, c, r, n: (0, 0))
+    return pl.pallas_call(
+        functools.partial(attend_kernel, chunk * rows),
+        out_shape=(shape, shape),
+        grid_spec=pltpu.PrefetchScalarGridSpec(
+            num_scalar_prefetch=3,
+            grid=(spans,),
+            in_specs=[
+                pl.BlockSpec(
+                    (rows, queries.shape[1]),
+                    lambda i, c, r, n: (span_at(i, c) * CHUNKS + chunk, 0),
+                ),
+                new_spec,
+                new_spec,
+                old_spec,
+                old_spec,
+                pl.BlockSpec(memory_space=pltpu.HBM),
+            ],
+            out_specs=[out_spec, out_spec],
+            scratch_shapes=[
+                pltpu.VMEM(out_proj.shape, out_proj.dtype),
+                pltpu.SemaphoreType.DMA,
+            ],
+        ),
+        cost_estimate=pl.CostEstimate(
+            flops=2 * macs, transcendentals=0, bytes_accessed=out_proj.size * 2
+        ),
+        compiler_params=pltpu.CompilerParams(vmem_limit_bytes=20 << 20),
+        name="attend",
+    )(
+        core,
+        span_req,
+        cache_len,
+        *map(in_hbm, (queries, new_keys, new_values, cache_keys, cache_values, out_proj)),
+    )
+
+
+def norm_kernel(near_ref, far_ref, resid_ref, gain_ref, hidden_ref, normed_ref):
+    state = resid_ref[...].astype(jnp.float32) + (near_ref[...] + far_ref[...])
+    state = state.astype(jnp.bfloat16)
+    hidden_ref[...] = state
+    state = state.astype(jnp.float32)
+    mean_square = jnp.mean(state * state, axis=-1, keepdims=True)
+    normed_ref[...] = (state * lax.rsqrt(mean_square + 1e-06) * gain_ref[...]).astype(jnp.bfloat16)
+
+
+def norm_chunk(chunk, near, far, resid, gain):
+    rows, width = near.shape
+    whole = pl.BlockSpec((rows, width), lambda i: (0, 0))
+    return pl.pallas_call(
+        norm_kernel,
+        grid=(1,),
+        out_shape=(pltpu.VMEM((rows, width), jnp.bfloat16),) * 2,
+        in_specs=[
+            whole,
+            whole,
+            pl.BlockSpec((rows, width), lambda i: (chunk, 0)),
+            pl.BlockSpec((1, width), lambda i: (0, 0)),
+        ],
+        out_specs=(whole, whole),
+        compiler_params=SMALL,
+        name="norm",
+    )(in_vmem(near), in_vmem(far), in_hbm(resid), gain.reshape(1, width))
+
+
+def experts_kernel(n_expert, firsts, offsets, ids, *refs):
+    count = len(firsts)
+    e, c = ids[0], ids[1]
+    at = place_of(e, n_expert)
+    local = (2 * e + c, 2 * e + 1 - c)
+    blocks, (tables_ref, g0, u0, d0, g1, u1, d1), outs = (
+        refs[:count],
+        refs[count : count + 7],
+        refs[count + 7 :],
+    )
+    rows = blocks[0].shape[0]
+    x = jnp.concatenate([b[...] for b in blocks], axis=0) if count > 1 else blocks[0][...]
+    turned = [
+        jnp.transpose(tables_ref[chip_at(lax.rem(at + o + n_expert, n_expert), n_expert) ^ e])
+        for o in offsets
+    ]
+    name_at = lax.broadcasted_iota(jnp.int32, turned[0].shape, 1)
+    total = None
+    for j, (g, u, d) in enumerate(((g0, u0, d0), (g1, u1, d1))):
+        scale = jnp.concatenate(
+            [
+                jnp.sum(jnp.where(name_at == local[j], t, 0.0), axis=1, keepdims=True)[f : f + rows]
+                for t, f in zip(turned, firsts)
+            ],
+            axis=0,
+        )
+        gate_part = jnp.dot(x, g[...], preferred_element_type=jnp.float32)
+        up_part = jnp.dot(x, u[...], preferred_element_type=jnp.float32)
+        act = gate_part / (1.0 + jnp.exp(-gate_part)) * up_part * scale
+        part = jnp.dot(act.astype(jnp.bfloat16), d[...], preferred_element_type=jnp.float32)
+        total = part if total is None else total + part
+    for i, out in enumerate(outs):
+        out[...] = total[i * rows : (i + 1) * rows].astype(out.dtype)
+
+
+def run_experts(n_expert, ids, blocks, firsts, offsets, kinds, tables, mine, other):
+    rows, width = blocks[0].shape
+    weights = (*mine, *other)
+    outs = tuple(pltpu.VMEM((rows, width), kind) for kind in kinds)
+    flops = 2 * rows * len(blocks) * sum(w.size for w in weights)
+    return pl.pallas_call(
+        functools.partial(experts_kernel, n_expert, firsts, offsets),
+        out_shape=outs,
+        in_specs=[SMEM]
+        + [VMEM] * (len(blocks) + 1 + len(weights)),
+        out_specs=tuple(VMEM for _ in blocks),
+        cost_estimate=pl.CostEstimate(
+            flops=flops, transcendentals=0, bytes_accessed=sum(w.size for w in weights) * 2
+        ),
+        compiler_params=pltpu.CompilerParams(vmem_limit_bytes=12 << 20),
+        name="experts",
+    )(ids, *map(in_vmem, blocks), in_vmem(tables), *map(in_vmem, weights))
+
+
+def add_kernel(count, *refs):
+    for part, got, out in zip(refs[:count], refs[count : 2 * count], refs[2 * count :]):
+        out[...] = (part[...] + got[...].astype(jnp.float32)).astype(out.dtype)
+
+
+def add_parts(parts, arrived):
+    count = len(parts)
+    return pl.pallas_call(
+        functools.partial(add_kernel, count),
+        out_shape=tuple(pltpu.VMEM(x.shape, x.dtype) for x in arrived),
+        in_specs=[VMEM] * (2 * count),
+        out_specs=(VMEM,) * count,
+        compiler_params=SMALL,
+        name="add",
+    )(*map(in_vmem, (*parts, *arrived)))
+
+
+def final_kernel(count, *refs):
+    out_ref = refs[-1]
+    rows = refs[0].shape[0]
+    for k in range(count):
+        hidden, home, ahead, behind = (refs[i * count + k][...] for i in range(4))
+        mixed = home + ahead.astype(jnp.float32) + behind.astype(jnp.float32)
+        out_ref[k * rows : (k + 1) * rows] = (hidden.astype(jnp.float32) + mixed).astype(
+            out_ref.dtype
+        )
+
+
+def finish(hidden, home, ahead, behind):
+    count = len(hidden)
+    rows, width = hidden[0].shape
+    return pl.pallas_call(
+        functools.partial(final_kernel, count),
+        out_shape=jax.ShapeDtypeStruct((count * rows, width), jnp.bfloat16),
+        in_specs=[VMEM] * (4 * count),
+        out_specs=VMEM,
+        compiler_params=SMALL,
+        name="finish",
+    )(*map(in_vmem, (*hidden, *home, *ahead, *behind)))
+
+
+def weigh_kernel(routes_ref, gates_ref, out_ref):
+    gates = gates_ref[...]
+    weight = gates / jnp.sum(gates, axis=0, keepdims=True)
+    routes = routes_ref[...]
+    out_ref[0] = jnp.concatenate(
+        [
+            jnp.sum(jnp.where(routes == j, weight, 0.0), axis=0, keepdims=True)
+            for j in range(out_ref.shape[1])
+        ],
+        axis=0,
+    )
+
+
+def weigh(routes, gates, experts):
+    return pl.pallas_call(
+        weigh_kernel,
+        out_shape=pltpu.VMEM((1, experts, routes.shape[0]), jnp.float32),
+        in_specs=[VMEM] * 2,
+        out_specs=VMEM,
+        compiler_params=SMALL,
+        name="weigh",
+    )(routes.T, gates.T)
+
+
+def dense_layer(
     queries,
     new_keys,
     new_values,
@@ -28,16 +332,100 @@
     w_up,
     w_down,
 ):
-    n_attn = lax.axis_size("attn")
     n_expert = lax.axis_size("expert")
+    experts = n_expert * lax.axis_size("attn")
+    e = lax.axis_index("expert")
+    c = lax.axis_index("attn")
+    own_rows = resid.shape[0]
+    rows = own_rows // CHUNKS
+    swap = [(0, 1), (1, 0)]
+    order = ring_order(n_expert)
+    steps = {}
+    steps[1] = [(order[i], order[(i + 1) % n_expert]) for i in range(n_expert)]
+    steps[-1] = [(b, a) for a, b in steps[1]]
+    reach = n_expert // 2
+
+    mine = (w_gate[0], w_up[0], w_down[0])
+    other = tuple(lax.ppermute(w, "attn", swap) for w in mine)
+
+    tables = weigh(routes, gates, experts)
+    for bit in range(n_expert.bit_length() - 1):
+        pairs = [(i, i ^ (1 << bit)) for i in range(n_expert)]
+        tables = jnp.concatenate([tables, lax.ppermute(tables, "expert", pairs)], axis=0)
+
+    core = c.reshape(1)
+    ids = jnp.stack([e, c])
+    near, far = [], []
+    for k in range(CHUNKS):
+        theirs, ours = attend_chunk(
+            k,
+            core,
+            span_req,
+            cache_len,
+            queries,
+            new_keys,
+            new_values,
+            cache_keys,
+            cache_values,
+            out_proj,
+        )
+        near.append(ours)
+        far.append(lax.ppermute(theirs, "attn", swap))
+    hidden, normed = [], []
+    for k in range(CHUNKS):
+        h, x = norm_chunk(k, near[k], far[k], resid, norm_gain)
+        hidden.append(h)
+        normed.append(x)
+
+    def compute(blocks, firsts, offsets, kinds):
+        return run_experts(
+            n_expert, ids, blocks, firsts, offsets, kinds, tables, mine, other
+        )
+
+    wide, sent = jnp.float32, jnp.bfloat16
+    longer = [1 if k % 2 == 0 else -1 for k in range(CHUNKS)]
+    shorter = [-way for way in longer]
+    parts = [{} for _ in range(CHUNKS)]
+    moving = [{1: x, -1: x} for x in normed]
+    home = compute(normed, [k * rows for k in range(CHUNKS)], [0] * CHUNKS, [wide] * CHUNKS)
+    for s in range(1, reach):
+        for k in range(CHUNKS):
+            for way in (1, -1):
+                moving[k][way] = lax.ppermute(moving[k][way], "expert", steps[way])
+            got = compute(
+                [moving[k][way] for way in (1, -1)],
+                [k * rows] * 2,
+                [-s, s],
+                [sent if o == shorter[k] * (reach - 1) else wide for o in (-s, s)],
+            )
+            parts[k][-s], parts[k][s] = got
+    last = []
+    for k in range(CHUNKS):
+        last.append(lax.ppermute(moving[k][longer[k]], "expert", steps[longer[k]]))
+    got = compute(last, [k * rows for k in range(CHUNKS)], [reach] * CHUNKS, [sent] * CHUNKS)
+
+    def send(blocks, ways):
+        return [lax.ppermute(x, "expert", steps[way]) for x, way in zip(blocks, ways)]
+
+    early = [(parts[k][shorter[k] * (reach - 1)]) for k in range(CHUNKS)]
+    early = send(early, shorter)
+    late = send(got, longer)
+    for s in range(reach - 1, 0, -1):
+        late = add_parts([parts[k][longer[k] * s] for k in range(CHUNKS)], late)
+        late = send(late, longer)
+        if s > 1:
+            early = add_parts([parts[k][shorter[k] * (s - 1)] for k in range(CHUNKS)], early)
+            early = send(early, shorter)
+    return finish(hidden, home, early, late)
+
+
+def attend(queries, new_keys, new_values, cache_keys, cache_values, cache_len, span_req):
     spans = cache_keys.shape[0]
     cache_size = cache_keys.shape[1]
     length = queries.shape[0] // spans
     kv_local = cache_keys.shape[2] // HD
     head_count = queries.shape[1] // HD
     group_size = head_count // kv_local
-    model_width = resid.shape[1]
-    own_rows = resid.shape[0]
     local_req = span_req % spans
     lengths = cache_len[local_req]
     queries_split = queries.reshape(spans, length, kv_local, group_size, HD)
@@ -60,20 +448,12 @@
     attended = jnp.einsum(
         "cgqlk,ckgd->clgqd", weights, all_values, preferred_element_type=jnp.float32
     )
-    attended = attended.astype(jnp.bfloat16).reshape(spans * length, head_count * HD)
-    attn_out = lax.psum_scatter(
-        jnp.dot(attended, out_proj, preferred_element_type=jnp.float32),
-        "attn",
-        scatter_dimension=0,
-        tiled=True,
-    )
-    hidden = (resid.astype(jnp.float32) + attn_out).astype(jnp.bfloat16)
-    state_float = hidden.astype(jnp.float32)
-    mean_square = jnp.mean(state_float * state_float, axis=-1, keepdims=True)
-    normed = (state_float * lax.rsqrt(mean_square + 1e-06) * norm_gain).astype(jnp.bfloat16)
+    return attended.astype(jnp.bfloat16).reshape(spans * length, head_count * HD)
+
+
+def routed_mix(normed, routes, gates, w_gate, w_up, w_down, capacity, experts):
+    own_rows, model_width = normed.shape
     top_count = routes.shape[1]
-    experts = n_expert * n_attn
-    capacity = 2 * top_count * own_rows // experts
     flat_routes = routes.reshape(-1)
     one_hot = (flat_routes[:, None] == jnp.arange(experts, dtype=jnp.int32)[None, :]).astype(
         jnp.int32
@@ -99,10 +479,56 @@
     returned = lax.all_to_all(computed, ("expert", "attn"), split_axis=0, concat_axis=0, tiled=True)
     picked = returned.reshape(experts * capacity, model_width)[slot_target].astype(jnp.float32)
     weight = gates / jnp.sum(gates, axis=-1, keepdims=True)
-    mixed = jnp.sum(
+    return jnp.sum(
         (picked * weight.reshape(-1, 1)).reshape(own_rows, top_count, model_width), axis=1
     )
+
+
+def routed_layer(
+    queries,
+    new_keys,
+    new_values,
+    cache_keys,
+    cache_values,
+    cache_len,
+    span_req,
+    out_proj,
+    resid,
+    norm_gain,
+    routes,
+    gates,
+    w_gate,
+    w_up,
+    w_down,
+):
+    experts = lax.axis_size("expert") * lax.axis_size("attn")
+    capacity = 2 * routes.shape[1] * resid.shape[0] // experts
+    attended = attend(
+        queries, new_keys, new_values, cache_keys, cache_values, cache_len, span_req
+    )
+    attn_out = lax.psum_scatter(
+        jnp.dot(attended, out_proj, preferred_element_type=jnp.float32),
+        "attn",
+        scatter_dimension=0,
+        tiled=True,
+    )
+    hidden = (resid.astype(jnp.float32) + attn_out).astype(jnp.bfloat16)
+    state_float = hidden.astype(jnp.float32)
+    mean_square = jnp.mean(state_float * state_float, axis=-1, keepdims=True)
+    normed = (state_float * lax.rsqrt(mean_square + 1e-06) * norm_gain).astype(jnp.bfloat16)
+    mixed = routed_mix(normed, routes, gates, w_gate, w_up, w_down, capacity, experts)
     return (state_float + mixed).astype(jnp.bfloat16)
+
+
+def per_device(*args):
+    cache_keys, routes = args[3], args[10]
+    n_expert, n_attn = lax.axis_size("expert"), lax.axis_size("attn")
+    everywhere = 2 * routes.shape[1] >= n_expert * n_attn
+    fits = n_attn == 2 and n_expert > 2 and n_expert & (n_expert - 1) == 0
+    fits = fits and cache_keys.shape[0] == 2 and cache_keys.shape[2] == HD
+    if everywhere and fits:
+        return dense_layer(*args)
+    return routed_layer(*args)
 
 
 def solution(mesh):

time: 472 us -> 133 us (0.28)
  the two profiles are of different devices: /device:TPU:13 before, /device:TPU:0 now
where the time goes in v2:
time: 133 us
  Pallas kernels  57.6 us (43%)
  starting transfers between devices  38.5 us (29%)
  waiting for transfers between devices  29.1 us (22%)
  local copies, waits for them, and re-layouts  7.1 us (5%)
    pallas_call x8, Pallas kernels, run_experts(): pl.pallas_call(functools.partial(experts_kernel, n_expert, firsts, offset...  38.3 us
    ppermute x12, waiting for transfers between devices, dense_layer(): moving[k][way] = lax.ppermute(moving[k][way], 'expert', steps[way])  17 us
    pallas_call x2, Pallas kernels, attend_chunk(): pl.pallas_call(functools.partial(attend_kernel, chunk * rows), out_shape=...  15.2 us
    ppermute x14, starting transfers between devices, send(): lax.ppermute(x, 'expert', steps[way])  14.8 us
    ppermute x12, starting transfers between devices, dense_layer(): moving[k][way] = lax.ppermute(moving[k][way], 'expert', steps[way])  13.4 us
    unnamed x60, local copies, waits for them, and re-layouts  7.1 us
    ppermute x3, starting transfers between devices, dense_layer(): lax.ppermute(tables, 'expert', pairs)  7.09 us
    ppermute x2, waiting for transfers between devices, dense_layer(): last.append(lax.ppermute(moving[k][longer[k]], 'expert', steps[longer[k]]))  6.32 us
  transfers between devices with their start and end apart: 36, of which 10 were waited for; matrix products, arithmetic and copies ran while one was open for 0% of the time, Pallas kernels for 37%

profile of v2, /device:TPU:0, one launch (start us, length us, event | category | flops | bytes accessed | tf_op | source)
XLA Modules:
  0.0 132.8 jit_solution(2532313555754500923)
XLA Ops:
  0.0 0.7 copy-done.27
  0.7 0.7 copy-done.29
  1.3 7.8 %attend.3 = (f32[64,2048]{1,0:T(8,128)S(1)}, f32[64,2048]{1,0:T(8,128)S(1)}) custom-call(s32[1]{0:T(128)} %bitcast.core, s32[2]{0:T(128)S(1)} %copy-done.27, s32[2]{0:T(128)S(1)} %copy-done.29, bf16[256,1024]{1,0:T(8,128)(2,1)} %q_ref.3, bf16[256,128]{1,0:T(8,128)(2,1)} %nk_ref.3, bf16[256,128]{1,0:T(8,128)(2,1)} %nv_ref.3, bf16[2,1024,128]{2,1,0:T(8,128)(2,1)} %ck_ref.3, ...), custom_call_target="tpu_custom_call" | custom-call | flops 1140850688 | bytes 4194304 | tf_op jit(solution)/shard_map/attend/pallas_call | solution.py:135
  9.2 0.6 collective-permute-start.1
  9.7 7.4 %attend.2 = (f32[64,2048]{1,0:T(8,128)S(1)}, f32[64,2048]{1,0:T(8,128)S(1)}) custom-call(s32[1]{0:T(128)} %bitcast.core, s32[2]{0:T(128)S(1)} %copy-done.28, s32[2]{0:T(128)S(1)} %copy-done.29, bf16[256,1024]{1,0:T(8,128)(2,1)} %q_ref.3, bf16[256,128]{1,0:T(8,128)(2,1)} %nk_ref.3, bf16[256,128]{1,0:T(8,128)(2,1)} %nv_ref.3, bf16[2,1024,128]{2,1,0:T(8,128)(2,1)} %ck_ref.3, ...), custom_call_target="tpu_custom_call" | custom-call | flops 1140850688 | bytes 4194304 | tf_op jit(solution)/shard_map/attend/pallas_call | solution.py:135
  17.3 3.0 %collective-permute-start.2 = (f32[1,16,128]{2,1,0:T(8,128)S(1)}, f32[1,16,128]{2,1,0:T(8,128)S(1)}, u32[]{:S(2)}, u32[]{:S(2)}) collective-permute-start(f32[1,16,128]{2,1,0:T(8,128)S(1)} %weigh.1), channel_id=1, source_target_pairs={{0,2},{2,0},{4,6},{6,4},{8,10},{10,8},{12,14},{14,12},{1,3},{3,1},... | collective-permute-start | bytes 24584 | tf_op jit(solution)/shard_map/ppermute | solution.py:354
  20.3 1.6 %collective-permute-done.2 = f32[1,16,128]{2,1,0:T(8,128)S(1)} collective-permute-done((f32[1,16,128]{2,1,0:T(8,128)S(1)}, f32[1,16,128]{2,1,0:T(8,128)S(1)}, u32[]{:S(2)}, u32[]{:S(2)}) %collective-permute-start.2) | collective-permute-done | bytes 8224 | tf_op jit(solution)/shard_map/ppermute | solution.py:354
  21.9 2.1 %collective-permute-start.3 = (f32[2,16,128]{2,1,0:T(8,128)S(1)}, f32[2,16,128]{2,1,0:T(8,128)S(1)}, u32[]{:S(2)}, u32[]{:S(2)}) collective-permute-start(f32[2,16,128]{2,1,0:T(8,128)S(1)} %pad_maximum_fusion.2), channel_id=1, source_target_pairs={{0,4},{2,6},{4,0},{6,2},{8,12},{10,14},{12,8},{14,10},{1,5},{3,7},... | collective-permute-start | bytes 49160 | tf_op jit(solution)/shard_map/ppermute | solution.py:354
  24.0 1.2 norm.3
  25.2 1.6 %collective-permute-start.11 = (bf16[64,2048]{1,0:T(8,128)(2,1)S(1)}, bf16[64,2048]{1,0:T(8,128)(2,1)S(1)}, u32[]{:S(2)}, u32[]{:S(2)}) collective-permute-start(bf16[64,2048]{1,0:T(8,128)(2,1)S(1)} %get-tuple-element.46.refs_1_), channel_id=1, source_target_pairs={{4,0},{8,4},{12,8},{14,12},{10,14},{6,10},{2,6},{0,2},{5,1},{9,5},... | collective-permute-start | bytes 786440 | tf_op jit(solution)/shard_map/ppermute | solution.py:394
  26.8 2.0 %collective-permute-start.4 = (f32[4,16,128]{2,1,0:T(8,128)S(1)}, f32[4,16,128]{2,1,0:T(8,128)S(1)}, u32[]{:S(2)}, u32[]{:S(2)}) collective-permute-start(f32[4,16,128]{2,1,0:T(8,128)S(1)} %pad_maximum_fusion.1), channel_id=1, source_target_pairs={{0,8},{2,10},{4,12},{6,14},{8,0},{10,2},{12,4},{14,6},{1,9},{3,11}... | collective-permute-start | bytes 98312 | tf_op jit(solution)/shard_map/ppermute | solution.py:354
  28.8 1.6 %collective-permute-start.10 = (bf16[64,2048]{1,0:T(8,128)(2,1)S(1)}, bf16[64,2048]{1,0:T(8,128)(2,1)S(1)}, u32[]{:S(2)}, u32[]{:S(2)}) collective-permute-start(bf16[64,2048]{1,0:T(8,128)(2,1)S(1)} %get-tuple-element.46.refs_1_), channel_id=1, source_target_pairs={{0,4},{4,8},{8,12},{12,14},{14,10},{10,6},{6,2},{2,0},{1,5},{5,9},... | collective-permute-start | bytes 786440 | tf_op jit(solution)/shard_map/ppermute | solution.py:394
  30.4 3.6 %collective-permute-done.4 = f32[4,16,128]{2,1,0:T(8,128)S(1)} collective-permute-done((f32[4,16,128]{2,1,0:T(8,128)S(1)}, f32[4,16,128]{2,1,0:T(8,128)S(1)}, u32[]{:S(2)}, u32[]{:S(2)}) %collective-permute-start.4) | collective-permute-done | bytes 32800 | tf_op jit(solution)/shard_map/ppermute | solution.py:354
  34.0 0.5 collective-permute-start.7
  34.5 1.2 norm.2
  35.7 0.7 copy-done.4
  36.5 2.0 %collective-permute-start.8 = (bf16[64,2048]{1,0:T(8,128)(2,1)S(1)}, bf16[64,2048]{1,0:T(8,128)(2,1)S(1)}, u32[]{:S(2)}, u32[]{:S(2)}) collective-permute-start(bf16[64,2048]{1,0:T(8,128)(2,1)S(1)} %get-tuple-element.45.refs_0_), channel_id=1, source_target_pairs={{0,4},{4,8},{8,12},{12,14},{14,10},{10,6},{6,2},{2,0},{1,5},{5,9},... | collective-permute-start | bytes 786440 | tf_op jit(solution)/shard_map/ppermute | solution.py:394
  38.5 0.7 copy-done.6
  39.2 5.5 %collective-permute-done.9.refs_1_ = bf16[64,2048]{1,0:T(8,128)(2,1)S(1)} collective-permute-done((bf16[64,2048]{1,0:T(8,128)(2,1)S(1)}, bf16[64,2048]{1,0:T(8,128)(2,1)S(1)}, u32[]{:S(2)}, u32[]{:S(2)}) %collective-permute-start.9) | collective-permute-done | bytes 262176 | tf_op jit(solution)/shard_map/ppermute | solution.py:394
  45.0 0.7 copy-done.8
  45.7 1.7 %collective-permute-start.14 = (bf16[64,2048]{1,0:T(8,128)(2,1)S(1)}, bf16[64,2048]{1,0:T(8,128)(2,1)S(1)}, u32[]{:S(2)}, u32[]{:S(2)}) collective-permute-start(bf16[64,2048]{1,0:T(8,128)(2,1)S(1)} %collective-permute-done.10.refs_0_), channel_id=1, source_target_pairs={{0,4},{4,8},{8,12},{12,14},{14,10},{10,6},{6,2},{2,0},{1,5},{5,9},... | collective-permute-start | bytes 786440 | tf_op jit(solution)/shard_map/ppermute | solution.py:394
  47.5 0.7 copy-done.10
  48.2 4.0 %collective-permute-done.15.refs_1_ = bf16[64,2048]{1,0:T(8,128)(2,1)S(1)} collective-permute-done((bf16[64,2048]{1,0:T(8,128)(2,1)S(1)}, bf16[64,2048]{1,0:T(8,128)(2,1)S(1)}, u32[]{:S(2)}, u32[]{:S(2)}) %collective-permute-start.15) | collective-permute-done | bytes 262176 | tf_op jit(solution)/shard_map/ppermute | solution.py:394
  52.1 0.6 collective-permute-start.13
  52.7 0.7 copy-done.12
  53.4 1.5 %collective-permute-start.12 = (bf16[64,2048]{1,0:T(8,128)(2,1)S(1)}, bf16[64,2048]{1,0:T(8,128)(2,1)S(1)}, u32[]{:S(2)}, u32[]{:S(2)}) collective-permute-start(bf16[64,2048]{1,0:T(8,128)(2,1)S(1)} %collective-permute-done.8.refs_0_), channel_id=1, source_target_pairs={{0,4},{4,8},{8,12},{12,14},{14,10},{10,6},{6,2},{2,0},{1,5},{5,9},... | collective-permute-start | bytes 786440 | tf_op jit(solution)/shard_map/ppermute | solution.py:394
  54.9 0.7 copy-done.14
  55.6 3.1 %collective-permute-done.13.refs_1_ = bf16[64,2048]{1,0:T(8,128)(2,1)S(1)} collective-permute-done((bf16[64,2048]{1,0:T(8,128)(2,1)S(1)}, bf16[64,2048]{1,0:T(8,128)(2,1)S(1)}, u32[]{:S(2)}, u32[]{:S(2)}) %collective-permute-start.13) | collective-permute-done | bytes 262176 | tf_op jit(solution)/shard_map/ppermute | solution.py:394
  58.7 0.8 collective-permute-start.20
  59.6 0.7 copy-done.16
  60.3 1.2 collective-permute-start.16
  61.5 0.7 copy-done.22
  62.2 3.7 %collective-permute-done.20.refs_1_ = bf16[64,2048]{1,0:T(8,128)(2,1)} collective-permute-done((bf16[64,2048]{1,0:T(8,128)(2,1)S(1)}, bf16[64,2048]{1,0:T(8,128)(2,1)}, u32[]{:S(2)}, u32[]{:S(2)}) %collective-permute-start.20) | collective-permute-done | bytes 262176 | tf_op jit(solution)/shard_map/ppermute | solution.py:394
  65.9 0.6 collective-permute-start.27
  66.5 0.7 collective-permute-done.16.refs_0_
  67.2 1.5 %collective-permute-start.26 = (bf16[64,2048]{1,0:T(8,128)(2,1)}, bf16[64,2048]{1,0:T(8,128)(2,1)}, u32[]{:S(2)}, u32[]{:S(2)}) collective-permute-start(bf16[64,2048]{1,0:T(8,128)(2,1)} %collective-permute-done.16.refs_0_), channel_id=1, source_target_pairs={{0,4},{4,8},{8,12},{12,14},{14,10},{10,6},{6,2},{2,0},{1,5},{5,9},... | collective-permute-start | bytes 786440 | tf_op jit(solution)/shard_map/ppermute | solution.py:404
  68.7 5.6 %collective-permute-done.27.refs_1_ = bf16[64,2048]{1,0:T(8,128)(2,1)} collective-permute-done((bf16[64,2048]{1,0:T(8,128)(2,1)}, bf16[64,2048]{1,0:T(8,128)(2,1)}, u32[]{:S(2)}, u32[]{:S(2)}) %collective-permute-start.27) | collective-permute-done | bytes 262176 | tf_op jit(solution)/shard_map/ppermute | solution.py:404
  74.4 0.4 collective-permute-start.17
  74.8 0.7 collective-permute-done.26.refs_0_
  75.5 1.7 %collective-permute-start.19 = (bf16[64,2048]{1,0:T(8,128)(2,1)}, bf16[64,2048]{1,0:T(8,128)(2,1)S(1)}, u32[]{:S(2)}, u32[]{:S(2)}) collective-permute-start(bf16[64,2048]{1,0:T(8,128)(2,1)} %copy-done.18), channel_id=1, source_target_pairs={{0,4},{4,8},{8,12},{12,14},{14,10},{10,6},{6,2},{2,0},{1,5},{5,9},... | collective-permute-start | bytes 786440 | tf_op jit(solution)/shard_map/ppermute | solution.py:394
  77.2 4.9 %experts.15 = (bf16[64,2048]{1,0:T(8,128)(2,1)S(1)}, bf16[64,2048]{1,0:T(8,128)(2,1)S(1)}) custom-call(s32[2]{0:T(128)S(1)} %pad_add_fusion.ids, bf16[64,2048]{1,0:T(8,128)(2,1)} %collective-permute-done.26.refs_0_, bf16[64,2048]{1,0:T(8,128)(2,1)} %collective-permute-done.27.refs_1_, f32[8,16,128]{2,1,0:T(8,128)S(1)} %pad_maximum_fusion.refs_2_, ...), custom_call_target="tpu_custom_call" | custom-call | flops 1207959552 | bytes 9437184 | tf_op jit(solution)/shard_map/experts/pallas_call | solution.py:239
  82.2 0.5 collective-permute-start.28
  82.7 1.6 %collective-permute-start.29 = (bf16[64,2048]{1,0:T(8,128)(2,1)S(1)}, bf16[64,2048]{1,0:T(8,128)(2,1)S(1)}, u32[]{:S(2)}, u32[]{:S(2)}) collective-permute-start(bf16[64,2048]{1,0:T(8,128)(2,1)S(1)} %get-tuple-element.66), channel_id=1, source_target_pairs={{4,0},{8,4},{12,8},{14,12},{10,14},{6,10},{2,6},{0,2},{5,1},{9,5},... | collective-permute-start | bytes 786440 | tf_op jit(solution)/shard_map/ppermute | solution.py:408
  84.2 4.8 %experts.13 = (bf16[64,2048]{1,0:T(8,128)(2,1)S(1)}, f32[64,2048]{1,0:T(8,128)S(1)}) custom-call(s32[2]{0:T(128)S(1)} %pad_add_fusion.ids, bf16[64,2048]{1,0:T(8,128)(2,1)} %collective-permute-done.16.refs_0_, bf16[64,2048]{1,0:T(8,128)(2,1)S(1)} %collective-permute-done.17.refs_1_, f32[8,16,128]{2,1,0:T(8,128)S(1)} %pad_maximum_fusion.refs_2_, ...), custom_call_target="tpu_custom_call" | custom-call | flops 1207959552 | bytes 9437184 | tf_op jit(solution)/shard_map/experts/pallas_call | solution.py:239
  89.1 0.5 collective-permute-start.18
  89.6 4.8 %experts.14 = (f32[64,2048]{1,0:T(8,128)S(1)}, bf16[64,2048]{1,0:T(8,128)(2,1)S(1)}) custom-call(s32[2]{0:T(128)S(1)} %pad_add_fusion.ids, bf16[64,2048]{1,0:T(8,128)(2,1)S(1)} %collective-permute-done.19.refs_0_, bf16[64,2048]{1,0:T(8,128)(2,1)} %collective-permute-done.20.refs_1_, f32[8,16,128]{2,1,0:T(8,128)S(1)} %pad_maximum_fusion.refs_2_, ...), custom_call_target="tpu_custom_call" | custom-call | flops 1207959552 | bytes 9437184 | tf_op jit(solution)/shard_map/experts/pallas_call | solution.py:239
  94.4 1.8 %collective-permute-start.21 = (bf16[64,2048]{1,0:T(8,128)(2,1)S(1)}, bf16[64,2048]{1,0:T(8,128)(2,1)S(1)}, u32[]{:S(2)}, u32[]{:S(2)}) collective-permute-start(bf16[64,2048]{1,0:T(8,128)(2,1)S(1)} %get-tuple-element.54), channel_id=1, source_target_pairs={{0,4},{4,8},{8,12},{12,14},{14,10},{10,6},{6,2},{2,0},{1,5},{5,9},... | collective-permute-start | bytes 786440 | tf_op jit(solution)/shard_map/ppermute | solution.py:408
  96.4 0.5 collective-permute-start.30
  96.9 1.6 %collective-permute-start.31 = (bf16[64,2048]{1,0:T(8,128)(2,1)S(1)}, bf16[64,2048]{1,0:T(8,128)(2,1)S(1)}, u32[]{:S(2)}, u32[]{:S(2)}) collective-permute-start(bf16[64,2048]{1,0:T(8,128)(2,1)S(1)} %get-tuple-element.68), channel_id=1, source_target_pairs={{4,0},{8,4},{12,8},{14,12},{10,14},{6,10},{2,6},{0,2},{5,1},{9,5},... | collective-permute-start | bytes 786440 | tf_op jit(solution)/shard_map/ppermute | solution.py:408
  98.5 4.7 %experts.12 = (f32[64,2048]{1,0:T(8,128)S(1)}, f32[64,2048]{1,0:T(8,128)S(1)}) custom-call(s32[2]{0:T(128)S(1)} %pad_add_fusion.ids, bf16[64,2048]{1,0:T(8,128)(2,1)S(1)} %copy-done.19, bf16[64,2048]{1,0:T(8,128)(2,1)S(1)} %copy-done.17, f32[8,16,128]{2,1,0:T(8,128)S(1)} %pad_maximum_fusion.refs_2_, bf16[2048,384]{1,0:T(8,128)(2,1)S(1)} %bitcast.12, ...), custom_call_target="tpu_custom_call" | custom-call | flops 1207959552 | bytes 9437184 | tf_op jit(solution)/shard_map/experts/pallas_call | solution.py:239
  103.3 4.8 %experts.11 = (f32[64,2048]{1,0:T(8,128)S(1)}, f32[64,2048]{1,0:T(8,128)S(1)}) custom-call(s32[2]{0:T(128)S(1)} %pad_add_fusion.ids, bf16[64,2048]{1,0:T(8,128)(2,1)S(1)} %copy-done.23, bf16[64,2048]{1,0:T(8,128)(2,1)S(1)} %copy-done.21, f32[8,16,128]{2,1,0:T(8,128)S(1)} %pad_maximum_fusion.refs_2_, bf16[2048,384]{1,0:T(8,128)(2,1)S(1)} %bitcast.13, ...), custom_call_target="tpu_custom_call" | custom-call | flops 1207959552 | bytes 9437184 | tf_op jit(solution)/shard_map/experts/pallas_call | solution.py:239
  108.2 0.3 collective-permute-start.22
  108.5 1.8 %collective-permute-start.23 = (bf16[64,2048]{1,0:T(8,128)(2,1)S(1)}, bf16[64,2048]{1,0:T(8,128)(2,1)S(1)}, u32[]{:S(2)}, u32[]{:S(2)}) collective-permute-start(bf16[64,2048]{1,0:T(8,128)(2,1)S(1)} %get-tuple-element.56), channel_id=1, source_target_pairs={{0,4},{4,8},{8,12},{12,14},{14,10},{10,6},{6,2},{2,0},{1,5},{5,9},... | collective-permute-start | bytes 786440 | tf_op jit(solution)/shard_map/ppermute | solution.py:408
  110.4 0.5 collective-permute-start.32
  111.0 1.6 %collective-permute-start.33 = (bf16[64,2048]{1,0:T(8,128)(2,1)S(1)}, bf16[64,2048]{1,0:T(8,128)(2,1)S(1)}, u32[]{:S(2)}, u32[]{:S(2)}) collective-permute-start(bf16[64,2048]{1,0:T(8,128)(2,1)S(1)} %get-tuple-element.70), channel_id=1, source_target_pairs={{4,0},{8,4},{12,8},{14,12},{10,14},{6,10},{2,6},{0,2},{5,1},{9,5},... | collective-permute-start | bytes 786440 | tf_op jit(solution)/shard_map/ppermute | solution.py:408
  112.5 4.7 %experts.10 = (f32[64,2048]{1,0:T(8,128)S(1)}, f32[64,2048]{1,0:T(8,128)S(1)}) custom-call(s32[2]{0:T(128)S(1)} %pad_add_fusion.ids, bf16[64,2048]{1,0:T(8,128)(2,1)S(1)} %copy-done.11, bf16[64,2048]{1,0:T(8,128)(2,1)S(1)} %copy-done.9, f32[8,16,128]{2,1,0:T(8,128)S(1)} %pad_maximum_fusion.refs_2_, bf16[2048,384]{1,0:T(8,128)(2,1)S(1)} %bitcast.14, ...), custom_call_target="tpu_custom_call" | custom-call | flops 1207959552 | bytes 9437184 | tf_op jit(solution)/shard_map/experts/pallas_call | solution.py:239
  117.3 4.7 %experts.9 = (f32[64,2048]{1,0:T(8,128)S(1)}, f32[64,2048]{1,0:T(8,128)S(1)}) custom-call(s32[2]{0:T(128)S(1)} %pad_add_fusion.ids, bf16[64,2048]{1,0:T(8,128)(2,1)S(1)} %copy-done.15, bf16[64,2048]{1,0:T(8,128)(2,1)S(1)} %copy-done.13, f32[8,16,128]{2,1,0:T(8,128)S(1)} %pad_maximum_fusion.refs_2_, bf16[2048,384]{1,0:T(8,128)(2,1)S(1)} %bitcast.15, ...), custom_call_target="tpu_custom_call" | custom-call | flops 1207959552 | bytes 9437184 | tf_op jit(solution)/shard_map/experts/pallas_call | solution.py:239
  122.3 0.3 collective-permute-start.24
  122.6 1.7 %collective-permute-start.25 = (bf16[64,2048]{1,0:T(8,128)(2,1)S(1)}, bf16[64,2048]{1,0:T(8,128)(2,1)S(1)}, u32[]{:S(2)}, u32[]{:S(2)}) collective-permute-start(bf16[64,2048]{1,0:T(8,128)(2,1)S(1)} %get-tuple-element.58), channel_id=1, source_target_pairs={{0,4},{4,8},{8,12},{12,14},{14,10},{10,6},{6,2},{2,0},{1,5},{5,9},... | collective-permute-start | bytes 786440 | tf_op jit(solution)/shard_map/ppermute | solution.py:408
  124.5 0.5 collective-permute-start.34
  125.0 1.6 %collective-permute-start.35 = (bf16[64,2048]{1,0:T(8,128)(2,1)S(1)}, bf16[64,2048]{1,0:T(8,128)(2,1)S(1)}, u32[]{:S(2)}, u32[]{:S(2)}) collective-permute-start(bf16[64,2048]{1,0:T(8,128)(2,1)S(1)} %get-tuple-element.72), channel_id=1, source_target_pairs={{4,0},{8,4},{12,8},{14,12},{10,14},{6,10},{2,6},{0,2},{5,1},{9,5},... | collective-permute-start | bytes 786440 | tf_op jit(solution)/shard_map/ppermute | solution.py:408
  126.5 4.7 %experts.8 = (f32[64,2048]{1,0:T(8,128)S(1)}, f32[64,2048]{1,0:T(8,128)S(1)}) custom-call(s32[2]{0:T(128)S(1)} %pad_add_fusion.ids, bf16[64,2048]{1,0:T(8,128)(2,1)S(1)} %copy-done.7, bf16[64,2048]{1,0:T(8,128)(2,1)S(1)} %copy-done.3, f32[8,16,128]{2,1,0:T(8,128)S(1)} %pad_maximum_fusion.refs_2_, bf16[2048,384]{1,0:T(8,128)(2,1)S(1)} %bitcast.16, ...), custom_call_target="tpu_custom_call" | custom-call | flops 1207959552 | bytes 9437184 | tf_op jit(solution)/shard_map/experts/pallas_call | solution.py:239
  131.3 0.4 collective-permute-done.34.refs_6_
  131.8 1.0 finish.1
  (91 shorter events, 1.4 us)
Async XLA Ops:
  1.3 8.4 %copy-start.28 = (s32[2]{0:T(128)S(1)}, s32[2]{0:T(128)}, u32[]{:S(2)}) copy-start(s32[2]{0:T(128)} %span_req.3) | copy-start | bytes 28
  9.1 8.1 %copy-start.25 = (s32[128,8]{0,1:T(8,128)S(1)}, s32[128,8]{0,1:T(8,128)}, u32[]{:S(2)}) copy-start(s32[128,8]{0,1:T(8,128)} %param.25) | copy-start | bytes 12292
  9.1 8.1 %copy-start.26 = (f32[128,8]{0,1:T(8,128)S(1)}, f32[128,8]{0,1:T(8,128)}, u32[]{:S(2)}) copy-start(f32[128,8]{0,1:T(8,128)} %param.26) | copy-start | bytes 12292
  9.1 14.9 %copy-start.24 = (f32[2048]{0:T(1024)S(1)}, f32[2048]{0:T(1024)}, u32[]{:S(2)}) copy-start(f32[2048]{0:T(1024)} %param.24) | copy-start | bytes 24580
  9.2 14.9 %collective-permute-start.1 = (f32[64,2048]{1,0:T(8,128)S(1)}, f32[64,2048]{1,0:T(8,128)S(1)}, u32[]{:S(2)}, u32[]{:S(2)}) collective-permute-start(f32[64,2048]{1,0:T(8,128)S(1)} %get-tuple-element.43), channel_id=1, source_target_pairs={{0,1},{1,0},{2,3},{3,2},{4,5},{5,4},{6,7},{7,6},{8,9},{9,8},{10,11... | collective-permute-start | bytes 1572872 | tf_op jit(solution)/shard_map/ppermute | solution.py:373
  9.7 24.3 %copy-start.1 = (bf16[1,2048,384]{2,1,0:T(8,128)(2,1)S(1)}, bf16[1,2048,384]{2,1,0:T(8,128)(2,1)}, u32[]{:S(2)}) copy-start(bf16[1,2048,384]{2,1,0:T(8,128)(2,1)} %param.28) | copy-start | bytes 4718596
  17.1 13.3 %copy-start = (bf16[1,2048,384]{2,1,0:T(8,128)(2,1)S(1)}, bf16[1,2048,384]{2,1,0:T(8,128)(2,1)}, u32[]{:S(2)}) copy-start(bf16[1,2048,384]{2,1,0:T(8,128)(2,1)} %param.27) | copy-start | bytes 4718596
  17.1 16.9 %collective-permute-start = (f32[64,2048]{1,0:T(8,128)S(1)}, f32[64,2048]{1,0:T(8,128)S(1)}, u32[]{:S(2)}, u32[]{:S(2)}) collective-permute-start(f32[64,2048]{1,0:T(8,128)S(1)} %get-tuple-element.40), channel_id=1, source_target_pairs={{0,1},{1,0},{2,3},{3,2},{4,5},{5,4},{6,7},{7,6},{8,9},{9,8},{10,11... | collective-permute-start | bytes 1572872 | tf_op jit(solution)/shard_map/ppermute | solution.py:373
  17.3 4.7 %collective-permute-start.2 = (f32[1,16,128]{2,1,0:T(8,128)S(1)}, f32[1,16,128]{2,1,0:T(8,128)S(1)}, u32[]{:S(2)}, u32[]{:S(2)}) collective-permute-start(f32[1,16,128]{2,1,0:T(8,128)S(1)} %weigh.1), channel_id=1, source_target_pairs={{0,2},{2,0},{4,6},{6,4},{8,10},{10,8},{12,14},{14,12},{1,3},{3,1},... | collective-permute-start | bytes 24584 | tf_op jit(solution)/shard_map/ppermute | solution.py:354
  21.9 4.9 %collective-permute-start.3 = (f32[2,16,128]{2,1,0:T(8,128)S(1)}, f32[2,16,128]{2,1,0:T(8,128)S(1)}, u32[]{:S(2)}, u32[]{:S(2)}) collective-permute-start(f32[2,16,128]{2,1,0:T(8,128)S(1)} %pad_maximum_fusion.2), channel_id=1, source_target_pairs={{0,4},{2,6},{4,0},{6,2},{8,12},{10,14},{12,8},{14,10},{1,5},{3,7},... | collective-permute-start | bytes 49160 | tf_op jit(solution)/shard_map/ppermute | solution.py:354
  25.2 10.5 %copy-start.2 = (bf16[64,2048]{1,0:T(8,128)(2,1)}, bf16[64,2048]{1,0:T(8,128)(2,1)S(1)}, u32[]{:S(2)}) copy-start(bf16[64,2048]{1,0:T(8,128)(2,1)S(1)} %get-tuple-element.46.refs_1_) | copy-start | bytes 786436
  25.2 11.2 %collective-permute-start.11 = (bf16[64,2048]{1,0:T(8,128)(2,1)S(1)}, bf16[64,2048]{1,0:T(8,128)(2,1)S(1)}, u32[]{:S(2)}, u32[]{:S(2)}) collective-permute-start(bf16[64,2048]{1,0:T(8,128)(2,1)S(1)} %get-tuple-element.46.refs_1_), channel_id=1, source_target_pairs={{4,0},{8,4},{12,8},{14,12},{10,14},{6,10},{2,6},{0,2},{5,1},{9,5},... | collective-permute-start | bytes 786440 | tf_op jit(solution)/shard_map/ppermute | solution.py:394
  26.8 7.2 %collective-permute-start.4 = (f32[4,16,128]{2,1,0:T(8,128)S(1)}, f32[4,16,128]{2,1,0:T(8,128)S(1)}, u32[]{:S(2)}, u32[]{:S(2)}) collective-permute-start(f32[4,16,128]{2,1,0:T(8,128)S(1)} %pad_maximum_fusion.1), channel_id=1, source_target_pairs={{0,8},{2,10},{4,12},{6,14},{8,0},{10,2},{12,4},{14,6},{1,9},{3,11}... | collective-permute-start | bytes 98312 | tf_op jit(solution)/shard_map/ppermute | solution.py:354
  28.8 7.7 %collective-permute-start.10 = (bf16[64,2048]{1,0:T(8,128)(2,1)S(1)}, bf16[64,2048]{1,0:T(8,128)(2,1)S(1)}, u32[]{:S(2)}, u32[]{:S(2)}) collective-permute-start(bf16[64,2048]{1,0:T(8,128)(2,1)S(1)} %get-tuple-element.46.refs_1_), channel_id=1, source_target_pairs={{0,4},{4,8},{8,12},{12,14},{14,10},{10,6},{6,2},{2,0},{1,5},{5,9},... | collective-permute-start | bytes 786440 | tf_op jit(solution)/shard_map/ppermute | solution.py:394
  30.4 46.9 %collective-permute-start.5 = (bf16[2048,384]{1,0:T(8,128)(2,1)S(1)}, bf16[2048,384]{1,0:T(8,128)(2,1)}, u32[]{:S(2)}, u32[]{:S(2)}) collective-permute-start(bf16[2048,384]{1,0:T(8,128)(2,1)S(1)} %bitcast.8), channel_id=1, source_target_pairs={{0,1},{1,0},{2,3},{3,2},{4,5},{5,4},{6,7},{7,6},{8,9},{9,8},{10,11... | collective-permute-start | bytes 4718600 | tf_op jit(solution)/shard_map/ppermute | solution.py:349
  34.0 43.2 %collective-permute-start.6 = (bf16[2048,384]{1,0:T(8,128)(2,1)S(1)}, bf16[2048,384]{1,0:T(8,128)(2,1)}, u32[]{:S(2)}, u32[]{:S(2)}) collective-permute-start(bf16[2048,384]{1,0:T(8,128)(2,1)S(1)} %bitcast.17), channel_id=1, source_target_pairs={{0,1},{1,0},{2,3},{3,2},{4,5},{5,4},{6,7},{7,6},{8,9},{9,8},{10,11... | collective-permute-start | bytes 4718600 | tf_op jit(solution)/shard_map/ppermute | solution.py:349
  34.0 43.2 %collective-permute-start.7 = (bf16[384,2048]{1,0:T(8,128)(2,1)}, bf16[384,2048]{1,0:T(8,128)(2,1)}, u32[]{:S(2)}, u32[]{:S(2)}) collective-permute-start(bf16[384,2048]{1,0:T(8,128)(2,1)} %bitcast.7.refs_5_), channel_id=1, source_target_pairs={{0,1},{1,0},{2,3},{3,2},{4,5},{5,4},{6,7},{7,6},{8,9},{9,8},{10,11... | collective-permute-start | bytes 4718600 | tf_op jit(solution)/shard_map/ppermute | solution.py:349
  35.7 0.7 copy-start.4
  36.4 8.3 %collective-permute-start.9 = (bf16[64,2048]{1,0:T(8,128)(2,1)S(1)}, bf16[64,2048]{1,0:T(8,128)(2,1)S(1)}, u32[]{:S(2)}, u32[]{:S(2)}) collective-permute-start(bf16[64,2048]{1,0:T(8,128)(2,1)S(1)} %get-tuple-element.45.refs_0_), channel_id=1, source_target_pairs={{4,0},{8,4},{12,8},{14,12},{10,14},{6,10},{2,6},{0,2},{5,1},{9,5},... | collective-permute-start | bytes 786440 | tf_op jit(solution)/shard_map/ppermute | solution.py:394
  36.5 9.3 %collective-permute-start.8 = (bf16[64,2048]{1,0:T(8,128)(2,1)S(1)}, bf16[64,2048]{1,0:T(8,128)(2,1)S(1)}, u32[]{:S(2)}, u32[]{:S(2)}) collective-permute-start(bf16[64,2048]{1,0:T(8,128)(2,1)S(1)} %get-tuple-element.45.refs_0_), channel_id=1, source_target_pairs={{0,4},{4,8},{8,12},{12,14},{14,10},{10,6},{6,2},{2,0},{1,5},{5,9},... | collective-permute-start | bytes 786440 | tf_op jit(solution)/shard_map/ppermute | solution.py:394
  38.5 0.7 copy-start.6
  44.7 7.4 %collective-permute-start.15 = (bf16[64,2048]{1,0:T(8,128)(2,1)S(1)}, bf16[64,2048]{1,0:T(8,128)(2,1)S(1)}, u32[]{:S(2)}, u32[]{:S(2)}) collective-permute-start(bf16[64,2048]{1,0:T(8,128)(2,1)S(1)} %collective-permute-done.11.refs_1_), channel_id=1, source_target_pairs={{4,0},{8,4},{12,8},{14,12},{10,14},{6,10},{2,6},{0,2},{5,1},{9,5},... | collective-permute-start | bytes 786440 | tf_op jit(solution)/shard_map/ppermute | solution.py:394
  45.0 0.7 copy-start.8
  45.7 7.7 %collective-permute-start.14 = (bf16[64,2048]{1,0:T(8,128)(2,1)S(1)}, bf16[64,2048]{1,0:T(8,128)(2,1)S(1)}, u32[]{:S(2)}, u32[]{:S(2)}) collective-permute-start(bf16[64,2048]{1,0:T(8,128)(2,1)S(1)} %collective-permute-done.10.refs_0_), channel_id=1, source_target_pairs={{0,4},{4,8},{8,12},{12,14},{14,10},{10,6},{6,2},{2,0},{1,5},{5,9},... | collective-permute-start | bytes 786440 | tf_op jit(solution)/shard_map/ppermute | solution.py:394
  47.5 0.7 copy-start.10
  52.1 6.6 %collective-permute-start.13 = (bf16[64,2048]{1,0:T(8,128)(2,1)S(1)}, bf16[64,2048]{1,0:T(8,128)(2,1)S(1)}, u32[]{:S(2)}, u32[]{:S(2)}) collective-permute-start(bf16[64,2048]{1,0:T(8,128)(2,1)S(1)} %collective-permute-done.9.refs_1_), channel_id=1, source_target_pairs={{4,0},{8,4},{12,8},{14,12},{10,14},{6,10},{2,6},{0,2},{5,1},{9,5},... | collective-permute-start | bytes 786440 | tf_op jit(solution)/shard_map/ppermute | solution.py:394
  52.7 0.7 copy-start.12
  53.4 12.4 %copy-start.18 = (bf16[64,2048]{1,0:T(8,128)(2,1)}, bf16[64,2048]{1,0:T(8,128)(2,1)S(1)}, u32[]{:S(2)}) copy-start(bf16[64,2048]{1,0:T(8,128)(2,1)S(1)} %collective-permute-done.14.refs_0_) | copy-start | bytes 786436
  53.4 6.9 %collective-permute-start.12 = (bf16[64,2048]{1,0:T(8,128)(2,1)S(1)}, bf16[64,2048]{1,0:T(8,128)(2,1)S(1)}, u32[]{:S(2)}, u32[]{:S(2)}) collective-permute-start(bf16[64,2048]{1,0:T(8,128)(2,1)S(1)} %collective-permute-done.8.refs_0_), channel_id=1, source_target_pairs={{0,4},{4,8},{8,12},{12,14},{14,10},{10,6},{6,2},{2,0},{1,5},{5,9},... | collective-permute-start | bytes 786440 | tf_op jit(solution)/shard_map/ppermute | solution.py:394
  54.9 0.7 copy-start.14
  58.7 7.8 %copy-start.20 = (bf16[64,2048]{1,0:T(8,128)(2,1)}, bf16[64,2048]{1,0:T(8,128)(2,1)S(1)}, u32[]{:S(2)}) copy-start(bf16[64,2048]{1,0:T(8,128)(2,1)S(1)} %collective-permute-done.13.refs_1_) | copy-start | bytes 786436
  58.7 7.1 %collective-permute-start.20 = (bf16[64,2048]{1,0:T(8,128)(2,1)S(1)}, bf16[64,2048]{1,0:T(8,128)(2,1)}, u32[]{:S(2)}, u32[]{:S(2)}) collective-permute-start(bf16[64,2048]{1,0:T(8,128)(2,1)S(1)} %collective-permute-done.15.refs_1_), channel_id=1, source_target_pairs={{4,0},{8,4},{12,8},{14,12},{10,14},{6,10},{2,6},{0,2},{5,1},{9,5},... | collective-permute-start | bytes 786440 | tf_op jit(solution)/shard_map/ppermute | solution.py:394
  59.6 0.7 copy-start.16
  60.3 6.9 %collective-permute-start.16 = (bf16[64,2048]{1,0:T(8,128)(2,1)S(1)}, bf16[64,2048]{1,0:T(8,128)(2,1)}, u32[]{:S(2)}, u32[]{:S(2)}) collective-permute-start(bf16[64,2048]{1,0:T(8,128)(2,1)S(1)} %collective-permute-done.12.refs_0_), channel_id=1, source_target_pairs={{0,4},{4,8},{8,12},{12,14},{14,10},{10,6},{6,2},{2,0},{1,5},{5,9},... | collective-permute-start | bytes 786440 | tf_op jit(solution)/shard_map/ppermute | solution.py:394
  61.5 0.7 copy-start.22
  65.9 8.5 %collective-permute-start.27 = (bf16[64,2048]{1,0:T(8,128)(2,1)}, bf16[64,2048]{1,0:T(8,128)(2,1)}, u32[]{:S(2)}, u32[]{:S(2)}) collective-permute-start(bf16[64,2048]{1,0:T(8,128)(2,1)} %collective-permute-done.20.refs_1_), channel_id=1, source_target_pairs={{4,0},{8,4},{12,8},{14,12},{10,14},{6,10},{2,6},{0,2},{5,1},{9,5},... | collective-permute-start | bytes 786440 | tf_op jit(solution)/shard_map/ppermute | solution.py:404
  67.2 8.3 %collective-permute-start.26 = (bf16[64,2048]{1,0:T(8,128)(2,1)}, bf16[64,2048]{1,0:T(8,128)(2,1)}, u32[]{:S(2)}, u32[]{:S(2)}) collective-permute-start(bf16[64,2048]{1,0:T(8,128)(2,1)} %collective-permute-done.16.refs_0_), channel_id=1, source_target_pairs={{0,4},{4,8},{8,12},{12,14},{14,10},{10,6},{6,2},{2,0},{1,5},{5,9},... | collective-permute-start | bytes 786440 | tf_op jit(solution)/shard_map/ppermute | solution.py:404
  74.4 9.9 %collective-permute-start.17 = (bf16[64,2048]{1,0:T(8,128)(2,1)}, bf16[64,2048]{1,0:T(8,128)(2,1)S(1)}, u32[]{:S(2)}, u32[]{:S(2)}) collective-permute-start(bf16[64,2048]{1,0:T(8,128)(2,1)} %copy-done.20), channel_id=1, source_target_pairs={{4,0},{8,4},{12,8},{14,12},{10,14},{6,10},{2,6},{0,2},{5,1},{9,5},... | collective-permute-start | bytes 786440 | tf_op jit(solution)/shard_map/ppermute | solution.py:394
  75.5 14.1 %collective-permute-start.19 = (bf16[64,2048]{1,0:T(8,128)(2,1)}, bf16[64,2048]{1,0:T(8,128)(2,1)S(1)}, u32[]{:S(2)}, u32[]{:S(2)}) collective-permute-start(bf16[64,2048]{1,0:T(8,128)(2,1)} %copy-done.18), channel_id=1, source_target_pairs={{0,4},{4,8},{8,12},{12,14},{14,10},{10,6},{6,2},{2,0},{1,5},{5,9},... | collective-permute-start | bytes 786440 | tf_op jit(solution)/shard_map/ppermute | solution.py:394
  82.2 14.1 %collective-permute-start.28 = (bf16[64,2048]{1,0:T(8,128)(2,1)S(1)}, bf16[64,2048]{1,0:T(8,128)(2,1)S(1)}, u32[]{:S(2)}, u32[]{:S(2)}) collective-permute-start(bf16[64,2048]{1,0:T(8,128)(2,1)S(1)} %get-tuple-element.65), channel_id=1, source_target_pairs={{0,4},{4,8},{8,12},{12,14},{14,10},{10,6},{6,2},{2,0},{1,5},{5,9},... | collective-permute-start | bytes 786440 | tf_op jit(solution)/shard_map/ppermute | solution.py:408
  82.7 13.6 %collective-permute-start.29 = (bf16[64,2048]{1,0:T(8,128)(2,1)S(1)}, bf16[64,2048]{1,0:T(8,128)(2,1)S(1)}, u32[]{:S(2)}, u32[]{:S(2)}) collective-permute-start(bf16[64,2048]{1,0:T(8,128)(2,1)S(1)} %get-tuple-element.66), channel_id=1, source_target_pairs={{4,0},{8,4},{12,8},{14,12},{10,14},{6,10},{2,6},{0,2},{5,1},{9,5},... | collective-permute-start | bytes 786440 | tf_op jit(solution)/shard_map/ppermute | solution.py:408
  89.1 19.0 %collective-permute-start.18 = (bf16[64,2048]{1,0:T(8,128)(2,1)S(1)}, bf16[64,2048]{1,0:T(8,128)(2,1)S(1)}, u32[]{:S(2)}, u32[]{:S(2)}) collective-permute-start(bf16[64,2048]{1,0:T(8,128)(2,1)S(1)} %get-tuple-element.53), channel_id=1, source_target_pairs={{4,0},{8,4},{12,8},{14,12},{10,14},{6,10},{2,6},{0,2},{5,1},{9,5},... | collective-permute-start | bytes 786440 | tf_op jit(solution)/shard_map/ppermute | solution.py:408
  94.4 4.1 %copy-start.17 = (bf16[64,2048]{1,0:T(8,128)(2,1)S(1)}, bf16[64,2048]{1,0:T(8,128)(2,1)}, u32[]{:S(2)}) copy-start(bf16[64,2048]{1,0:T(8,128)(2,1)} %copy-done.16) | copy-start | bytes 786436
  94.4 4.1 %copy-start.19 = (bf16[64,2048]{1,0:T(8,128)(2,1)S(1)}, bf16[64,2048]{1,0:T(8,128)(2,1)}, u32[]{:S(2)}) copy-start(bf16[64,2048]{1,0:T(8,128)(2,1)} %copy-done.18) | copy-start | bytes 786436
  94.4 13.6 %collective-permute-start.21 = (bf16[64,2048]{1,0:T(8,128)(2,1)S(1)}, bf16[64,2048]{1,0:T(8,128)(2,1)S(1)}, u32[]{:S(2)}, u32[]{:S(2)}) collective-permute-start(bf16[64,2048]{1,0:T(8,128)(2,1)S(1)} %get-tuple-element.54), channel_id=1, source_target_pairs={{0,4},{4,8},{8,12},{12,14},{14,10},{10,6},{6,2},{2,0},{1,5},{5,9},... | collective-permute-start | bytes 786440 | tf_op jit(solution)/shard_map/ppermute | solution.py:408
  96.4 13.9 %collective-permute-start.30 = (bf16[64,2048]{1,0:T(8,128)(2,1)S(1)}, bf16[64,2048]{1,0:T(8,128)(2,1)S(1)}, u32[]{:S(2)}, u32[]{:S(2)}) collective-permute-start(bf16[64,2048]{1,0:T(8,128)(2,1)S(1)} %get-tuple-element.67), channel_id=1, source_target_pairs={{0,4},{4,8},{8,12},{12,14},{14,10},{10,6},{6,2},{2,0},{1,5},{5,9},... | collective-permute-start | bytes 786440 | tf_op jit(solution)/shard_map/ppermute | solution.py:408
  96.9 6.3 %copy-start.21 = (bf16[64,2048]{1,0:T(8,128)(2,1)S(1)}, bf16[64,2048]{1,0:T(8,128)(2,1)}, u32[]{:S(2)}) copy-start(bf16[64,2048]{1,0:T(8,128)(2,1)} %copy-done.20) | copy-start | bytes 786436
  96.9 6.3 %copy-start.23 = (bf16[64,2048]{1,0:T(8,128)(2,1)S(1)}, bf16[64,2048]{1,0:T(8,128)(2,1)}, u32[]{:S(2)}) copy-start(bf16[64,2048]{1,0:T(8,128)(2,1)} %copy-done.22) | copy-start | bytes 786436
  96.9 13.4 %collective-permute-start.31 = (bf16[64,2048]{1,0:T(8,128)(2,1)S(1)}, bf16[64,2048]{1,0:T(8,128)(2,1)S(1)}, u32[]{:S(2)}, u32[]{:S(2)}) collective-permute-start(bf16[64,2048]{1,0:T(8,128)(2,1)S(1)} %get-tuple-element.68), channel_id=1, source_target_pairs={{4,0},{8,4},{12,8},{14,12},{10,14},{6,10},{2,6},{0,2},{5,1},{9,5},... | collective-permute-start | bytes 786440 | tf_op jit(solution)/shard_map/ppermute | solution.py:408
  108.0 4.5 %copy-start.9 = (bf16[64,2048]{1,0:T(8,128)(2,1)S(1)}, bf16[64,2048]{1,0:T(8,128)(2,1)}, u32[]{:S(2)}) copy-start(bf16[64,2048]{1,0:T(8,128)(2,1)} %copy-done.8) | copy-start | bytes 786436
  108.1 4.5 %copy-start.11 = (bf16[64,2048]{1,0:T(8,128)(2,1)S(1)}, bf16[64,2048]{1,0:T(8,128)(2,1)}, u32[]{:S(2)}) copy-start(bf16[64,2048]{1,0:T(8,128)(2,1)} %copy-done.10) | copy-start | bytes 786436
  108.2 13.9 %collective-permute-start.22 = (bf16[64,2048]{1,0:T(8,128)(2,1)S(1)}, bf16[64,2048]{1,0:T(8,128)(2,1)S(1)}, u32[]{:S(2)}, u32[]{:S(2)}) collective-permute-start(bf16[64,2048]{1,0:T(8,128)(2,1)S(1)} %get-tuple-element.55), channel_id=1, source_target_pairs={{4,0},{8,4},{12,8},{14,12},{10,14},{6,10},{2,6},{0,2},{5,1},{9,5},... | collective-permute-start | bytes 786440 | tf_op jit(solution)/shard_map/ppermute | solution.py:408
  108.5 13.5 %collective-permute-start.23 = (bf16[64,2048]{1,0:T(8,128)(2,1)S(1)}, bf16[64,2048]{1,0:T(8,128)(2,1)S(1)}, u32[]{:S(2)}, u32[]{:S(2)}) collective-permute-start(bf16[64,2048]{1,0:T(8,128)(2,1)S(1)} %get-tuple-element.56), channel_id=1, source_target_pairs={{0,4},{4,8},{8,12},{12,14},{14,10},{10,6},{6,2},{2,0},{1,5},{5,9},... | collective-permute-start | bytes 786440 | tf_op jit(solution)/shard_map/ppermute | solution.py:408
  110.4 13.9 %collective-permute-start.32 = (bf16[64,2048]{1,0:T(8,128)(2,1)S(1)}, bf16[64,2048]{1,0:T(8,128)(2,1)S(1)}, u32[]{:S(2)}, u32[]{:S(2)}) collective-permute-start(bf16[64,2048]{1,0:T(8,128)(2,1)S(1)} %get-tuple-element.69), channel_id=1, source_target_pairs={{0,4},{4,8},{8,12},{12,14},{14,10},{10,6},{6,2},{2,0},{1,5},{5,9},... | collective-permute-start | bytes 786440 | tf_op jit(solution)/shard_map/ppermute | solution.py:408
  111.0 6.3 %copy-start.13 = (bf16[64,2048]{1,0:T(8,128)(2,1)S(1)}, bf16[64,2048]{1,0:T(8,128)(2,1)}, u32[]{:S(2)}) copy-start(bf16[64,2048]{1,0:T(8,128)(2,1)} %copy-done.12) | copy-start | bytes 786436
  111.0 6.3 %copy-start.15 = (bf16[64,2048]{1,0:T(8,128)(2,1)S(1)}, bf16[64,2048]{1,0:T(8,128)(2,1)}, u32[]{:S(2)}) copy-start(bf16[64,2048]{1,0:T(8,128)(2,1)} %copy-done.14) | copy-start | bytes 786436
  111.0 13.4 %collective-permute-start.33 = (bf16[64,2048]{1,0:T(8,128)(2,1)S(1)}, bf16[64,2048]{1,0:T(8,128)(2,1)S(1)}, u32[]{:S(2)}, u32[]{:S(2)}) collective-permute-start(bf16[64,2048]{1,0:T(8,128)(2,1)S(1)} %get-tuple-element.70), channel_id=1, source_target_pairs={{4,0},{8,4},{12,8},{14,12},{10,14},{6,10},{2,6},{0,2},{5,1},{9,5},... | collective-permute-start | bytes 786440 | tf_op jit(solution)/shard_map/ppermute | solution.py:408
  122.1 4.5 %copy-start.3 = (bf16[64,2048]{1,0:T(8,128)(2,1)S(1)}, bf16[64,2048]{1,0:T(8,128)(2,1)}, u32[]{:S(2)}) copy-start(bf16[64,2048]{1,0:T(8,128)(2,1)} %copy-done.2) | copy-start | bytes 786436
  122.1 4.5 %copy-start.7 = (bf16[64,2048]{1,0:T(8,128)(2,1)S(1)}, bf16[64,2048]{1,0:T(8,128)(2,1)}, u32[]{:S(2)}) copy-start(bf16[64,2048]{1,0:T(8,128)(2,1)} %copy-done.6) | copy-start | bytes 786436
  122.3 9.1 %collective-permute-start.24 = (bf16[64,2048]{1,0:T(8,128)(2,1)S(1)}, bf16[64,2048]{1,0:T(8,128)(2,1)S(1)}, u32[]{:S(2)}, u32[]{:S(2)}) collective-permute-start(bf16[64,2048]{1,0:T(8,128)(2,1)S(1)} %get-tuple-element.57), channel_id=1, source_target_pairs={{4,0},{8,4},{12,8},{14,12},{10,14},{6,10},{2,6},{0,2},{5,1},{9,5},... | collective-permute-start | bytes 786440 | tf_op jit(solution)/shard_map/ppermute | solution.py:408
  122.6 8.7 %collective-permute-start.25 = (bf16[64,2048]{1,0:T(8,128)(2,1)S(1)}, bf16[64,2048]{1,0:T(8,128)(2,1)S(1)}, u32[]{:S(2)}, u32[]{:S(2)}) collective-permute-start(bf16[64,2048]{1,0:T(8,128)(2,1)S(1)} %get-tuple-element.58), channel_id=1, source_target_pairs={{0,4},{4,8},{8,12},{12,14},{14,10},{10,6},{6,2},{2,0},{1,5},{5,9},... | collective-permute-start | bytes 786440 | tf_op jit(solution)/shard_map/ppermute | solution.py:408
  124.5 7.3 %collective-permute-start.34 = (bf16[64,2048]{1,0:T(8,128)(2,1)S(1)}, bf16[64,2048]{1,0:T(8,128)(2,1)S(1)}, u32[]{:S(2)}, u32[]{:S(2)}) collective-permute-start(bf16[64,2048]{1,0:T(8,128)(2,1)S(1)} %get-tuple-element.71), channel_id=1, source_target_pairs={{0,4},{4,8},{8,12},{12,14},{14,10},{10,6},{6,2},{2,0},{1,5},{5,9},... | collective-permute-start | bytes 786440 | tf_op jit(solution)/shard_map/ppermute | solution.py:408
  125.0 6.8 %copy-start.5 = (bf16[64,2048]{1,0:T(8,128)(2,1)S(1)}, bf16[64,2048]{1,0:T(8,128)(2,1)}, u32[]{:S(2)}) copy-start(bf16[64,2048]{1,0:T(8,128)(2,1)} %copy-done.4) | copy-start | bytes 786436
  125.0 6.8 %collective-permute-start.35 = (bf16[64,2048]{1,0:T(8,128)(2,1)S(1)}, bf16[64,2048]{1,0:T(8,128)(2,1)S(1)}, u32[]{:S(2)}, u32[]{:S(2)}) collective-permute-start(bf16[64,2048]{1,0:T(8,128)(2,1)S(1)} %get-tuple-element.72), channel_id=1, source_target_pairs={{4,0},{8,4},{12,8},{14,12},{10,14},{6,10},{2,6},{0,2},{5,1},{9,5},... | collective-permute-start | bytes 786440 | tf_op jit(solution)/shard_map/ppermute | solution.py:408
  (2 other events, 1.3 us)

commit v3 on v2

--- a/solution.py
+++ b/solution.py
@@ -40,73 +40,93 @@
 
 def attend_kernel(
     first_row,
-    core,
+    ids,
     span_req,
     cache_len,
+    q_hbm,
+    nk_hbm,
+    nv_hbm,
+    ck_hbm,
+    cv_hbm,
+    w_hbm,
+    far_ref,
+    near_ref,
     q_ref,
     nk_ref,
     nv_ref,
     ck_ref,
     cv_ref,
-    w_hbm,
-    far_ref,
-    near_ref,
     w_ref,
-    w_sem,
+    sems,
 ):
-    step = pl.program_id(0)
-    spans = pl.num_programs(0)
-    fetch = pltpu.make_async_copy(w_hbm, w_ref, w_sem)
-
-    @pl.when(step == 0)
-    def _():
-        fetch.start()
-
-    rows = q_ref.shape[0]
-    heads = q_ref.shape[1] // HD
-    length = nk_ref.shape[0]
+    spans, rows, width = q_ref.shape
+    heads = width // HD
+    length = nk_ref.shape[1]
     to_exp2 = math.log2(math.e) / math.sqrt(HD)
-    span = lax.rem(core[0] + step + 1, spans)
-    held = cache_len[lax.rem(span_req[span], spans)]
-    q = jnp.concatenate([q_ref[:, h * HD : (h + 1) * HD] for h in range(heads)], axis=0)
     dims = (((1,), (1,)), ((), ()))
-    old = lax.dot_general(q, ck_ref[0], dims, preferred_element_type=jnp.float32)
-    new = lax.dot_general(q, nk_ref[...], dims, preferred_element_type=jnp.float32)
-    key_at = lax.broadcasted_iota(jnp.int32, (1, old.shape[1]), 1)
-    old = jnp.where(key_at < held, old, negative_fill)
+    copies, held = [], []
+    for i in range(spans):
+        span = lax.rem(ids[1] + i + 1, spans)
+        request = lax.rem(span_req[span], spans)
+        held.append(cache_len[request])
+        first = pl.multiple_of(span * length, length)
+        sources = (
+            q_hbm.at[pl.ds(pl.multiple_of(first + first_row, rows), rows)],
+            ck_hbm.at[request],
+            nk_hbm.at[pl.ds(first, length)],
+            cv_hbm.at[request],
+            nv_hbm.at[pl.ds(first, length)],
+        )
+        copies.append(
+            [
+                pltpu.make_async_copy(source, target.at[i], sems.at[i, j])
+                for j, (source, target) in enumerate(
+                    zip(sources, (q_ref, ck_ref, nk_ref, cv_ref, nv_ref))
+                )
+            ]
+        )
+        for copy in copies[i]:
+            copy.start()
+    fetch = pltpu.make_async_copy(w_hbm, w_ref, sems.at[spans, 0])
+    fetch.start()
     own_at = lax.broadcasted_iota(jnp.int32, (rows, length), 1)
     own_row = first_row + lax.broadcasted_iota(jnp.int32, (rows, length), 0)
     fill = jnp.where(own_at <= own_row, 0.0, negative_fill)
-    new = new + jnp.concatenate([fill] * heads, axis=0)
-    top = jnp.maximum(
-        jnp.max(old, axis=1, keepdims=True), jnp.max(new, axis=1, keepdims=True)
-    )
-    old = jnp.exp2((old - top) * to_exp2)
-    new = jnp.exp2((new - top) * to_exp2)
-    total = jnp.sum(old, axis=1, keepdims=True) + jnp.sum(new, axis=1, keepdims=True)
-    out = jnp.dot(old.astype(jnp.bfloat16), cv_ref[0], preferred_element_type=jnp.float32)
-    out += jnp.dot(new.astype(jnp.bfloat16), nv_ref[...], preferred_element_type=jnp.float32)
-    out = (out / total).astype(jnp.bfloat16)
-    out = jnp.concatenate([out[h * rows : (h + 1) * rows] for h in range(heads)], axis=1)
-
-    @pl.when(step == 0)
-    def _():
-        fetch.wait()
-
-    out = jnp.dot(out, w_ref[...], preferred_element_type=jnp.float32)
-
-    @pl.when(step == 0)
-    def _():
-        far_ref[...] = out
-
-    @pl.when(step == spans - 1)
-    def _():
-        near_ref[...] = out
+    fill = jnp.concatenate([fill] * heads, axis=0)
+    key_at = lax.broadcasted_iota(jnp.int32, (1, ck_ref.shape[1]), 1)
+    attended = []
+    for i in range(spans):
+        for copy in copies[i][:3]:
+            copy.wait()
+        q = jnp.concatenate([q_ref[i, :, h * HD : (h + 1) * HD] for h in range(heads)], axis=0)
+        old = lax.dot_general(q, ck_ref[i], dims, preferred_element_type=jnp.float32)
+        new = lax.dot_general(q, nk_ref[i], dims, preferred_element_type=jnp.float32) + fill
+        old = jnp.where(key_at < held[i], old, negative_fill)
+        top = jnp.maximum(
+            jnp.max(old, axis=1, keepdims=True), jnp.max(new, axis=1, keepdims=True)
+        )
+        old = jnp.exp2((old - top) * to_exp2)
+        new = jnp.exp2((new - top) * to_exp2)
+        total = jnp.sum(old, axis=1, keepdims=True) + jnp.sum(new, axis=1, keepdims=True)
+        for copy in copies[i][3:]:
+            copy.wait()
+        out = jnp.dot(old.astype(jnp.bfloat16), cv_ref[i], preferred_element_type=jnp.float32)
+        out += jnp.dot(new.astype(jnp.bfloat16), nv_ref[i], preferred_element_type=jnp.float32)
+        out = (out / total).astype(jnp.bfloat16)
+        attended.append(
+            jnp.concatenate([out[h * rows : (h + 1) * rows] for h in range(heads)], axis=1)
+        )
+    fetch.wait()
+    out = jnp.dot(
+        jnp.concatenate(attended, axis=0), w_ref[...], preferred_element_type=jnp.float32
+    )
+    far_ref[...] = out[:rows]
+    near_ref[...] = out[rows:]
 
 
 def attend_chunk(
     chunk,
-    core,
+    ids,
     span_req,
     cache_len,
     queries,
@@ -120,57 +140,38 @@
     length = queries.shape[0] // spans
     rows = length // CHUNKS
     width = out_proj.shape[1]
-    shape = pltpu.VMEM((rows, width), jnp.float32)
+    kind = queries.dtype
     macs = spans * rows * (queries.shape[1] * (2 * (cache_size + length) + width))
-
-    def span_at(i, core):
-        return lax.rem(core[0] + i + 1, spans)
-
-    def request_at(i, core, span_req):
-        return lax.rem(span_req[span_at(i, core)], spans)
-
-    new_spec = pl.BlockSpec((length, HD), lambda i, c, r, n: (span_at(i, c), 0))
-    old_spec = pl.BlockSpec((1, cache_size, HD), lambda i, c, r, n: (request_at(i, c, r), 0, 0))
-    out_spec = pl.BlockSpec((rows, width), lambda i, c, r, n: (0, 0))
     return pl.pallas_call(
         functools.partial(attend_kernel, chunk * rows),
-        out_shape=(shape, shape),
-        grid_spec=pltpu.PrefetchScalarGridSpec(
-            num_scalar_prefetch=3,
-            grid=(spans,),
-            in_specs=[
-                pl.BlockSpec(
-                    (rows, queries.shape[1]),
-                    lambda i, c, r, n: (span_at(i, c) * CHUNKS + chunk, 0),
-                ),
-                new_spec,
-                new_spec,
-                old_spec,
-                old_spec,
-                pl.BlockSpec(memory_space=pltpu.HBM),
-            ],
-            out_specs=[out_spec, out_spec],
-            scratch_shapes=[
-                pltpu.VMEM(out_proj.shape, out_proj.dtype),
-                pltpu.SemaphoreType.DMA,
-            ],
-        ),
+        out_shape=(pltpu.VMEM((rows, width), jnp.float32),) * 2,
+        in_specs=[SMEM] * 3 + [pl.BlockSpec(memory_space=pltpu.HBM)] * 6,
+        out_specs=(VMEM,) * 2,
+        scratch_shapes=[
+            pltpu.VMEM((spans, rows, queries.shape[1]), kind),
+            pltpu.VMEM((spans, length, HD), kind),
+            pltpu.VMEM((spans, length, HD), kind),
+            pltpu.VMEM(cache_keys.shape, kind),
+            pltpu.VMEM(cache_keys.shape, kind),
+            pltpu.VMEM(out_proj.shape, kind),
+            pltpu.SemaphoreType.DMA((spans + 1, 5)),
+        ],
         cost_estimate=pl.CostEstimate(
             flops=2 * macs, transcendentals=0, bytes_accessed=out_proj.size * 2
         ),
-        compiler_params=pltpu.CompilerParams(vmem_limit_bytes=20 << 20),
+        compiler_params=pltpu.CompilerParams(vmem_limit_bytes=24 << 20),
         name="attend",
     )(
-        core,
-        span_req,
-        cache_len,
+        ids,
+        *map(in_hbm, (span_req, cache_len)),
         *map(in_hbm, (queries, new_keys, new_values, cache_keys, cache_values, out_proj)),
     )
 
 
-def norm_kernel(near_ref, far_ref, resid_ref, gain_ref, hidden_ref, normed_ref):
-    state = resid_ref[...].astype(jnp.float32) + (near_ref[...] + far_ref[...])
-    state = state.astype(jnp.bfloat16)
+def norm_kernel(first_row, near_ref, far_ref, resid_ref, gain_ref, hidden_ref, normed_ref):
+    rows = near_ref.shape[0]
+    state = resid_ref[first_row : first_row + rows].astype(jnp.float32)
+    state = (state + (near_ref[...] + far_ref[...])).astype(jnp.bfloat16)
     hidden_ref[...] = state
     state = state.astype(jnp.float32)
     mean_square = jnp.mean(state * state, axis=-1, keepdims=True)
@@ -179,21 +180,14 @@
 
 def norm_chunk(chunk, near, far, resid, gain):
     rows, width = near.shape
-    whole = pl.BlockSpec((rows, width), lambda i: (0, 0))
     return pl.pallas_call(
-        norm_kernel,
-        grid=(1,),
+        functools.partial(norm_kernel, chunk * rows),
         out_shape=(pltpu.VMEM((rows, width), jnp.bfloat16),) * 2,
-        in_specs=[
-            whole,
-            whole,
-            pl.BlockSpec((rows, width), lambda i: (chunk, 0)),
-            pl.BlockSpec((1, width), lambda i: (0, 0)),
-        ],
-        out_specs=(whole, whole),
+        in_specs=[VMEM] * 4,
+        out_specs=(VMEM,) * 2,
         compiler_params=SMALL,
         name="norm",
-    )(in_vmem(near), in_vmem(far), in_hbm(resid), gain.reshape(1, width))
+    )(*map(in_vmem, (near, far, resid, gain.reshape(1, width))))
 
 
 def experts_kernel(n_expert, firsts, offsets, ids, *refs):
@@ -345,21 +339,19 @@
     steps[-1] = [(b, a) for a, b in steps[1]]
     reach = n_expert // 2
 
+    ids = jnp.stack([e, c])
     mine = (w_gate[0], w_up[0], w_down[0])
     other = tuple(lax.ppermute(w, "attn", swap) for w in mine)
-
     tables = weigh(routes, gates, experts)
     for bit in range(n_expert.bit_length() - 1):
         pairs = [(i, i ^ (1 << bit)) for i in range(n_expert)]
         tables = jnp.concatenate([tables, lax.ppermute(tables, "expert", pairs)], axis=0)
 
-    core = c.reshape(1)
-    ids = jnp.stack([e, c])
     near, far = [], []
     for k in range(CHUNKS):
         theirs, ours = attend_chunk(
             k,
-            core,
+            ids,
             span_req,
             cache_len,
             queries,

time: 133 us -> 117 us (0.88)
  Pallas kernels: 57.6 us -> 34.1 us
  waiting for transfers between devices: 29.1 us -> 42.5 us
  local copies, waits for them, and re-layouts: 7.1 us -> 0.04 us
    pallas_call x8, Pallas kernels: 38.3 us -> 20 us  [run_experts(): pl.pallas_call(functools.partial(experts_kernel, n_expert, firsts, offset...]
    ppermute x14, waiting for transfers between devices: 0.48 us -> 8.66 us  [send(): lax.ppermute(x, 'expert', steps[way])]
    unnamed x60 -> x14, local copies, waits for them, and re-layouts: 7.1 us -> 0.04 us
    ppermute x12, waiting for transfers between devices: 17 us -> 23.2 us  [dense_layer(): moving[k][way] = lax.ppermute(moving[k][way], 'expert', steps[way])]
    pallas_call x2, Pallas kernels: 15.2 us -> 12.1 us  [attend_chunk(): pl.pallas_call(functools.partial(attend_kernel, chunk * rows), out_shape=...]
    pallas_call x2, Pallas kernels: 2.38 us -> 0.46 us  [norm_chunk(): pl.pallas_call(functools.partial(norm_kernel, chunk * rows), out_shape=(p...]
  transfers between devices with their start and end apart: 36 -> 36, of which waited for: 10 -> 13; matrix products, arithmetic and copies ran while one was open for 0% -> 0% of each run, Pallas kernels for 37% -> 23%
where the time goes in v3:
time: 117 us
  waiting for transfers between devices  42.5 us (36%)
  starting transfers between devices  39.6 us (34%)
  Pallas kernels  34.1 us (29%)
    ppermute x12, waiting for transfers between devices, dense_layer(): moving[k][way] = lax.ppermute(moving[k][way], 'expert', steps[way])  23.2 us
    pallas_call x8, Pallas kernels, run_experts(): pl.pallas_call(functools.partial(experts_kernel, n_expert, firsts, offset...  20 us
    ppermute x14, starting transfers between devices, send(): lax.ppermute(x, 'expert', steps[way])  14.9 us
    ppermute x12, starting transfers between devices, dense_layer(): moving[k][way] = lax.ppermute(moving[k][way], 'expert', steps[way])  13.1 us
    pallas_call x2, Pallas kernels, attend_chunk(): pl.pallas_call(functools.partial(attend_kernel, chunk * rows), out_shape=...  12.1 us
    ppermute x14, waiting for transfers between devices, send(): lax.ppermute(x, 'expert', steps[way])  8.66 us
    ppermute x3, starting transfers between devices, dense_layer(): lax.ppermute(tables, 'expert', pairs)  8.11 us
    ppermute x2, waiting for transfers between devices, dense_layer(): last.append(lax.ppermute(moving[k][longer[k]], 'expert', steps[longer[k]]))  6.19 us
  transfers between devices with their start and end apart: 36, of which 13 were waited for; matrix products, arithmetic and copies ran while one was open for 0% of the time, Pallas kernels for 23%

profile of v3, /device:TPU:0, one launch (start us, length us, event | category | flops | bytes accessed | tf_op | source)
XLA Modules:
  0.0 116.6 jit_solution(3671163918352531786)
XLA Ops:
  0.0 0.1 pad_add_fusion.ids
  0.1 5.9 %attend.3 = (f32[64,2048]{1,0:T(8,128)S(1)}, f32[64,2048]{1,0:T(8,128)S(1)}) custom-call(s32[2]{0:T(128)S(1)} %pad_add_fusion.ids, s32[2]{0:T(128)} %span_req.3, s32[2]{0:T(128)} %cache_len.3, bf16[256,1024]{1,0:T(8,128)(2,1)} %q_hbm.3, bf16[256,128]{1,0:T(8,128)(2,1)} %nk_hbm.3, bf16[256,128]{1,0:T(8,128)(2,1)} %nv_hbm.3, bf16[2,1024,128]{2,1,0:T(8,128)(2,1)} %ck_hbm.3, ...), custom_call_target="tpu_custom_call" | custom-call | flops 1140850688 | bytes 4194304 | tf_op jit(solution)/shard_map/attend/pallas_call | solution.py:145
  6.1 0.6 collective-permute-start.1
  6.6 6.2 %attend.2 = (f32[64,2048]{1,0:T(8,128)S(1)}, f32[64,2048]{1,0:T(8,128)S(1)}) custom-call(s32[2]{0:T(128)S(1)} %pad_add_fusion.ids, s32[2]{0:T(128)} %span_req.3, s32[2]{0:T(128)} %cache_len.3, bf16[256,1024]{1,0:T(8,128)(2,1)} %q_hbm.3, bf16[256,128]{1,0:T(8,128)(2,1)} %nk_hbm.3, bf16[256,128]{1,0:T(8,128)(2,1)} %nv_hbm.3, bf16[2,1024,128]{2,1,0:T(8,128)(2,1)} %ck_hbm.3, ...), custom_call_target="tpu_custom_call" | custom-call | flops 1140850688 | bytes 4194304 | tf_op jit(solution)/shard_map/attend/pallas_call | solution.py:145
  12.8 0.2 collective-permute-start
  13.0 3.0 %collective-permute-start.2 = (f32[1,16,128]{2,1,0:T(8,128)S(1)}, f32[1,16,128]{2,1,0:T(8,128)S(1)}, u32[]{:S(2)}, u32[]{:S(2)}) collective-permute-start(f32[1,16,128]{2,1,0:T(8,128)S(1)} %weigh.1), channel_id=1, source_target_pairs={{0,2},{2,0},{4,6},{6,4},{8,10},{10,8},{12,14},{14,12},{1,3},{3,1},... | collective-permute-start | bytes 24584 | tf_op jit(solution)/shard_map/ppermute | solution.py:348
  16.0 1.6 %collective-permute-done.2 = f32[1,16,128]{2,1,0:T(8,128)S(1)} collective-permute-done((f32[1,16,128]{2,1,0:T(8,128)S(1)}, f32[1,16,128]{2,1,0:T(8,128)S(1)}, u32[]{:S(2)}, u32[]{:S(2)}) %collective-permute-start.2) | collective-permute-done | bytes 8224 | tf_op jit(solution)/shard_map/ppermute | solution.py:348
  17.7 2.1 %collective-permute-start.3 = (f32[2,16,128]{2,1,0:T(8,128)S(1)}, f32[2,16,128]{2,1,0:T(8,128)S(1)}, u32[]{:S(2)}, u32[]{:S(2)}) collective-permute-start(f32[2,16,128]{2,1,0:T(8,128)S(1)} %pad_maximum_fusion.2), channel_id=1, source_target_pairs={{0,4},{2,6},{4,0},{6,2},{8,12},{10,14},{12,8},{14,10},{1,5},{3,7},... | collective-permute-start | bytes 49160 | tf_op jit(solution)/shard_map/ppermute | solution.py:348
  19.8 0.2 norm.3
  20.0 1.6 %collective-permute-start.11 = (bf16[64,2048]{1,0:T(8,128)(2,1)S(1)}, bf16[64,2048]{1,0:T(8,128)(2,1)S(1)}, u32[]{:S(2)}, u32[]{:S(2)}) collective-permute-start(bf16[64,2048]{1,0:T(8,128)(2,1)S(1)} %get-tuple-element.46.refs_1_), channel_id=1, source_target_pairs={{4,0},{8,4},{12,8},{14,12},{10,14},{6,10},{2,6},{0,2},{5,1},{9,5},... | collective-permute-start | bytes 786440 | tf_op jit(solution)/shard_map/ppermute | solution.py:386
  21.6 3.1 %collective-permute-start.4 = (f32[4,16,128]{2,1,0:T(8,128)S(1)}, f32[4,16,128]{2,1,0:T(8,128)S(1)}, u32[]{:S(2)}, u32[]{:S(2)}) collective-permute-start(f32[4,16,128]{2,1,0:T(8,128)S(1)} %pad_maximum_fusion.1), channel_id=1, source_target_pairs={{0,8},{2,10},{4,12},{6,14},{8,0},{10,2},{12,4},{14,6},{1,9},{3,11}... | collective-permute-start | bytes 98312 | tf_op jit(solution)/shard_map/ppermute | solution.py:348
  24.7 1.4 %collective-permute-start.10 = (bf16[64,2048]{1,0:T(8,128)(2,1)S(1)}, bf16[64,2048]{1,0:T(8,128)(2,1)S(1)}, u32[]{:S(2)}, u32[]{:S(2)}) collective-permute-start(bf16[64,2048]{1,0:T(8,128)(2,1)S(1)} %get-tuple-element.46.refs_1_), channel_id=1, source_target_pairs={{0,4},{4,8},{8,12},{12,14},{14,10},{10,6},{6,2},{2,0},{1,5},{5,9},... | collective-permute-start | bytes 786440 | tf_op jit(solution)/shard_map/ppermute | solution.py:386
  26.1 2.7 %collective-permute-done.4 = f32[4,16,128]{2,1,0:T(8,128)S(1)} collective-permute-done((f32[4,16,128]{2,1,0:T(8,128)S(1)}, f32[4,16,128]{2,1,0:T(8,128)S(1)}, u32[]{:S(2)}, u32[]{:S(2)}) %collective-permute-start.4) | collective-permute-done | bytes 32800 | tf_op jit(solution)/shard_map/ppermute | solution.py:348
  28.8 0.5 collective-permute-start.7
  29.3 0.2 norm.2
  29.7 1.4 %collective-permute-done.10.refs_0_ = bf16[64,2048]{1,0:T(8,128)(2,1)S(1)} collective-permute-done((bf16[64,2048]{1,0:T(8,128)(2,1)S(1)}, bf16[64,2048]{1,0:T(8,128)(2,1)S(1)}, u32[]{:S(2)}, u32[]{:S(2)}) %collective-permute-start.10) | collective-permute-done | bytes 262176 | tf_op jit(solution)/shard_map/ppermute | solution.py:386
  31.0 1.4 %collective-permute-start.8 = (bf16[64,2048]{1,0:T(8,128)(2,1)S(1)}, bf16[64,2048]{1,0:T(8,128)(2,1)S(1)}, u32[]{:S(2)}, u32[]{:S(2)}) collective-permute-start(bf16[64,2048]{1,0:T(8,128)(2,1)S(1)} %get-tuple-element.45.refs_0_), channel_id=1, source_target_pairs={{0,4},{4,8},{8,12},{12,14},{14,10},{10,6},{6,2},{2,0},{1,5},{5,9},... | collective-permute-start | bytes 786440 | tf_op jit(solution)/shard_map/ppermute | solution.py:386
  32.4 5.5 %collective-permute-done.9.refs_1_ = bf16[64,2048]{1,0:T(8,128)(2,1)S(1)} collective-permute-done((bf16[64,2048]{1,0:T(8,128)(2,1)S(1)}, bf16[64,2048]{1,0:T(8,128)(2,1)S(1)}, u32[]{:S(2)}, u32[]{:S(2)}) %collective-permute-start.9) | collective-permute-done | bytes 262176 | tf_op jit(solution)/shard_map/ppermute | solution.py:386
  37.9 0.3 collective-permute-start.15
  38.2 1.7 %collective-permute-start.14 = (bf16[64,2048]{1,0:T(8,128)(2,1)S(1)}, bf16[64,2048]{1,0:T(8,128)(2,1)S(1)}, u32[]{:S(2)}, u32[]{:S(2)}) collective-permute-start(bf16[64,2048]{1,0:T(8,128)(2,1)S(1)} %collective-permute-done.10.refs_0_), channel_id=1, source_target_pairs={{0,4},{4,8},{8,12},{12,14},{14,10},{10,6},{6,2},{2,0},{1,5},{5,9},... | collective-permute-start | bytes 786440 | tf_op jit(solution)/shard_map/ppermute | solution.py:386
  40.0 5.4 %collective-permute-done.15.refs_1_ = bf16[64,2048]{1,0:T(8,128)(2,1)S(1)} collective-permute-done((bf16[64,2048]{1,0:T(8,128)(2,1)S(1)}, bf16[64,2048]{1,0:T(8,128)(2,1)S(1)}, u32[]{:S(2)}, u32[]{:S(2)}) %collective-permute-start.15) | collective-permute-done | bytes 262176 | tf_op jit(solution)/shard_map/ppermute | solution.py:386
  45.4 0.6 collective-permute-start.13
  45.9 1.5 %collective-permute-start.12 = (bf16[64,2048]{1,0:T(8,128)(2,1)S(1)}, bf16[64,2048]{1,0:T(8,128)(2,1)S(1)}, u32[]{:S(2)}, u32[]{:S(2)}) collective-permute-start(bf16[64,2048]{1,0:T(8,128)(2,1)S(1)} %collective-permute-done.8.refs_0_), channel_id=1, source_target_pairs={{0,4},{4,8},{8,12},{12,14},{14,10},{10,6},{6,2},{2,0},{1,5},{5,9},... | collective-permute-start | bytes 786440 | tf_op jit(solution)/shard_map/ppermute | solution.py:386
  47.4 4.5 %collective-permute-done.13.refs_1_ = bf16[64,2048]{1,0:T(8,128)(2,1)S(1)} collective-permute-done((bf16[64,2048]{1,0:T(8,128)(2,1)S(1)}, bf16[64,2048]{1,0:T(8,128)(2,1)S(1)}, u32[]{:S(2)}, u32[]{:S(2)}) %collective-permute-start.13) | collective-permute-done | bytes 262176 | tf_op jit(solution)/shard_map/ppermute | solution.py:386
  51.9 0.8 collective-permute-start.20
  52.8 1.2 %collective-permute-start.16 = (bf16[64,2048]{1,0:T(8,128)(2,1)S(1)}, bf16[64,2048]{1,0:T(8,128)(2,1)S(1)}, u32[]{:S(2)}, u32[]{:S(2)}) collective-permute-start(bf16[64,2048]{1,0:T(8,128)(2,1)S(1)} %collective-permute-done.12.refs_0_), channel_id=1, source_target_pairs={{0,4},{4,8},{8,12},{12,14},{14,10},{10,6},{6,2},{2,0},{1,5},{5,9},... | collective-permute-start | bytes 786440 | tf_op jit(solution)/shard_map/ppermute | solution.py:386
  54.0 5.3 %collective-permute-done.20.refs_1_ = bf16[64,2048]{1,0:T(8,128)(2,1)S(1)} collective-permute-done((bf16[64,2048]{1,0:T(8,128)(2,1)S(1)}, bf16[64,2048]{1,0:T(8,128)(2,1)S(1)}, u32[]{:S(2)}, u32[]{:S(2)}) %collective-permute-start.20) | collective-permute-done | bytes 262176 | tf_op jit(solution)/shard_map/ppermute | solution.py:386
  59.3 0.6 collective-permute-start.27
  59.9 1.7 %collective-permute-start.26 = (bf16[64,2048]{1,0:T(8,128)(2,1)S(1)}, bf16[64,2048]{1,0:T(8,128)(2,1)S(1)}, u32[]{:S(2)}, u32[]{:S(2)}) collective-permute-start(bf16[64,2048]{1,0:T(8,128)(2,1)S(1)} %collective-permute-done.16.refs_0_), channel_id=1, source_target_pairs={{0,4},{4,8},{8,12},{12,14},{14,10},{10,6},{6,2},{2,0},{1,5},{5,9},... | collective-permute-start | bytes 786440 | tf_op jit(solution)/shard_map/ppermute | solution.py:396
  61.6 6.2 %collective-permute-done.27.refs_1_ = bf16[64,2048]{1,0:T(8,128)(2,1)S(1)} collective-permute-done((bf16[64,2048]{1,0:T(8,128)(2,1)S(1)}, bf16[64,2048]{1,0:T(8,128)(2,1)S(1)}, u32[]{:S(2)}, u32[]{:S(2)}) %collective-permute-start.27) | collective-permute-done | bytes 262176 | tf_op jit(solution)/shard_map/ppermute | solution.py:396
  67.8 0.4 collective-permute-start.17
  68.2 2.2 %collective-permute-start.19 = (bf16[64,2048]{1,0:T(8,128)(2,1)S(1)}, bf16[64,2048]{1,0:T(8,128)(2,1)S(1)}, u32[]{:S(2)}, u32[]{:S(2)}) collective-permute-start(bf16[64,2048]{1,0:T(8,128)(2,1)S(1)} %collective-permute-done.14.refs_0_), channel_id=1, source_target_pairs={{0,4},{4,8},{8,12},{12,14},{14,10},{10,6},{6,2},{2,0},{1,5},{5,9},... | collective-permute-start | bytes 786440 | tf_op jit(solution)/shard_map/ppermute | solution.py:386
  70.4 2.5 %experts.15 = (bf16[64,2048]{1,0:T(8,128)(2,1)S(1)}, bf16[64,2048]{1,0:T(8,128)(2,1)S(1)}) custom-call(s32[2]{0:T(128)S(1)} %pad_add_fusion.ids, bf16[64,2048]{1,0:T(8,128)(2,1)S(1)} %collective-permute-done.26.refs_0_, bf16[64,2048]{1,0:T(8,128)(2,1)S(1)} %collective-permute-done.27.refs_1_, f32[8,16,128]{2,1,0:T(8,128)S(1)} %pad_maximum_fusion.refs_2_, ...), custom_call_target="tpu_custom_call" | custom-call | flops 1207959552 | bytes 9437184 | tf_op jit(solution)/shard_map/experts/pallas_call | solution.py:233
  72.9 1.3 %collective-permute-start.28 = (bf16[64,2048]{1,0:T(8,128)(2,1)S(1)}, bf16[64,2048]{1,0:T(8,128)(2,1)S(1)}, u32[]{:S(2)}, u32[]{:S(2)}) collective-permute-start(bf16[64,2048]{1,0:T(8,128)(2,1)S(1)} %get-tuple-element.65), channel_id=1, source_target_pairs={{0,4},{4,8},{8,12},{12,14},{14,10},{10,6},{6,2},{2,0},{1,5},{5,9},... | collective-permute-start | bytes 786440 | tf_op jit(solution)/shard_map/ppermute | solution.py:400
  74.2 0.8 collective-permute-start.29
  75.0 1.1 collective-permute-done.17.refs_1_
  76.0 2.5 %experts.13 = (bf16[64,2048]{1,0:T(8,128)(2,1)S(1)}, f32[64,2048]{1,0:T(8,128)S(1)}) custom-call(s32[2]{0:T(128)S(1)} %pad_add_fusion.ids, bf16[64,2048]{1,0:T(8,128)(2,1)S(1)} %collective-permute-done.16.refs_0_, bf16[64,2048]{1,0:T(8,128)(2,1)S(1)} %collective-permute-done.17.refs_1_, f32[8,16,128]{2,1,0:T(8,128)S(1)} %pad_maximum_fusion.refs_2_, ...), custom_call_target="tpu_custom_call" | custom-call | flops 1207959552 | bytes 9437184 | tf_op jit(solution)/shard_map/experts/pallas_call | solution.py:233
  78.6 0.1 collective-permute-start.18
  78.6 2.5 %experts.14 = (f32[64,2048]{1,0:T(8,128)S(1)}, bf16[64,2048]{1,0:T(8,128)(2,1)S(1)}) custom-call(s32[2]{0:T(128)S(1)} %pad_add_fusion.ids, bf16[64,2048]{1,0:T(8,128)(2,1)S(1)} %collective-permute-done.19.refs_0_, bf16[64,2048]{1,0:T(8,128)(2,1)S(1)} %collective-permute-done.20.refs_1_, f32[8,16,128]{2,1,0:T(8,128)S(1)} %pad_maximum_fusion.refs_2_, ...), custom_call_target="tpu_custom_call" | custom-call | flops 1207959552 | bytes 9437184 | tf_op jit(solution)/shard_map/experts/pallas_call | solution.py:233
  81.1 2.1 %collective-permute-start.21 = (bf16[64,2048]{1,0:T(8,128)(2,1)S(1)}, bf16[64,2048]{1,0:T(8,128)(2,1)S(1)}, u32[]{:S(2)}, u32[]{:S(2)}) collective-permute-start(bf16[64,2048]{1,0:T(8,128)(2,1)S(1)} %get-tuple-element.54), channel_id=1, source_target_pairs={{0,4},{4,8},{8,12},{12,14},{14,10},{10,6},{6,2},{2,0},{1,5},{5,9},... | collective-permute-start | bytes 786440 | tf_op jit(solution)/shard_map/ppermute | solution.py:400
  83.2 0.1 add.9
  83.3 1.3 %collective-permute-start.30 = (bf16[64,2048]{1,0:T(8,128)(2,1)S(1)}, bf16[64,2048]{1,0:T(8,128)(2,1)S(1)}, u32[]{:S(2)}, u32[]{:S(2)}) collective-permute-start(bf16[64,2048]{1,0:T(8,128)(2,1)S(1)} %get-tuple-element.67), channel_id=1, source_target_pairs={{0,4},{4,8},{8,12},{12,14},{14,10},{10,6},{6,2},{2,0},{1,5},{5,9},... | collective-permute-start | bytes 786440 | tf_op jit(solution)/shard_map/ppermute | solution.py:400
  84.6 0.8 collective-permute-start.31
  85.4 2.5 %experts.12 = (f32[64,2048]{1,0:T(8,128)S(1)}, f32[64,2048]{1,0:T(8,128)S(1)}) custom-call(s32[2]{0:T(128)S(1)} %pad_add_fusion.ids, bf16[64,2048]{1,0:T(8,128)(2,1)S(1)} %collective-permute-done.14.refs_0_, bf16[64,2048]{1,0:T(8,128)(2,1)S(1)} %collective-permute-done.15.refs_1_, f32[8,16,128]{2,1,0:T(8,128)S(1)} %pad_maximum_fusion.refs_2_, ...), custom_call_target="tpu_custom_call" | custom-call | flops 1207959552 | bytes 9437184 | tf_op jit(solution)/shard_map/experts/pallas_call | solution.py:233
  87.9 2.5 %experts.11 = (f32[64,2048]{1,0:T(8,128)S(1)}, f32[64,2048]{1,0:T(8,128)S(1)}) custom-call(s32[2]{0:T(128)S(1)} %pad_add_fusion.ids, bf16[64,2048]{1,0:T(8,128)(2,1)S(1)} %collective-permute-done.12.refs_0_, bf16[64,2048]{1,0:T(8,128)(2,1)S(1)} %collective-permute-done.13.refs_1_, f32[8,16,128]{2,1,0:T(8,128)S(1)} %pad_maximum_fusion.refs_2_, ...), custom_call_target="tpu_custom_call" | custom-call | flops 1207959552 | bytes 9437184 | tf_op jit(solution)/shard_map/experts/pallas_call | solution.py:233
  90.4 0.1 add.7
  90.5 0.1 collective-permute-start.22
  90.6 2.0 %collective-permute-start.23 = (bf16[64,2048]{1,0:T(8,128)(2,1)S(1)}, bf16[64,2048]{1,0:T(8,128)(2,1)S(1)}, u32[]{:S(2)}, u32[]{:S(2)}) collective-permute-start(bf16[64,2048]{1,0:T(8,128)(2,1)S(1)} %get-tuple-element.56), channel_id=1, source_target_pairs={{0,4},{4,8},{8,12},{12,14},{14,10},{10,6},{6,2},{2,0},{1,5},{5,9},... | collective-permute-start | bytes 786440 | tf_op jit(solution)/shard_map/ppermute | solution.py:400
  92.6 3.4 %collective-permute-done.30.refs_2_ = bf16[64,2048]{1,0:T(8,128)(2,1)S(1)} collective-permute-done((bf16[64,2048]{1,0:T(8,128)(2,1)S(1)}, bf16[64,2048]{1,0:T(8,128)(2,1)S(1)}, u32[]{:S(2)}, u32[]{:S(2)}) %collective-permute-start.30) | collective-permute-done | bytes 262176 | tf_op jit(solution)/shard_map/ppermute | solution.py:400
  96.0 0.1 add.10
  96.1 2.1 %collective-permute-start.32 = (bf16[64,2048]{1,0:T(8,128)(2,1)S(1)}, bf16[64,2048]{1,0:T(8,128)(2,1)S(1)}, u32[]{:S(2)}, u32[]{:S(2)}) collective-permute-start(bf16[64,2048]{1,0:T(8,128)(2,1)S(1)} %get-tuple-element.69), channel_id=1, source_target_pairs={{0,4},{4,8},{8,12},{12,14},{14,10},{10,6},{6,2},{2,0},{1,5},{5,9},... | collective-permute-start | bytes 786440 | tf_op jit(solution)/shard_map/ppermute | solution.py:400
  98.2 2.5 %experts.10 = (f32[64,2048]{1,0:T(8,128)S(1)}, f32[64,2048]{1,0:T(8,128)S(1)}) custom-call(s32[2]{0:T(128)S(1)} %pad_add_fusion.ids, bf16[64,2048]{1,0:T(8,128)(2,1)S(1)} %collective-permute-done.10.refs_0_, bf16[64,2048]{1,0:T(8,128)(2,1)S(1)} %collective-permute-done.11.refs_1_, f32[8,16,128]{2,1,0:T(8,128)S(1)} %pad_maximum_fusion.refs_2_, ...), custom_call_target="tpu_custom_call" | custom-call | flops 1207959552 | bytes 9437184 | tf_op jit(solution)/shard_map/experts/pallas_call | solution.py:233
  100.7 2.5 %experts.9 = (f32[64,2048]{1,0:T(8,128)S(1)}, f32[64,2048]{1,0:T(8,128)S(1)}) custom-call(s32[2]{0:T(128)S(1)} %pad_add_fusion.ids, bf16[64,2048]{1,0:T(8,128)(2,1)S(1)} %collective-permute-done.8.refs_0_, bf16[64,2048]{1,0:T(8,128)(2,1)S(1)} %collective-permute-done.9.refs_1_, f32[8,16,128]{2,1,0:T(8,128)S(1)} %pad_maximum_fusion.refs_2_, ...), custom_call_target="tpu_custom_call" | custom-call | flops 1207959552 | bytes 9437184 | tf_op jit(solution)/shard_map/experts/pallas_call | solution.py:233
  103.2 0.1 add.8
  103.3 0.5 collective-permute-start.24
  103.8 1.9 %collective-permute-start.25 = (bf16[64,2048]{1,0:T(8,128)(2,1)S(1)}, bf16[64,2048]{1,0:T(8,128)(2,1)S(1)}, u32[]{:S(2)}, u32[]{:S(2)}) collective-permute-start(bf16[64,2048]{1,0:T(8,128)(2,1)S(1)} %get-tuple-element.58), channel_id=1, source_target_pairs={{0,4},{4,8},{8,12},{12,14},{14,10},{10,6},{6,2},{2,0},{1,5},{5,9},... | collective-permute-start | bytes 786440 | tf_op jit(solution)/shard_map/ppermute | solution.py:400
  105.7 1.6 %collective-permute-done.32.refs_2_ = bf16[64,2048]{1,0:T(8,128)(2,1)S(1)} collective-permute-done((bf16[64,2048]{1,0:T(8,128)(2,1)S(1)}, bf16[64,2048]{1,0:T(8,128)(2,1)S(1)}, u32[]{:S(2)}, u32[]{:S(2)}) %collective-permute-start.32) | collective-permute-done | bytes 262176 | tf_op jit(solution)/shard_map/ppermute | solution.py:400
  107.2 0.1 add.11
  107.3 1.9 %collective-permute-start.34 = (bf16[64,2048]{1,0:T(8,128)(2,1)S(1)}, bf16[64,2048]{1,0:T(8,128)(2,1)S(1)}, u32[]{:S(2)}, u32[]{:S(2)}) collective-permute-start(bf16[64,2048]{1,0:T(8,128)(2,1)S(1)} %get-tuple-element.71), channel_id=1, source_target_pairs={{0,4},{4,8},{8,12},{12,14},{14,10},{10,6},{6,2},{2,0},{1,5},{5,9},... | collective-permute-start | bytes 786440 | tf_op jit(solution)/shard_map/ppermute | solution.py:400
  109.2 0.2 collective-permute-start.35
  109.4 2.5 %experts.8 = (f32[64,2048]{1,0:T(8,128)S(1)}, f32[64,2048]{1,0:T(8,128)S(1)}) custom-call(s32[2]{0:T(128)S(1)} %pad_add_fusion.ids, bf16[64,2048]{1,0:T(8,128)(2,1)S(1)} %get-tuple-element.45.refs_0_, bf16[64,2048]{1,0:T(8,128)(2,1)S(1)} %get-tuple-element.46.refs_1_, f32[8,16,128]{2,1,0:T(8,128)S(1)} %pad_maximum_fusion.refs_2_, ...), custom_call_target="tpu_custom_call" | custom-call | flops 1207959552 | bytes 9437184 | tf_op jit(solution)/shard_map/experts/pallas_call | solution.py:233
  111.9 1.8 %collective-permute-done.34.refs_6_ = bf16[64,2048]{1,0:T(8,128)(2,1)S(1)} collective-permute-done((bf16[64,2048]{1,0:T(8,128)(2,1)S(1)}, bf16[64,2048]{1,0:T(8,128)(2,1)S(1)}, u32[]{:S(2)}, u32[]{:S(2)}) %collective-permute-start.34) | collective-permute-done | bytes 262176 | tf_op jit(solution)/shard_map/ppermute | solution.py:400
  113.8 1.9 %collective-permute-done.35.refs_7_ = bf16[64,2048]{1,0:T(8,128)(2,1)S(1)} collective-permute-done((bf16[64,2048]{1,0:T(8,128)(2,1)S(1)}, bf16[64,2048]{1,0:T(8,128)(2,1)S(1)}, u32[]{:S(2)}, u32[]{:S(2)}) %collective-permute-start.35) | collective-permute-done | bytes 262176 | tf_op jit(solution)/shard_map/ppermute | solution.py:400
  115.6 1.0 finish.1
  (45 shorter events, 0.3 us)
Async XLA Ops:
  6.0 7.0 %copy-start.5 = (s32[128,8]{0,1:T(8,128)S(1)}, s32[128,8]{0,1:T(8,128)}, u32[]{:S(2)}) copy-start(s32[128,8]{0,1:T(8,128)} %param.25) | copy-start | bytes 12292
  6.0 7.0 %copy-start.6 = (f32[128,8]{0,1:T(8,128)S(1)}, f32[128,8]{0,1:T(8,128)}, u32[]{:S(2)}) copy-start(f32[128,8]{0,1:T(8,128)} %param.26) | copy-start | bytes 12292
  6.0 13.7 %copy-start.3 = (bf16[128,2048]{1,0:T(8,128)(2,1)S(1)}, bf16[128,2048]{1,0:T(8,128)(2,1)}, u32[]{:S(2)}) copy-start(bf16[128,2048]{1,0:T(8,128)(2,1)} %resid_ref.3) | copy-start | bytes 1572868
  6.1 13.7 %copy-start.4 = (f32[2048]{0:T(1024)S(1)}, f32[2048]{0:T(1024)}, u32[]{:S(2)}) copy-start(f32[2048]{0:T(1024)} %param.24) | copy-start | bytes 24580
  6.1 13.7 %collective-permute-start.1 = (f32[64,2048]{1,0:T(8,128)S(1)}, f32[64,2048]{1,0:T(8,128)S(1)}, u32[]{:S(2)}, u32[]{:S(2)}) collective-permute-start(f32[64,2048]{1,0:T(8,128)S(1)} %get-tuple-element.43), channel_id=1, source_target_pairs={{0,1},{1,0},{2,3},{3,2},{4,5},{5,4},{6,7},{7,6},{8,9},{9,8},{10,11... | collective-permute-start | bytes 1572872 | tf_op jit(solution)/shard_map/ppermute | solution.py:365
  6.6 22.2 %copy-start.1 = (bf16[1,2048,384]{2,1,0:T(8,128)(2,1)S(1)}, bf16[1,2048,384]{2,1,0:T(8,128)(2,1)}, u32[]{:S(2)}) copy-start(bf16[1,2048,384]{2,1,0:T(8,128)(2,1)} %param.28) | copy-start | bytes 4718596
  6.6 22.2 %copy-start.2 = (bf16[1,384,2048]{2,1,0:T(8,128)(2,1)S(1)}, bf16[1,384,2048]{2,1,0:T(8,128)(2,1)}, u32[]{:S(2)}) copy-start(bf16[1,384,2048]{2,1,0:T(8,128)(2,1)} %param.29) | copy-start | bytes 4718596
  12.8 13.2 %copy-start = (bf16[1,2048,384]{2,1,0:T(8,128)(2,1)S(1)}, bf16[1,2048,384]{2,1,0:T(8,128)(2,1)}, u32[]{:S(2)}) copy-start(bf16[1,2048,384]{2,1,0:T(8,128)(2,1)} %param.27) | copy-start | bytes 4718596
  12.8 16.0 %collective-permute-start = (f32[64,2048]{1,0:T(8,128)S(1)}, f32[64,2048]{1,0:T(8,128)S(1)}, u32[]{:S(2)}, u32[]{:S(2)}) collective-permute-start(f32[64,2048]{1,0:T(8,128)S(1)} %get-tuple-element.40), channel_id=1, source_target_pairs={{0,1},{1,0},{2,3},{3,2},{4,5},{5,4},{6,7},{7,6},{8,9},{9,8},{10,11... | collective-permute-start | bytes 1572872 | tf_op jit(solution)/shard_map/ppermute | solution.py:365
  13.0 4.6 %collective-permute-start.2 = (f32[1,16,128]{2,1,0:T(8,128)S(1)}, f32[1,16,128]{2,1,0:T(8,128)S(1)}, u32[]{:S(2)}, u32[]{:S(2)}) collective-permute-start(f32[1,16,128]{2,1,0:T(8,128)S(1)} %weigh.1), channel_id=1, source_target_pairs={{0,2},{2,0},{4,6},{6,4},{8,10},{10,8},{12,14},{14,12},{1,3},{3,1},... | collective-permute-start | bytes 24584 | tf_op jit(solution)/shard_map/ppermute | solution.py:348
  17.7 3.9 %collective-permute-start.3 = (f32[2,16,128]{2,1,0:T(8,128)S(1)}, f32[2,16,128]{2,1,0:T(8,128)S(1)}, u32[]{:S(2)}, u32[]{:S(2)}) collective-permute-start(f32[2,16,128]{2,1,0:T(8,128)S(1)} %pad_maximum_fusion.2), channel_id=1, source_target_pairs={{0,4},{2,6},{4,0},{6,2},{8,12},{10,14},{12,8},{14,10},{1,5},{3,7},... | collective-permute-start | bytes 49160 | tf_op jit(solution)/shard_map/ppermute | solution.py:348
  20.0 9.6 %collective-permute-start.11 = (bf16[64,2048]{1,0:T(8,128)(2,1)S(1)}, bf16[64,2048]{1,0:T(8,128)(2,1)S(1)}, u32[]{:S(2)}, u32[]{:S(2)}) collective-permute-start(bf16[64,2048]{1,0:T(8,128)(2,1)S(1)} %get-tuple-element.46.refs_1_), channel_id=1, source_target_pairs={{4,0},{8,4},{12,8},{14,12},{10,14},{6,10},{2,6},{0,2},{5,1},{9,5},... | collective-permute-start | bytes 786440 | tf_op jit(solution)/shard_map/ppermute | solution.py:386
  21.6 7.2 %collective-permute-start.4 = (f32[4,16,128]{2,1,0:T(8,128)S(1)}, f32[4,16,128]{2,1,0:T(8,128)S(1)}, u32[]{:S(2)}, u32[]{:S(2)}) collective-permute-start(f32[4,16,128]{2,1,0:T(8,128)S(1)} %pad_maximum_fusion.1), channel_id=1, source_target_pairs={{0,8},{2,10},{4,12},{6,14},{8,0},{10,2},{12,4},{14,6},{1,9},{3,11}... | collective-permute-start | bytes 98312 | tf_op jit(solution)/shard_map/ppermute | solution.py:348
  24.7 6.4 %collective-permute-start.10 = (bf16[64,2048]{1,0:T(8,128)(2,1)S(1)}, bf16[64,2048]{1,0:T(8,128)(2,1)S(1)}, u32[]{:S(2)}, u32[]{:S(2)}) collective-permute-start(bf16[64,2048]{1,0:T(8,128)(2,1)S(1)} %get-tuple-element.46.refs_1_), channel_id=1, source_target_pairs={{0,4},{4,8},{8,12},{12,14},{14,10},{10,6},{6,2},{2,0},{1,5},{5,9},... | collective-permute-start | bytes 786440 | tf_op jit(solution)/shard_map/ppermute | solution.py:386
  26.1 44.3 %collective-permute-start.5 = (bf16[2048,384]{1,0:T(8,128)(2,1)S(1)}, bf16[2048,384]{1,0:T(8,128)(2,1)S(1)}, u32[]{:S(2)}, u32[]{:S(2)}) collective-permute-start(bf16[2048,384]{1,0:T(8,128)(2,1)S(1)} %bitcast.8), channel_id=1, source_target_pairs={{0,1},{1,0},{2,3},{3,2},{4,5},{5,4},{6,7},{7,6},{8,9},{9,8},{10,11... | collective-permute-start | bytes 4718600 | tf_op jit(solution)/shard_map/ppermute | solution.py:344
  28.8 41.6 %collective-permute-start.6 = (bf16[2048,384]{1,0:T(8,128)(2,1)S(1)}, bf16[2048,384]{1,0:T(8,128)(2,1)S(1)}, u32[]{:S(2)}, u32[]{:S(2)}) collective-permute-start(bf16[2048,384]{1,0:T(8,128)(2,1)S(1)} %bitcast.17), channel_id=1, source_target_pairs={{0,1},{1,0},{2,3},{3,2},{4,5},{5,4},{6,7},{7,6},{8,9},{9,8},{10,11... | collective-permute-start | bytes 4718600 | tf_op jit(solution)/shard_map/ppermute | solution.py:344
  28.8 41.5 %collective-permute-start.7 = (bf16[384,2048]{1,0:T(8,128)(2,1)S(1)}, bf16[384,2048]{1,0:T(8,128)(2,1)S(1)}, u32[]{:S(2)}, u32[]{:S(2)}) collective-permute-start(bf16[384,2048]{1,0:T(8,128)(2,1)S(1)} %bitcast.26), channel_id=1, source_target_pairs={{0,1},{1,0},{2,3},{3,2},{4,5},{5,4},{6,7},{7,6},{8,9},{9,8},{10,11... | collective-permute-start | bytes 4718600 | tf_op jit(solution)/shard_map/ppermute | solution.py:344
  29.6 8.3 %collective-permute-start.9 = (bf16[64,2048]{1,0:T(8,128)(2,1)S(1)}, bf16[64,2048]{1,0:T(8,128)(2,1)S(1)}, u32[]{:S(2)}, u32[]{:S(2)}) collective-permute-start(bf16[64,2048]{1,0:T(8,128)(2,1)S(1)} %get-tuple-element.45.refs_0_), channel_id=1, source_target_pairs={{4,0},{8,4},{12,8},{14,12},{10,14},{6,10},{2,6},{0,2},{5,1},{9,5},... | collective-permute-start | bytes 786440 | tf_op jit(solution)/shard_map/ppermute | solution.py:386
  31.0 7.2 %collective-permute-start.8 = (bf16[64,2048]{1,0:T(8,128)(2,1)S(1)}, bf16[64,2048]{1,0:T(8,128)(2,1)S(1)}, u32[]{:S(2)}, u32[]{:S(2)}) collective-permute-start(bf16[64,2048]{1,0:T(8,128)(2,1)S(1)} %get-tuple-element.45.refs_0_), channel_id=1, source_target_pairs={{0,4},{4,8},{8,12},{12,14},{14,10},{10,6},{6,2},{2,0},{1,5},{5,9},... | collective-permute-start | bytes 786440 | tf_op jit(solution)/shard_map/ppermute | solution.py:386
  37.9 7.4 %collective-permute-start.15 = (bf16[64,2048]{1,0:T(8,128)(2,1)S(1)}, bf16[64,2048]{1,0:T(8,128)(2,1)S(1)}, u32[]{:S(2)}, u32[]{:S(2)}) collective-permute-start(bf16[64,2048]{1,0:T(8,128)(2,1)S(1)} %collective-permute-done.11.refs_1_), channel_id=1, source_target_pairs={{4,0},{8,4},{12,8},{14,12},{10,14},{6,10},{2,6},{0,2},{5,1},{9,5},... | collective-permute-start | bytes 786440 | tf_op jit(solution)/shard_map/ppermute | solution.py:386
  38.2 7.7 %collective-permute-start.14 = (bf16[64,2048]{1,0:T(8,128)(2,1)S(1)}, bf16[64,2048]{1,0:T(8,128)(2,1)S(1)}, u32[]{:S(2)}, u32[]{:S(2)}) collective-permute-start(bf16[64,2048]{1,0:T(8,128)(2,1)S(1)} %collective-permute-done.10.refs_0_), channel_id=1, source_target_pairs={{0,4},{4,8},{8,12},{12,14},{14,10},{10,6},{6,2},{2,0},{1,5},{5,9},... | collective-permute-start | bytes 786440 | tf_op jit(solution)/shard_map/ppermute | solution.py:386
  45.4 6.6 %collective-permute-start.13 = (bf16[64,2048]{1,0:T(8,128)(2,1)S(1)}, bf16[64,2048]{1,0:T(8,128)(2,1)S(1)}, u32[]{:S(2)}, u32[]{:S(2)}) collective-permute-start(bf16[64,2048]{1,0:T(8,128)(2,1)S(1)} %collective-permute-done.9.refs_1_), channel_id=1, source_target_pairs={{4,0},{8,4},{12,8},{14,12},{10,14},{6,10},{2,6},{0,2},{5,1},{9,5},... | collective-permute-start | bytes 786440 | tf_op jit(solution)/shard_map/ppermute | solution.py:386
  45.9 6.9 %collective-permute-start.12 = (bf16[64,2048]{1,0:T(8,128)(2,1)S(1)}, bf16[64,2048]{1,0:T(8,128)(2,1)S(1)}, u32[]{:S(2)}, u32[]{:S(2)}) collective-permute-start(bf16[64,2048]{1,0:T(8,128)(2,1)S(1)} %collective-permute-done.8.refs_0_), channel_id=1, source_target_pairs={{0,4},{4,8},{8,12},{12,14},{14,10},{10,6},{6,2},{2,0},{1,5},{5,9},... | collective-permute-start | bytes 786440 | tf_op jit(solution)/shard_map/ppermute | solution.py:386
  51.9 7.3 %collective-permute-start.20 = (bf16[64,2048]{1,0:T(8,128)(2,1)S(1)}, bf16[64,2048]{1,0:T(8,128)(2,1)S(1)}, u32[]{:S(2)}, u32[]{:S(2)}) collective-permute-start(bf16[64,2048]{1,0:T(8,128)(2,1)S(1)} %collective-permute-done.15.refs_1_), channel_id=1, source_target_pairs={{4,0},{8,4},{12,8},{14,12},{10,14},{6,10},{2,6},{0,2},{5,1},{9,5},... | collective-permute-start | bytes 786440 | tf_op jit(solution)/shard_map/ppermute | solution.py:386
  52.8 7.1 %collective-permute-start.16 = (bf16[64,2048]{1,0:T(8,128)(2,1)S(1)}, bf16[64,2048]{1,0:T(8,128)(2,1)S(1)}, u32[]{:S(2)}, u32[]{:S(2)}) collective-permute-start(bf16[64,2048]{1,0:T(8,128)(2,1)S(1)} %collective-permute-done.12.refs_0_), channel_id=1, source_target_pairs={{0,4},{4,8},{8,12},{12,14},{14,10},{10,6},{6,2},{2,0},{1,5},{5,9},... | collective-permute-start | bytes 786440 | tf_op jit(solution)/shard_map/ppermute | solution.py:386
  59.3 8.5 %collective-permute-start.27 = (bf16[64,2048]{1,0:T(8,128)(2,1)S(1)}, bf16[64,2048]{1,0:T(8,128)(2,1)S(1)}, u32[]{:S(2)}, u32[]{:S(2)}) collective-permute-start(bf16[64,2048]{1,0:T(8,128)(2,1)S(1)} %collective-permute-done.20.refs_1_), channel_id=1, source_target_pairs={{4,0},{8,4},{12,8},{14,12},{10,14},{6,10},{2,6},{0,2},{5,1},{9,5},... | collective-permute-start | bytes 786440 | tf_op jit(solution)/shard_map/ppermute | solution.py:396
  59.9 8.3 %collective-permute-start.26 = (bf16[64,2048]{1,0:T(8,128)(2,1)S(1)}, bf16[64,2048]{1,0:T(8,128)(2,1)S(1)}, u32[]{:S(2)}, u32[]{:S(2)}) collective-permute-start(bf16[64,2048]{1,0:T(8,128)(2,1)S(1)} %collective-permute-done.16.refs_0_), channel_id=1, source_target_pairs={{0,4},{4,8},{8,12},{12,14},{14,10},{10,6},{6,2},{2,0},{1,5},{5,9},... | collective-permute-start | bytes 786440 | tf_op jit(solution)/shard_map/ppermute | solution.py:396
  67.8 8.3 %collective-permute-start.17 = (bf16[64,2048]{1,0:T(8,128)(2,1)S(1)}, bf16[64,2048]{1,0:T(8,128)(2,1)S(1)}, u32[]{:S(2)}, u32[]{:S(2)}) collective-permute-start(bf16[64,2048]{1,0:T(8,128)(2,1)S(1)} %collective-permute-done.13.refs_1_), channel_id=1, source_target_pairs={{4,0},{8,4},{12,8},{14,12},{10,14},{6,10},{2,6},{0,2},{5,1},{9,5},... | collective-permute-start | bytes 786440 | tf_op jit(solution)/shard_map/ppermute | solution.py:386
  68.2 10.4 %collective-permute-start.19 = (bf16[64,2048]{1,0:T(8,128)(2,1)S(1)}, bf16[64,2048]{1,0:T(8,128)(2,1)S(1)}, u32[]{:S(2)}, u32[]{:S(2)}) collective-permute-start(bf16[64,2048]{1,0:T(8,128)(2,1)S(1)} %collective-permute-done.14.refs_0_), channel_id=1, source_target_pairs={{0,4},{4,8},{8,12},{12,14},{14,10},{10,6},{6,2},{2,0},{1,5},{5,9},... | collective-permute-start | bytes 786440 | tf_op jit(solution)/shard_map/ppermute | solution.py:386
  72.9 10.3 %collective-permute-start.28 = (bf16[64,2048]{1,0:T(8,128)(2,1)S(1)}, bf16[64,2048]{1,0:T(8,128)(2,1)S(1)}, u32[]{:S(2)}, u32[]{:S(2)}) collective-permute-start(bf16[64,2048]{1,0:T(8,128)(2,1)S(1)} %get-tuple-element.65), channel_id=1, source_target_pairs={{0,4},{4,8},{8,12},{12,14},{14,10},{10,6},{6,2},{2,0},{1,5},{5,9},... | collective-permute-start | bytes 786440 | tf_op jit(solution)/shard_map/ppermute | solution.py:400
  74.2 9.1 %collective-permute-start.29 = (bf16[64,2048]{1,0:T(8,128)(2,1)S(1)}, bf16[64,2048]{1,0:T(8,128)(2,1)S(1)}, u32[]{:S(2)}, u32[]{:S(2)}) collective-permute-start(bf16[64,2048]{1,0:T(8,128)(2,1)S(1)} %get-tuple-element.66), channel_id=1, source_target_pairs={{4,0},{8,4},{12,8},{14,12},{10,14},{6,10},{2,6},{0,2},{5,1},{9,5},... | collective-permute-start | bytes 786440 | tf_op jit(solution)/shard_map/ppermute | solution.py:400
  78.6 11.9 %collective-permute-start.18 = (bf16[64,2048]{1,0:T(8,128)(2,1)S(1)}, bf16[64,2048]{1,0:T(8,128)(2,1)S(1)}, u32[]{:S(2)}, u32[]{:S(2)}) collective-permute-start(bf16[64,2048]{1,0:T(8,128)(2,1)S(1)} %get-tuple-element.53), channel_id=1, source_target_pairs={{4,0},{8,4},{12,8},{14,12},{10,14},{6,10},{2,6},{0,2},{5,1},{9,5},... | collective-permute-start | bytes 786440 | tf_op jit(solution)/shard_map/ppermute | solution.py:400
  81.1 9.3 %collective-permute-start.21 = (bf16[64,2048]{1,0:T(8,128)(2,1)S(1)}, bf16[64,2048]{1,0:T(8,128)(2,1)S(1)}, u32[]{:S(2)}, u32[]{:S(2)}) collective-permute-start(bf16[64,2048]{1,0:T(8,128)(2,1)S(1)} %get-tuple-element.54), channel_id=1, source_target_pairs={{0,4},{4,8},{8,12},{12,14},{14,10},{10,6},{6,2},{2,0},{1,5},{5,9},... | collective-permute-start | bytes 786440 | tf_op jit(solution)/shard_map/ppermute | solution.py:400
  83.3 12.7 %collective-permute-start.30 = (bf16[64,2048]{1,0:T(8,128)(2,1)S(1)}, bf16[64,2048]{1,0:T(8,128)(2,1)S(1)}, u32[]{:S(2)}, u32[]{:S(2)}) collective-permute-start(bf16[64,2048]{1,0:T(8,128)(2,1)S(1)} %get-tuple-element.67), channel_id=1, source_target_pairs={{0,4},{4,8},{8,12},{12,14},{14,10},{10,6},{6,2},{2,0},{1,5},{5,9},... | collective-permute-start | bytes 786440 | tf_op jit(solution)/shard_map/ppermute | solution.py:400
  84.6 11.4 %collective-permute-start.31 = (bf16[64,2048]{1,0:T(8,128)(2,1)S(1)}, bf16[64,2048]{1,0:T(8,128)(2,1)S(1)}, u32[]{:S(2)}, u32[]{:S(2)}) collective-permute-start(bf16[64,2048]{1,0:T(8,128)(2,1)S(1)} %get-tuple-element.68), channel_id=1, source_target_pairs={{4,0},{8,4},{12,8},{14,12},{10,14},{6,10},{2,6},{0,2},{5,1},{9,5},... | collective-permute-start | bytes 786440 | tf_op jit(solution)/shard_map/ppermute | solution.py:400
  90.5 12.7 %collective-permute-start.22 = (bf16[64,2048]{1,0:T(8,128)(2,1)S(1)}, bf16[64,2048]{1,0:T(8,128)(2,1)S(1)}, u32[]{:S(2)}, u32[]{:S(2)}) collective-permute-start(bf16[64,2048]{1,0:T(8,128)(2,1)S(1)} %get-tuple-element.55), channel_id=1, source_target_pairs={{4,0},{8,4},{12,8},{14,12},{10,14},{6,10},{2,6},{0,2},{5,1},{9,5},... | collective-permute-start | bytes 786440 | tf_op jit(solution)/shard_map/ppermute | solution.py:400
  90.6 12.6 %collective-permute-start.23 = (bf16[64,2048]{1,0:T(8,128)(2,1)S(1)}, bf16[64,2048]{1,0:T(8,128)(2,1)S(1)}, u32[]{:S(2)}, u32[]{:S(2)}) collective-permute-start(bf16[64,2048]{1,0:T(8,128)(2,1)S(1)} %get-tuple-element.56), channel_id=1, source_target_pairs={{0,4},{4,8},{8,12},{12,14},{14,10},{10,6},{6,2},{2,0},{1,5},{5,9},... | collective-permute-start | bytes 786440 | tf_op jit(solution)/shard_map/ppermute | solution.py:400
  96.1 11.1 %collective-permute-start.32 = (bf16[64,2048]{1,0:T(8,128)(2,1)S(1)}, bf16[64,2048]{1,0:T(8,128)(2,1)S(1)}, u32[]{:S(2)}, u32[]{:S(2)}) collective-permute-start(bf16[64,2048]{1,0:T(8,128)(2,1)S(1)} %get-tuple-element.69), channel_id=1, source_target_pairs={{0,4},{4,8},{8,12},{12,14},{14,10},{10,6},{6,2},{2,0},{1,5},{5,9},... | collective-permute-start | bytes 786440 | tf_op jit(solution)/shard_map/ppermute | solution.py:400
  98.1 9.1 %collective-permute-start.33 = (bf16[64,2048]{1,0:T(8,128)(2,1)S(1)}, bf16[64,2048]{1,0:T(8,128)(2,1)S(1)}, u32[]{:S(2)}, u32[]{:S(2)}) collective-permute-start(bf16[64,2048]{1,0:T(8,128)(2,1)S(1)} %get-tuple-element.70), channel_id=1, source_target_pairs={{4,0},{8,4},{12,8},{14,12},{10,14},{6,10},{2,6},{0,2},{5,1},{9,5},... | collective-permute-start | bytes 786440 | tf_op jit(solution)/shard_map/ppermute | solution.py:400
  103.3 8.6 %collective-permute-start.24 = (bf16[64,2048]{1,0:T(8,128)(2,1)S(1)}, bf16[64,2048]{1,0:T(8,128)(2,1)S(1)}, u32[]{:S(2)}, u32[]{:S(2)}) collective-permute-start(bf16[64,2048]{1,0:T(8,128)(2,1)S(1)} %get-tuple-element.57), channel_id=1, source_target_pairs={{4,0},{8,4},{12,8},{14,12},{10,14},{6,10},{2,6},{0,2},{5,1},{9,5},... | collective-permute-start | bytes 786440 | tf_op jit(solution)/shard_map/ppermute | solution.py:400
  103.8 8.2 %collective-permute-start.25 = (bf16[64,2048]{1,0:T(8,128)(2,1)S(1)}, bf16[64,2048]{1,0:T(8,128)(2,1)S(1)}, u32[]{:S(2)}, u32[]{:S(2)}) collective-permute-start(bf16[64,2048]{1,0:T(8,128)(2,1)S(1)} %get-tuple-element.58), channel_id=1, source_target_pairs={{0,4},{4,8},{8,12},{12,14},{14,10},{10,6},{6,2},{2,0},{1,5},{5,9},... | collective-permute-start | bytes 786440 | tf_op jit(solution)/shard_map/ppermute | solution.py:400
  107.3 6.4 %collective-permute-start.34 = (bf16[64,2048]{1,0:T(8,128)(2,1)S(1)}, bf16[64,2048]{1,0:T(8,128)(2,1)S(1)}, u32[]{:S(2)}, u32[]{:S(2)}) collective-permute-start(bf16[64,2048]{1,0:T(8,128)(2,1)S(1)} %get-tuple-element.71), channel_id=1, source_target_pairs={{0,4},{4,8},{8,12},{12,14},{14,10},{10,6},{6,2},{2,0},{1,5},{5,9},... | collective-permute-start | bytes 786440 | tf_op jit(solution)/shard_map/ppermute | solution.py:400
  109.2 6.4 %collective-permute-start.35 = (bf16[64,2048]{1,0:T(8,128)(2,1)S(1)}, bf16[64,2048]{1,0:T(8,128)(2,1)S(1)}, u32[]{:S(2)}, u32[]{:S(2)}) collective-permute-start(bf16[64,2048]{1,0:T(8,128)(2,1)S(1)} %get-tuple-element.72), channel_id=1, source_target_pairs={{4,0},{8,4},{12,8},{14,12},{10,14},{6,10},{2,6},{0,2},{5,1},{9,5},... | collective-permute-start | bytes 786440 | tf_op jit(solution)/shard_map/ppermute | solution.py:400
